TPU v7x, 32 devices: a whole 2x2x4 slice. The times are simulated.
32 devices in a mesh: rep: 4 (over y, x), inner: 8 (over z, core).
Axes of the slice: x: 2, y: 2, z: 4, core: 2. Of those that a mesh axis runs over, the one named last changes fastest.
Arguments:
- tokens: bfloat16 [4096, 1024], P(('rep', 'inner')), may hold values from -6 to 6
- cotangent: bfloat16 [4096, 1024], P(('rep', 'inner')), may hold values from -6 to 6
- qkv_weight: bfloat16 [1024, 3072], P('inner'), may hold values from -0.1875 to 0.1875
- out_weight: bfloat16 [1024, 1024], P('inner'), may hold values from -3.5 to 3.5
- in_weight: bfloat16 [1024, 5248], P('inner'), may hold values from -0.1875 to 0.1875
- down_weight: bfloat16 [2624, 1024], P('inner'), may hold values from -0.125 to 0.125
- gain_one: bfloat16 [1024], P('inner'), may hold values from 0.5 to 1.5
- gain_two: bfloat16 [1024], P('inner'), may hold values from 0.5 to 1.5
Outputs:
- layer_out: bfloat16 [4096, 1024], P(('rep', 'inner'))
- input_grad: bfloat16 [4096, 1024], P(('rep', 'inner'))
- qkv_grad: float32 [1024, 3072], P('inner')
- out_grad: float32 [1024, 1024], P('inner')
- in_grad: float32 [1024, 5248], P('inner')
- down_grad: float32 [2624, 1024], P('inner')
- gain_one_grad: float32 [1024], P('inner')
- gain_two_grad: float32 [1024], P('inner')
All inputs are finite; a program needn't handle non-finite values.
Results may differ from a plain program's by a relative error of at most 0.023.
Values may be sent and summed in bfloat16 or wider, within the bound.
No kernel may reach another device: no remote copies, remote signals or barrier semaphores. Data moves between devices by JAX's collectives and lax.ppermute only.
A program may use at most 256 MiB of HBM per device.

v0:
```python
import jax
import jax.numpy as jnp
from jax import lax
from jax.sharding import PartitionSpec as P

HEAD_DIM = 64


EPSILON = 1e-05
THETA = 160000.0


def norm_rows(values, gain_row):
    centred = values - jnp.mean(values, axis=-1, keepdims=True)
    inv_scale = lax.rsqrt(jnp.mean(centred * centred, axis=-1, keepdims=True) + EPSILON)
    return centred * inv_scale * gain_row


def rotate(values, cos_table, sine_table):
    half_width = values.shape[-1] // 2
    first_half = values[..., :half_width]
    second_half = values[..., half_width:]
    return jnp.concatenate(
        [
            first_half * cos_table - second_half * sine_table,
            second_half * cos_table + first_half * sine_table,
        ],
        axis=-1,
    )


def geglu(hidden):
    half_width = hidden.shape[-1] // 2
    return jax.nn.gelu(hidden[:, :half_width], approximate=False) * hidden[:, half_width:]


def contract_rows(left_mat, right_mat):
    return lax.dot_general(
        left_mat, right_mat, (((0,), (0,)), ((), ())), preferred_element_type=jnp.float32
    )


def contract_cols(left_mat, right_mat):
    return lax.dot_general(
        left_mat, right_mat, (((1,), (1,)), ((), ())), preferred_element_type=jnp.float32
    )


def on_device(
    tokens, cotangent, qkv_weight, out_weight, in_weight, down_weight, gain_one, gain_two
):
    row_count = tokens.shape[0]
    model_width = tokens.shape[1]
    head_count = model_width // HEAD_DIM
    score_scale = HEAD_DIM ** (-0.5)
    gathered = (
        lax.all_gather(qkv_weight, "inner", axis=0, tiled=True),
        lax.all_gather(out_weight, "inner", axis=0, tiled=True),
        lax.all_gather(in_weight, "inner", axis=0, tiled=True),
        lax.all_gather(down_weight, "inner", axis=0, tiled=True),
        lax.all_gather(gain_one, "inner", axis=0, tiled=True),
        lax.all_gather(gain_two, "inner", axis=0, tiled=True),
    )
    w_qkv, w_out, w_in, w_down, first_gain, second_gain = gathered
    tok_place = (
        lax.axis_index("inner") * row_count + jnp.arange(row_count, dtype=jnp.int32)
    ).astype(jnp.float32)
    inv_freq = 1.0 / THETA ** (jnp.arange(HEAD_DIM // 2, dtype=jnp.float32) * (2.0 / HEAD_DIM))
    tok_angle = tok_place[:, None] * inv_freq[None, :]
    cos_table = jnp.cos(tok_angle)[:, None, :]
    sine_table = jnp.sin(tok_angle)[:, None, :]

    def split_heads(projected):
        query_part = rotate(
            projected[:, :model_width].reshape(row_count, head_count, HEAD_DIM),
            cos_table,
            sine_table,
        )
        key_part = rotate(
            projected[:, model_width : 2 * model_width].reshape(row_count, head_count, HEAD_DIM),
            cos_table,
            sine_table,
        )
        value_part = projected[:, 2 * model_width :].reshape(row_count, head_count, HEAD_DIM)
        return (query_part, key_part, value_part)

    inputs = tokens.astype(jnp.float32)
    gain_first = first_gain.astype(jnp.float32)
    gain_second = second_gain.astype(jnp.float32)
    normed_one = norm_rows(inputs, gain_first).astype(jnp.bfloat16)
    projected = jnp.dot(normed_one, w_qkv, preferred_element_type=jnp.float32)
    query_part, key_part, value_part = split_heads(projected)
    query_heads = query_part.astype(jnp.bfloat16)
    key_flat = key_part.reshape(row_count, model_width).astype(jnp.bfloat16)
    value_flat = value_part.reshape(row_count, model_width).astype(jnp.bfloat16)
    all_keys, all_values = (
        lax.all_gather(key_flat, "inner", axis=0, tiled=True),
        lax.all_gather(value_flat, "inner", axis=0, tiled=True),
    )
    key_count = all_keys.shape[0]
    block_count = max(1, key_count // 512)
    block_rows = key_count // block_count

    def split_blocks(flat):
        return flat.reshape(block_count, block_rows, head_count, HEAD_DIM)

    def scores_of(key_block):
        return (
            jnp.einsum("qhd,khd->hqk", query_heads, key_block, preferred_element_type=jnp.float32)
            * score_scale
        )

    def stats_step(stat_carry, key_block):
        row_top, row_mass = stat_carry
        scores = scores_of(key_block)
        new_top = jnp.maximum(row_top, jnp.max(scores, axis=-1))
        row_mass = row_mass * jnp.exp(row_top - new_top) + jnp.sum(
            jnp.exp(scores - new_top[..., None]), axis=-1
        )
        return ((new_top, row_mass), None)

    start_top = jnp.full((head_count, row_count), -jnp.inf, jnp.float32)
    start_mass = jnp.zeros((head_count, row_count), jnp.float32)
    stat_final, unused_out = lax.scan(stats_step, (start_top, start_mass), split_blocks(all_keys))
    log_mass = stat_final[0] + jnp.log(stat_final[1])

    def mix_step(total_mix, blocks_pair):
        key_block, value_block = blocks_pair
        weights = jnp.exp(scores_of(key_block) - log_mass[..., None]).astype(jnp.bfloat16)
        return (
            total_mix
            + jnp.einsum("hqk,khd->qhd", weights, value_block, preferred_element_type=jnp.float32),
            None,
        )

    start_mix = jnp.zeros((row_count, head_count, HEAD_DIM), jnp.float32)
    mixed_heads, unused_mix = lax.scan(
        mix_step, start_mix, (split_blocks(all_keys), split_blocks(all_values))
    )
    attended = mixed_heads.reshape(row_count, model_width).astype(jnp.bfloat16)
    middle = inputs + jnp.dot(attended, w_out, preferred_element_type=jnp.float32)
    normed_two = norm_rows(middle, gain_second).astype(jnp.bfloat16)
    hidden = jnp.dot(normed_two, w_in, preferred_element_type=jnp.float32)
    gated = geglu(hidden).astype(jnp.bfloat16)
    layer_out = middle + jnp.dot(gated, w_down, preferred_element_type=jnp.float32)
    again = (
        lax.all_gather(qkv_weight, "inner", axis=0, tiled=True),
        lax.all_gather(out_weight, "inner", axis=0, tiled=True),
        lax.all_gather(in_weight, "inner", axis=0, tiled=True),
        lax.all_gather(down_weight, "inner", axis=0, tiled=True),
        lax.all_gather(gain_one, "inner", axis=0, tiled=True),
        lax.all_gather(gain_two, "inner", axis=0, tiled=True),
    )
    w_qkv, w_out, w_in, w_down, first_gain, second_gain = again
    gain_first = first_gain.astype(jnp.float32)
    gain_second = second_gain.astype(jnp.float32)
    grad_down = contract_rows(gated, cotangent)
    grad_gated = contract_cols(cotangent, w_down)
    gate_value, pull_gate = jax.vjp(geglu, hidden)
    grad_hidden = pull_gate(grad_gated)[0].astype(jnp.bfloat16)
    grad_in = contract_rows(normed_two, grad_hidden)
    grad_normed_two = contract_cols(grad_hidden, w_in)
    norm_value, pull_two = jax.vjp(norm_rows, middle, gain_second)
    back_middle, grad_gain_two = pull_two(grad_normed_two)
    grad_middle = cotangent.astype(jnp.float32) + back_middle
    grad_branch = grad_middle.astype(jnp.bfloat16)
    grad_wout = contract_rows(attended, grad_branch)
    grad_attended = contract_cols(grad_branch, w_out).astype(jnp.bfloat16)
    grad_heads = grad_attended.reshape(row_count, head_count, HEAD_DIM)
    offset = jnp.sum(
        grad_heads.astype(jnp.float32)
        * attended.reshape(row_count, head_count, HEAD_DIM).astype(jnp.float32),
        axis=-1,
    ).T
    all_keys, all_values = (
        lax.all_gather(key_flat, "inner", axis=0, tiled=True),
        lax.all_gather(value_flat, "inner", axis=0, tiled=True),
    )

    def score_grads(key_block, value_block):
        soft_probs = jnp.exp(scores_of(key_block) - log_mass[..., None])
        grad_probs = jnp.einsum(
            "qhd,khd->hqk", grad_heads, value_block, preferred_element_type=jnp.float32
        )
        grad_scores = (soft_probs * (grad_probs - offset[..., None])).astype(jnp.bfloat16)
        return (soft_probs, grad_scores)

    def back_step(grad_query, blocks_pair):
        key_block, value_block = blocks_pair
        soft_probs, grad_scores = score_grads(key_block, value_block)
        grad_value = jnp.einsum(
            "hqk,qhd->khd",
            soft_probs.astype(jnp.bfloat16),
            grad_heads,
            preferred_element_type=jnp.float32,
        )
        grad_key = (
            jnp.einsum("hqk,qhd->khd", grad_scores, query_heads, preferred_element_type=jnp.float32)
            * score_scale
        )
        grad_query = (
            grad_query
            + jnp.einsum("hqk,khd->qhd", grad_scores, key_block, preferred_element_type=jnp.float32)
            * score_scale
        )
        return (grad_query, (grad_key, grad_value))

    start_query = jnp.zeros((row_count, head_count, HEAD_DIM), jnp.float32)
    grad_query, key_parts = lax.scan(
        back_step, start_query, (split_blocks(all_keys), split_blocks(all_values))
    )
    own_keys, own_values = (
        lax.psum_scatter(
            key_parts[0].reshape(key_count, model_width).astype(jnp.bfloat16),
            "inner",
            scatter_dimension=0,
            tiled=True,
        ).astype(jnp.float32),
        lax.psum_scatter(
            key_parts[1].reshape(key_count, model_width).astype(jnp.bfloat16),
            "inner",
            scatter_dimension=0,
            tiled=True,
        ).astype(jnp.float32),
    )
    split_value, pull_split = jax.vjp(split_heads, projected)
    grad_projected = pull_split(
        (
            grad_query,
            own_keys.reshape(row_count, head_count, HEAD_DIM),
            own_values.reshape(row_count, head_count, HEAD_DIM),
        )
    )[0].astype(jnp.bfloat16)
    grad_qkv = contract_rows(normed_one, grad_projected)
    grad_normed_one = contract_cols(grad_projected, w_qkv)
    first_value, pull_one = jax.vjp(norm_rows, inputs, gain_first)
    back_inputs, grad_gain_one = pull_one(grad_normed_one)
    input_grad = (grad_middle + back_inputs).astype(jnp.bfloat16)
    summed = (
        lax.psum_scatter(
            grad_qkv.astype(jnp.bfloat16), "inner", scatter_dimension=0, tiled=True
        ).astype(jnp.float32),
        lax.psum_scatter(
            grad_wout.astype(jnp.bfloat16), "inner", scatter_dimension=0, tiled=True
        ).astype(jnp.float32),
        lax.psum_scatter(
            grad_in.astype(jnp.bfloat16), "inner", scatter_dimension=0, tiled=True
        ).astype(jnp.float32),
        lax.psum_scatter(
            grad_down.astype(jnp.bfloat16), "inner", scatter_dimension=0, tiled=True
        ).astype(jnp.float32),
        lax.psum_scatter(
            grad_gain_one.astype(jnp.bfloat16), "inner", scatter_dimension=0, tiled=True
        ).astype(jnp.float32),
        lax.psum_scatter(
            grad_gain_two.astype(jnp.bfloat16), "inner", scatter_dimension=0, tiled=True
        ).astype(jnp.float32),
    )
    summed = (
        lax.psum(summed[0].astype(jnp.bfloat16), "rep").astype(jnp.float32),
        lax.psum(summed[1].astype(jnp.bfloat16), "rep").astype(jnp.float32),
        lax.psum(summed[2].astype(jnp.bfloat16), "rep").astype(jnp.float32),
        lax.psum(summed[3].astype(jnp.bfloat16), "rep").astype(jnp.float32),
        lax.psum(summed[4].astype(jnp.bfloat16), "rep").astype(jnp.float32),
        lax.psum(summed[5].astype(jnp.bfloat16), "rep").astype(jnp.float32),
    )
    return (
        layer_out.astype(jnp.bfloat16),
        input_grad,
        summed[0],
        summed[1],
        summed[2],
        summed[3],
        summed[4],
        summed[5],
    )


def solution(mesh):
    return jax.shard_map(
        on_device,
        mesh=mesh,
        in_specs=(
            P(("rep", "inner"), None),
            P(("rep", "inner"), None),
            P("inner", None),
            P("inner", None),
            P("inner", None),
            P("inner", None),
            P("inner"),
            P("inner"),
        ),
        out_specs=(
            P(("rep", "inner"), None),
            P(("rep", "inner"), None),
            P("inner", None),
            P("inner", None),
            P("inner", None),
            P("inner", None),
            P("inner"),
            P("inner"),
        ),
        check_vma=False,
    )
```

profile of v0, /device:TPU:0, one launch (start us, length us, event | category | flops | bytes accessed | tf_op | source)
XLA Modules:
  0.0 841.9 jit_solution(2752431351207426690)
XLA Ops:
  8.0 13.5 %all-gather = bf16[8,1,128]{2,1,0:T(2,128)(2,1)S(1)} all-gather(bf16[1,1,128]{2,1,0:T(2,128)(2,1)} %bitcast.152), channel_id=1, replica_groups=mesh['rep'=4,'inner'=8] {'inner'}, dimensions={0}, use_global_device_ids=true | all-gather | bytes 2304 | tf_op jit(solution)/shard_map/all_gather | solution.py:61
  24.0 53.2 %all-gather.9.cloned.1.call-done = bf16[1024,3072]{1,0:T(8,128)(2,1)} async-done(((bf16[128,3072]{1,0:T(8,128)(2,1)}), bf16[1024,3072]{1,0:T(8,128)(2,1)}) %all-gather.9.cloned.1.call-update) | async-done | bytes 6291472 | tf_op jit(solution)/shard_map/all_gather | solution.py:57
  85.1 9.2 %all-gather.1 = bf16[8,1,128]{2,1,0:T(2,128)(2,1)S(1)} all-gather(bf16[1,1,128]{2,1,0:T(2,128)(2,1)S(1)} %bitcast.153), channel_id=1, replica_groups=mesh['rep'=4,'inner'=8] {'inner'}, dimensions={0}, use_global_device_ids=true | all-gather | bytes 2304 | tf_op jit(solution)/shard_map/all_gather | solution.py:62
  94.3 17.8 %all-gather.13.cloned.1.call-done = bf16[1024,1024]{0,1:T(8,128)(2,1)} async-done(((bf16[128,1024]{0,1:T(8,128)(2,1)}), bf16[1024,1024]{0,1:T(8,128)(2,1)}) %all-gather.13.cloned.1.call-update) | async-done | bytes 2097168 | tf_op jit(solution)/shard_map/all_gather | solution.py:97
  118.6 23.9 %all-gather.11.cloned.1.call-done = bf16[1024,1024]{1,0:T(8,128)(2,1)} async-done(((bf16[128,1024]{1,0:T(8,128)(2,1)}), bf16[1024,1024]{1,0:T(8,128)(2,1)}) %all-gather.11.cloned.1.call-update) | async-done | bytes 2097168 | tf_op jit(solution)/shard_map/all_gather | solution.py:98
  142.5 6.4 reshape.196
  154.4 11.6 %while.39 = (s32[]{:T(128)}, f32[16,128]{1,0:T(8,128)S(1)}, f32[16,128]{1,0:T(8,128)S(1)}, bf16[2,512,16,64]{1,3,2,0:T(8,128)(2,1)S(1)}, bf16[128,16,64]{0,2,1:T(8,128)(2,1)S(1)}, /*index=5*/s32[]{:T(128)}, s32[]{:T(128)}) while((s32[]{:T(128)}, f32[16,128]{1,0:T(8,128)S(1)}, f32[16,128]{1,0:T(8,128)S(1)}, ...), condition=%wide.region_5.6_spmd.clone, body=%wide.region_2.5_spmd.clone.sunk | while | flops 139470848 | bytes 9805916 | solution.py:124
  174.9 100.2 %all-gather.17.cloned.1.call-done = bf16[1024,5248]{1,0:T(8,128)(2,1)} async-done(((bf16[128,5248]{1,0:T(8,128)(2,1)}), bf16[1024,5248]{1,0:T(8,128)(2,1)}) %all-gather.17.cloned.1.call-update) | async-done | bytes 10747920 | tf_op jit(solution)/shard_map/all_gather | solution.py:59
  275.1 7.3 fusion.73
  282.4 49.7 %all-gather.19.cloned.1.call-done = bf16[2624,1024]{1,0:T(8,128)(2,1)} async-done(((bf16[328,1024]{1,0:T(8,128)(2,1)}), bf16[2624,1024]{1,0:T(8,128)(2,1)}) %all-gather.19.cloned.1.call-update) | async-done | bytes 5373968 | tf_op jit(solution)/shard_map/all_gather | solution.py:60
  332.1 7.0 fusion.57
  352.1 21.2 %while.41 = (s32[]{:T(128)}, f32[128,16,64]{0,2,1:T(8,128)}, bf16[2,512,16,64]{1,3,2,0:T(8,128)(2,1)}, bf16[2,512,16,64]{1,3,2,0:T(8,128)(2,1)}, bf16[2,512,16,6...) while((s32[]{:T(128)}, f32[128,16,64]{0,2,1:T(8,128)}, ...), condition=%wide.region_14.15_spmd.clone, body=%wide.region_13.14_spmd.clone.sunk | while | flops 680394752 | bytes 87058192 | solution.py:209
  379.5 6.5 reshape.192
  392.4 6.5 reshape.190
  407.4 13.4 %reduce-scatter.21.cloned.1.call-done = bf16[128,1024]{1,0:T(8,128)(2,1)} async-done(((bf16[1024,1024]{1,0:T(8,128)(2,1)}), bf16[128,1024]{1,0:T(8,128)(2,1)}) %reduce-scatter.21.cloned.1.call-update) | async-done | bytes 262160
  421.9 35.6 %reduce-scatter.19.cloned.1.call-done = bf16[128,1024]{1,0:T(8,128)(2,1)} async-done(((bf16[1024,1024]{1,0:T(8,128)(2,1)}), bf16[128,1024]{1,0:T(8,128)(2,1)}) %reduce-scatter.19.cloned.1.call-update) | async-done | bytes 262160
  465.0 7.3 convolution_convert_fusion
  472.3 22.0 %reduce-scatter.13.cloned.1.call-done = bf16[128,1024]{1,0:T(8,128)(2,1)} async-done(((bf16[1024,1024]{1,0:T(8,128)(2,1)}), bf16[128,1024]{1,0:T(8,128)(2,1)}) %reduce-scatter.13.cloned.1.call-update) | async-done | bytes 262160 | tf_op jit(solution)/shard_map/reduce_scatter | solution.py:243
  494.3 62.0 %reduce-scatter.17.cloned.1.call-done = bf16[328,1024]{1,0:T(8,128)(2,1)} async-done(((bf16[2624,1024]{1,0:T(8,128)(2,1)}), bf16[328,1024]{1,0:T(8,128)(2,1)}) %reduce-scatter.17.cloned.1.call-update) | async-done | bytes 671760 | tf_op jit(solution)/shard_map/reduce_scatter | solution.py:249
  556.3 70.6 %reduce-scatter.11.cloned.1.call-done = bf16[128,3072]{1,0:T(8,128)(2,1)} async-done(((bf16[1024,3072]{1,0:T(8,128)(2,1)}), bf16[128,3072]{1,0:T(8,128)(2,1)}) %reduce-scatter.11.cloned.1.call-update) | async-done | bytes 786448 | tf_op jit(solution)/shard_map/reduce_scatter | solution.py:240
  627.0 112.6 %reduce-scatter.15.cloned.1.call-done = bf16[128,5248]{1,0:T(8,128)(2,1)} async-done(((bf16[1024,5248]{1,0:T(8,128)(2,1)}), bf16[128,5248]{1,0:T(8,128)(2,1)}) %reduce-scatter.15.cloned.1.call-update) | async-done | bytes 1343504 | tf_op jit(solution)/shard_map/reduce_scatter | solution.py:246
  751.2 13.6 %all-reduce.11 = (bf16[1024]{0:T(1024)(128)(2,1)S(1)}, bf16[1024]{0:T(1024)(128)(2,1)S(1)}) all-reduce(bf16[1024]{0:T(1024)(128)(2,1)S(1)} %get-tuple-element.260, bf16[1024]{0:T(1024)(128)(2,1)S(1)} %get-tuple-element.258), channel_id=8, replica_groups=mesh['rep'=4,'inner'=8] {'inner'}, use_global_device_ids=true, to_apply=%region_28.29.clone | all-reduce | flops 2048 | bytes 8192
  764.9 9.4 %all-reduce.12 = (bf16[128]{0:T(256)(128)(2,1)S(1)}, bf16[128]{0:T(256)(128)(2,1)S(1)}) all-reduce(bf16[128]{0:T(256)(128)(2,1)S(1)} %dynamic-slice.1, bf16[128]{0:T(256)(128)(2,1)S(1)} %dynamic-slice.3), channel_id=1, replica_groups=mesh['rep'=4,'inner'=8] {'rep'}, use_global_device_ids=true, to_apply=%region_29.30 | all-reduce | flops 256 | bytes 1024 | tf_op jit(solution)/shard_map/psum | solution.py:264
  776.4 52.0 %all-reduce.16.cloned.1.call-done = (bf16[128,3072]{1,0:T(8,128)(2,1)}, bf16[128,1024]{1,0:T(8,128)(2,1)}, bf16[128,5248]{1,0:T(8,128)(2,1)}, bf16[328,1024]{1,0:T(8,128)(2,1)}) async-done(((bf16[128,3072]{1,0:T(8,128)(2,1)}, bf16[128,1024]{1,0:T(8,128)(2,1)}, bf16[128,5248]{1,0:T(8,128)(2,1)}, bf16[328,1024]{1,0:T(8,128)(2,1)}), (bf16[128,3072]{1,0:T(8,128)(2,1)}, bf16[128,1024]{1,0:T(8,128)(2,1)}, ...) | async-done | bytes 3063824 | tf_op jit(solution)/shard_map/psum | solution.py:260
  (192 shorter events, 131.9 us)
Async XLA Ops:
  7.2 70.0 %copy-start.7 = (bf16[128,1024]{1,0:T(8,128)(2,1)S(1)}, bf16[128,1024]{1,0:T(8,128)(2,1)}, u32[]{:S(2)}) copy-start(bf16[128,1024]{1,0:T(8,128)(2,1)} %param.14) | copy-start | bytes 786436
  7.2 70.0 %all-gather.9.cloned.1.call-start = ((), (), s32[]{:S(2)}) async-start(), calls=%async_computation.6 | async-start | bytes 7077888 | tf_op jit(solution)/shard_map/all_gather | solution.py:57
  7.9 104.2 %all-gather.13.cloned.1.call-start = ((), (), s32[]{:S(2)}) async-start(), calls=%async_computation.8 | async-start | bytes 2359296 | tf_op jit(solution)/shard_map/all_gather | solution.py:97
  82.4 60.0 %all-gather.11.cloned.1.call-start = ((), (), s32[]{:S(2)}) async-start(), calls=%async_computation.7 | async-start | bytes 2359296 | tf_op jit(solution)/shard_map/all_gather | solution.py:98
  83.3 89.3 %all-gather.15.cloned.1.call-start = ((), (), s32[]{:S(2)}) async-start(), calls=%async_computation.9 | async-start | bytes 2359296 | tf_op jit(solution)/shard_map/all_gather | solution.py:58
  83.8 191.3 %all-gather.17.cloned.1.call-start = ((), (), s32[]{:S(2)}) async-start(), calls=%async_computation.10 | async-start | bytes 12091392 | tf_op jit(solution)/shard_map/all_gather | solution.py:59
  84.4 247.7 %all-gather.19.cloned.1.call-start = ((), (), s32[]{:S(2)}) async-start(), calls=%async_computation.11 | async-start | bytes 6045696 | tf_op jit(solution)/shard_map/all_gather | solution.py:60
  85.0 335.7 %reduce-scatter.21.cloned.1.call-start = ((), (), s32[]{:S(2)}) async-start(), calls=%async_computation.17 | async-start | bytes 2359296
  275.1 57.0 %copy-start.16 = (bf16[128,1024]{1,0:T(8,128)(2,1)S(1)}, bf16[128,1024]{1,0:T(8,128)(2,1)}, u32[]{:S(2)}) copy-start(bf16[128,1024]{1,0:T(8,128)(2,1)} %param.15) | copy-start | bytes 786436
  332.1 7.0 copy-start.10
  332.1 8.7 %copy-start.4 = (bf16[1024,5248]{1,0:T(8,128)(2,1)S(1)}, bf16[1024,5248]{1,0:T(8,128)(2,1)}, u32[]{:S(2)}) copy-start(bf16[1024,5248]{1,0:T(8,128)(2,1)} %all-gather.17.cloned.1.call-done) | copy-start | bytes 32243716
  340.8 4.4 copy-start.8
  386.0 71.5 %reduce-scatter.19.cloned.1.call-start = ((), (), s32[]{:S(2)}) async-start(), calls=%async_computation.16 | async-start | bytes 2359296
  398.9 95.4 %reduce-scatter.13.cloned.1.call-start = ((), (), s32[]{:S(2)}) async-start(), calls=%async_computation.13 | async-start | bytes 2359296 | tf_op jit(solution)/shard_map/reduce_scatter | solution.py:243
  402.0 154.4 %reduce-scatter.17.cloned.1.call-start = ((), (), s32[]{:S(2)}) async-start(), calls=%async_computation.15 | async-start | bytes 6045696 | tf_op jit(solution)/shard_map/reduce_scatter | solution.py:249
  407.0 51.6 %copy-start.6 = (f32[128,16,64]{0,2,1:T(8,128)S(1)}, f32[128,16,64]{0,2,1:T(8,128)}, u32[]{:S(2)}) copy-start(f32[128,16,64]{0,2,1:T(8,128)} %get-tuple-element.127) | copy-start | bytes 1572868
  407.1 219.9 %reduce-scatter.11.cloned.1.call-start = ((), (), s32[]{:S(2)}) async-start(), calls=%async_computation.12 | async-start | bytes 7077888 | tf_op jit(solution)/shard_map/reduce_scatter | solution.py:240
  458.9 4.6 copy-start.24
  458.9 4.6 copy-start.26
  463.5 276.0 %reduce-scatter.15.cloned.1.call-start = ((), (), s32[]{:S(2)}) async-start(), calls=%async_computation.14 | async-start | bytes 12091392 | tf_op jit(solution)/shard_map/reduce_scatter | solution.py:246
  472.3 267.3 %copy-start.32 = (u32[32]{0:T(128)S(1)}, u32[32]{0:T(128)}, u32[]{:S(2)}) copy-start(u32[32]{0:T(128)} %constant.153) | copy-start | bytes 388
  472.3 356.1 %all-reduce.16.cloned.1.call-start = ((), (), s32[]{:S(2)}) async-start(), calls=%async_computation.18 | async-start | bytes 6127616 | tf_op jit(solution)/shard_map/psum | solution.py:260
  740.8 4.3 copy-start.25
  745.1 30.3 %copy-start.15 = (f32[128,1024]{1,0:T(8,128)S(1)}, f32[128,1024]{1,0:T(8,128)}, u32[]{:S(2)}) copy-start(f32[128,1024]{1,0:T(8,128)} %copy-done.14) | copy-start | bytes 1572868
  (27 other events, 52.4 us)
Sparse Core Ops, SparseCore 0:
  9.7 67.4 all-gather.8
  82.6 29.4 all-gather.12
  114.3 28.1 all-gather.10
  143.9 28.5 all-gather.14
  174.0 101.0 all-gather.16
  276.6 55.4 all-gather.18
  386.2 34.5 reduce-scatter.20
  423.0 34.4 reduce-scatter.18
  459.8 34.4 reduce-scatter.12
  496.5 59.8 reduce-scatter.16
  558.8 68.1 reduce-scatter.10
  629.2 110.2 reduce-scatter.14
  743.5 84.9 all-reduce.15
where the time goes:
time: 849 us; the launch traced here: 842 us
  waiting for transfers between devices  616 us (73%)
  matrix products  82.5 us (10%)
  local copies, waits for them, and re-layouts  57.7 us (7%)
  blocking collectives  45.8 us (5%)
  other arithmetic  23 us (3%)
  between operations  15.4 us (2%)
    reduce_scatter x1, waiting for transfers between devices, on_device(): lax.psum_scatter(grad_in.astype(jnp.bfloat16), 'inner', scatter_dimension...  113 us
    all_gather x1, waiting for transfers between devices, on_device(): lax.all_gather(in_weight, 'inner', axis=0, tiled=True)  100 us
    reduce_scatter x1, waiting for transfers between devices, on_device(): lax.psum_scatter(grad_qkv.astype(jnp.bfloat16), 'inner', scatter_dimensio...  70.6 us
    reduce_scatter x1, waiting for transfers between devices, on_device(): lax.psum_scatter(grad_down.astype(jnp.bfloat16), 'inner', scatter_dimensi...  62 us
    all_gather x1, waiting for transfers between devices, on_device(): lax.all_gather(qkv_weight, 'inner', axis=0, tiled=True)  53.2 us
    psum x1, waiting for transfers between devices, on_device(): lax.psum(summed[0].astype(jnp.bfloat16), 'rep').astype(jnp.float32)  52 us
    unnamed x15, waiting for transfers between devices  51.4 us
    all_gather x1, waiting for transfers between devices, on_device(): lax.all_gather(down_weight, 'inner', axis=0, tiled=True)  49.7 us
  transfers between devices with their start and end apart: 13, of which 13 were waited for; matrix products, arithmetic and copies ran while one was open for 11% of the time, Pallas kernels for 0%

commit v1 on v0

v1 whole, which is shorter than its diff:
```python
import functools

import jax
import jax.numpy as jnp
from jax import lax
from jax.experimental import pallas as pl
from jax.experimental.pallas import tpu as pltpu
from jax.sharding import PartitionSpec as P

HEAD_DIM = 64
EPSILON = 1e-05
THETA = 160000.0
F32 = jnp.float32
BF16 = jnp.bfloat16
NT = (((1,), (1,)), ((), ()))
TN = (((0,), (0,)), ((), ()))
VMEM_LIMIT = 56 * 1024 * 1024


def dot(a, b):
    return jnp.dot(a, b, preferred_element_type=F32)


def dot_nt(a, b):
    return lax.dot_general(a, b, NT, preferred_element_type=F32)


def dot_tn(a, b):
    return lax.dot_general(a, b, TN, preferred_element_type=F32)


def call(body, outs, args, scratch=(), n_smem=0):
    in_specs = [pl.BlockSpec(memory_space=pltpu.SMEM)] * n_smem + [
        pl.BlockSpec(memory_space=pltpu.VMEM)
    ] * (len(args) - n_smem)
    return pl.pallas_call(
        body,
        out_shape=[jax.ShapeDtypeStruct(s, d) for s, d in outs],
        in_specs=in_specs,
        out_specs=[pl.BlockSpec(memory_space=pltpu.VMEM)] * len(outs),
        scratch_shapes=[pltpu.VMEM(s, d) for s, d in scratch],
        compiler_params=pltpu.CompilerParams(vmem_limit_bytes=VMEM_LIMIT),
    )(*args)


def hat_of(values):
    centred = values - jnp.mean(values, axis=-1, keepdims=True)
    inv = lax.rsqrt(jnp.mean(centred * centred, axis=-1, keepdims=True) + EPSILON)
    return centred * inv, inv


def partner(x):
    width = x.shape[-1]
    half = HEAD_DIM // 2
    lane = lax.broadcasted_iota(jnp.int32, x.shape, x.ndim - 1)
    ahead = pltpu.roll(x, width - half, 1)
    behind = pltpu.roll(x, half, 1)
    return jnp.where(lane % HEAD_DIM < half, ahead, behind)


def tile_lanes(table, width):
    return jnp.concatenate([table] * (width // table.shape[-1]), axis=-1)


def head_mask(h, width):
    lane = lax.broadcasted_iota(jnp.int32, (1, width), 1)
    return ((lane >= h * HEAD_DIM) & (lane < (h + 1) * HEAD_DIM)).astype(BF16)


def qkv_kernel(n_rep, refs_x, w_ref, g_ref, cos_ref, sin_ref, q_ref, kv_ref, a_ref):
    rows = refs_x[0].shape[0]
    for m in range(n_rep):
        hat, _ = hat_of(refs_x[m][...].astype(F32))
        a_ref[m * rows : (m + 1) * rows, :] = (hat * g_ref[...]).astype(BF16)
    width = q_ref.shape[1]
    step = 2 * rows if n_rep % 2 == 0 else rows
    for r0 in range(0, n_rep * rows, step):
        sl = slice(r0, r0 + step)
        proj = dot(a_ref[sl, :], w_ref[...])
        cos = tile_lanes(cos_ref[sl, :], width)
        sin = tile_lanes(sin_ref[sl, :], width)
        query = proj[:, :width]
        key = proj[:, width : 2 * width]
        q_ref[sl, :] = ((query * cos + partner(query) * sin).astype(BF16).astype(F32) * HEAD_DIM**-0.5).astype(BF16)
        kv_ref[sl, :width] = (key * cos + partner(key) * sin).astype(BF16)
        kv_ref[sl, width:] = proj[:, 2 * width :].astype(BF16)


def attend_kernel(n_part, q_ref, refs_kv, o_ref, lse_ref, k_scr, vt_scr):
    rows, width = q_ref.shape
    keys = refs_kv[0].shape[0]
    for l in range(n_part):
        k_scr[l * keys : (l + 1) * keys, :] = refs_kv[l][:, :width]
        vt_scr[:, l * keys : (l + 1) * keys] = refs_kv[l][:, width:].astype(F32).T.astype(BF16)
    heads = width // HEAD_DIM
    step = min(256, rows)

    def body(c, carry):
        r0 = pl.multiple_of(c * step, step)
        for h in range(heads):
            pair = h // 2 * 128
            q = q_ref[pl.ds(r0, step), pair : pair + 128] * head_mask(h % 2, 128)
            s = dot_nt(k_scr[:, pair : pair + 128], q)
            top = jnp.max(s, axis=0, keepdims=True)
            e = jnp.exp(s - top)
            mass = jnp.sum(e, axis=0, keepdims=True)
            lse_ref[h : h + 1, pl.ds(r0, step)] = top + jnp.log(mass)
            ot = dot(vt_scr[h * HEAD_DIM : (h + 1) * HEAD_DIM, :], e.astype(BF16)) / mass
            ot_list.append(ot)
            if h % 2 == 1:
                both = jnp.concatenate(ot_list, axis=0)
                o_ref[pl.ds(r0, step), pair : pair + 128] = both.T.astype(BF16)
                ot_list.clear()
        return carry

    ot_list = []
    lax.fori_loop(0, rows // step, body, 0)


def ff_kernel(
    n_rep, sub_j, refs_x, refs_o, wout_ref, win_ref, wdown_ref, refs_c, g_ref,
    r_ref, a_ref, m_ref, du_ref, c_ref, o_ref, da_ref, gain_ref, hat_scr, u_scr, dm_scr,
):
    rows = refs_x[0].shape[0]
    total = n_rep * rows
    quarter = refs_o[0].shape[1]
    j = sub_j[0]
    for m in range(n_rep):
        hat_scr[m * rows : (m + 1) * rows, :] = refs_x[m][...].astype(F32)
        c_ref[m * rows : (m + 1) * rows, :] = refs_c[m][...]
    for m in range(n_rep):
        start = pl.multiple_of((j ^ m) * quarter, quarter)
        for k in range(n_rep):
            at = (k ^ m) * rows
            o_ref[k * rows : (k + 1) * rows, pl.ds(start, quarter)] = refs_o[m][at : at + rows, :]
    hat_scr[...] += dot(o_ref[...], wout_ref[...])
    r_ref[...] = hat_scr[:rows, :]

    def norm_step(c, carry):
        r0 = pl.multiple_of(c * 64, 64)
        hat, _ = hat_of(hat_scr[pl.ds(r0, 64), :])
        hat_scr[pl.ds(r0, 64), :] = hat
        a_ref[pl.ds(r0, 64), :] = (hat * g_ref[...]).astype(BF16)
        return carry

    lax.fori_loop(0, total // 64, norm_step, 0)
    u_scr[...] = dot(a_ref[...], win_ref[...])
    dm_scr[...] = dot_nt(c_ref[...], wdown_ref[...])
    width = m_ref.shape[1]

    def gate_step(c, carry):
        r0 = pl.multiple_of(c * 32, 32)
        sl = pl.ds(r0, 32)
        pre = u_scr[sl, :width]
        gate = u_scr[sl, width:]
        dm = dm_scr[sl, :]
        cdf = 0.5 * (1.0 + lax.erf(pre * (0.5**0.5)))
        pdf = jnp.exp(-0.5 * pre * pre) * 0.3989422804014327
        act = pre * cdf
        m_ref[sl, :] = (act * gate).astype(BF16)
        du_ref[sl, :width] = (dm * gate * (cdf + pre * pdf)).astype(BF16)
        du_ref[sl, width:] = (dm * act).astype(BF16)
        return carry

    lax.fori_loop(0, total // 32, gate_step, 0)
    da = dot_nt(du_ref[...], win_ref[...])
    da_ref[...] = da.astype(BF16)
    gain_ref[...] = jnp.sum(da * hat_scr[...], axis=0, keepdims=True)


def ff_grads_kernel(m_ref, wdown_ref, c_ref, a_ref, du_ref, lo_ref, din_ref, ddown_ref):
    lo_ref[...] = dot(m_ref[...], wdown_ref[...]).astype(BF16)
    din_ref[...] = dot_tn(a_ref[...], du_ref[...]).astype(BF16)
    ddown_ref[...] = dot_tn(m_ref[...], c_ref[...]).astype(BF16)


def norm_back(values, gain, grad):
    hat, inv = hat_of(values)
    dhat = grad * gain
    return inv * (
        dhat
        - jnp.mean(dhat, axis=-1, keepdims=True)
        - hat * jnp.mean(dhat * hat, axis=-1, keepdims=True)
    )


def middle_kernel(n_rep, refs_da, r_ref, c_ref, g_ref, dr_ref, dz_ref):
    rows = r_ref.shape[0]
    grad = refs_da[0][:rows, :].astype(F32)
    for m in range(1, n_rep):
        grad = grad + refs_da[m][...].astype(F32)
    dr = c_ref[...].astype(F32) + norm_back(r_ref[...], g_ref[...], grad)
    dr_ref[...] = dr
    dz_ref[...] = dr.astype(BF16)


def attend_back_kernel(
    n_rep, n_part, sub_j, refs_dz, wout_ref, o_ref, q_ref, refs_kv, lse_ref, cos_ref, sin_ref,
    dq_ref, dkv_ref, refs_send, dz_ref, do_scr, k_scr, v_scr, kt_scr, delta_scr, dk_scr, dv_scr,
):
    rows, width = q_ref.shape
    keys = refs_kv[0].shape[0]
    part = refs_dz[0].shape[0]
    j = sub_j[0]
    for m in range(n_rep):
        dz_ref[m * part : (m + 1) * part, :] = refs_dz[m][...]
    start = pl.multiple_of(j * width, width)
    dout = dot_nt(dz_ref[...], wout_ref[pl.ds(start, width), :]).astype(BF16)
    do_scr[...] = dout
    prod_t = (dout.astype(F32) * o_ref[...].astype(F32)).T
    heads = width // HEAD_DIM
    for h in range(heads):
        delta_scr[h : h + 1, :] = jnp.sum(
            prod_t[h * HEAD_DIM : (h + 1) * HEAD_DIM, :], axis=0, keepdims=True
        )
    for l in range(n_part):
        sl = slice(l * keys, (l + 1) * keys)
        k_scr[sl, :] = refs_kv[l][:, :width]
        v_scr[sl, :] = refs_kv[l][:, width:]
        kt_scr[:, sl] = refs_kv[l][:, :width].astype(F32).T.astype(BF16)
    dk_scr[...] = jnp.zeros_like(dk_scr)
    dv_scr[...] = jnp.zeros_like(dv_scr)
    step = min(256, rows)

    def body(c, carry):
        r0 = pl.multiple_of(c * step, step)
        for h in range(heads):
            pair = h // 2 * 128
            lanes = slice(pair, pair + 128)
            mask = head_mask(h % 2, 128)
            q = q_ref[pl.ds(r0, step), lanes] * mask
            do = do_scr[pl.ds(r0, step), lanes] * mask
            p = jnp.exp(dot_nt(k_scr[:, lanes], q) - lse_ref[h : h + 1, pl.ds(r0, step)])
            dp = dot_nt(v_scr[:, lanes], do)
            ds = (p * (dp - delta_scr[h : h + 1, pl.ds(r0, step)])).astype(BF16)
            dv_scr[:, lanes] += dot(p.astype(BF16), do)
            dk_scr[:, lanes] += dot(ds, q)
            dq_list.append(dot(kt_scr[h * HEAD_DIM : (h + 1) * HEAD_DIM, :], ds))
            if h % 2 == 1:
                dq = jnp.concatenate(dq_list, axis=0).T * HEAD_DIM**-0.5
                dq_list.clear()
                cos = cos_ref[pl.ds(r0, step), :]
                sin = sin_ref[pl.ds(r0, step), :]
                dq_ref[pl.ds(r0, step), lanes] = (dq * cos - partner(dq) * sin).astype(BF16)
        return carry

    dq_list = []
    lax.fori_loop(0, rows // step, body, 0)
    dkv_ref[:, :width] = dk_scr[:keys, :]
    dkv_ref[:, width:] = dv_scr[:keys, :]
    for l in range(1, n_part):
        sl = slice(l * keys, (l + 1) * keys)
        refs_send[l - 1][:, :width] = dk_scr[sl, :].astype(BF16)
        refs_send[l - 1][:, width:] = dv_scr[sl, :].astype(BF16)


def out_grad_kernel(sub_j, o_ref, dz_ref, dout_ref):
    quarter = dout_ref.shape[1]
    cols = dz_ref[:, pl.ds(pl.multiple_of(sub_j[0] * quarter, quarter), quarter)]
    dout_ref[...] = dot_tn(o_ref[...], cols).astype(BF16)


def qkv_back_kernel(
    n_rep, n_part, dq_ref, dkv_ref, refs_got, cos_ref, sin_ref, a_ref, w_ref, refs_x,
    dqkv_ref, da_ref, gain_ref, dp_scr,
):
    width = dq_ref.shape[1]
    part = refs_x[0].shape[0]
    dkv = dkv_ref[...]
    for l in range(n_part - 1):
        dkv = dkv + refs_got[l][...].astype(F32)
    dk = dkv[:, :width]
    cos = tile_lanes(cos_ref[...], width)
    sin = tile_lanes(sin_ref[...], width)
    dp_scr[:, :width] = dq_ref[...]
    dp_scr[:, width : 2 * width] = (dk * cos - partner(dk) * sin).astype(BF16)
    dp_scr[:, 2 * width :] = dkv[:, width:].astype(BF16)
    dqkv_ref[...] = dot_tn(a_ref[...], dp_scr[...]).astype(BF16)
    gain = jnp.zeros(gain_ref.shape, F32)
    da = dot_nt(dp_scr[...], w_ref[...])
    da_ref[...] = da.astype(BF16)
    for m in range(n_rep):
        hat, _ = hat_of(refs_x[m][...].astype(F32))
        gain = gain + jnp.sum(da[m * part : (m + 1) * part, :] * hat, axis=0, keepdims=True)
    gain_ref[...] = gain


def last_kernel(n_rep, refs_da, x_ref, dr_ref, g_ref, out_ref):
    rows = x_ref.shape[0]
    grad = refs_da[0][:rows, :].astype(F32)
    for m in range(1, n_rep):
        grad = grad + refs_da[m][...].astype(F32)
    out_ref[...] = (dr_ref[...] + norm_back(x_ref[...].astype(F32), g_ref[...], grad)).astype(BF16)


def split_refs(counts, refs):
    out, at = [], 0
    for n in counts:
        if n is None:
            out.append(refs[at])
            at += 1
        else:
            out.append(list(refs[at : at + n]))
            at += n
    return out


def grouped(kernel, static, counts):
    def body(*refs):
        kernel(*static, *split_refs(counts, refs))

    return body


def on_device(
    n_rep, n_inner,
    tokens, cotangent, qkv_weight, out_weight, in_weight, down_weight, gain_one, gain_two,
):
    part = n_inner // n_rep
    rows, dim = tokens.shape
    sub = rows // n_rep
    w_rows = qkv_weight.shape[0]
    width = dim // n_rep
    ff_shard = down_weight.shape[0]
    unit = -(-ff_shard // n_rep)
    pitch = -(-unit // 16) * 16
    ff = pitch * n_inner
    total = n_rep * rows
    j = lax.axis_index("rep")
    i = lax.axis_index("inner")
    s = i // part
    t = i % part
    j_arr = jnp.reshape(j, (1,)).astype(jnp.int32)

    def rep_swap(x, m):
        return lax.ppermute(x, "rep", [(a, a ^ m) for a in range(n_rep)])

    def plane_swap(x, m):
        pairs = [(a * part + b, (a ^ m) * part + b) for a in range(n_rep) for b in range(part)]
        return lax.ppermute(x, "inner", pairs)

    def part_swap(x, l):
        pairs = [(a * part + b, a * part + (b ^ l)) for a in range(n_rep) for b in range(part)]
        return lax.ppermute(x, "inner", pairs)

    def rep_gather(x):
        return [x] + [rep_swap(x, m) for m in range(1, n_rep)]

    def block(x, index, size):
        return lax.dynamic_slice_in_dim(x, index * size, size, 0)

    def to_plane(x):
        got = [block(x, j, sub)] + [rep_swap(block(x, j ^ m, sub), m) for m in range(1, n_rep)]
        stack = jnp.concatenate(got, axis=0)
        pieces = [block(stack, s ^ j, sub)]
        for m in range(1, n_rep):
            pieces.append(plane_swap(block(stack, s ^ m ^ j, sub), m))
        return jnp.concatenate(pieces, axis=0)

    def from_plane(x):
        got = []
        for k in range(n_rep):
            pairs = []
            for a in range(n_rep):
                for z in range(n_rep):
                    for b in range(part):
                        pairs.append((a * n_inner + z * part + b, z * n_inner + (a ^ k) * part + b))
            got.append(lax.ppermute(block(x, s ^ j ^ k, sub), ("rep", "inner"), pairs))
        stack = jnp.concatenate(got, axis=0)
        return jnp.concatenate([block(stack, s ^ a, sub) for a in range(n_rep)], axis=0)

    w_qkv_own = jnp.concatenate(
        [lax.dynamic_slice_in_dim(qkv_weight, p * dim + j * width, width, 1) for p in range(3)], axis=1
    )
    halves = jnp.pad(in_weight.reshape(w_rows, 2 * n_inner, ff_shard), ((0, 0), (0, 0), (0, unit * n_rep - ff_shard)))
    w_in_own = lax.dynamic_slice_in_dim(halves, j * unit, unit, 2)
    w_in_own = jnp.pad(w_in_own, ((0, 0), (0, 0), (0, pitch - unit))).reshape(w_rows, 2 * ff)
    w_down_own = lax.dynamic_slice_in_dim(jnp.pad(down_weight, ((0, unit * n_rep - ff_shard), (0, 0))), j * unit, unit, 0)
    w_down_own = jnp.pad(w_down_own, ((0, pitch - unit), (0, 0)))
    w_qkv = lax.all_gather(w_qkv_own, "inner", axis=0, tiled=True)
    w_out = lax.all_gather(out_weight, "inner", axis=0, tiled=True)
    w_down = lax.all_gather(w_down_own, "inner", axis=0, tiled=True)
    w_in = lax.all_gather(w_in_own, "inner", axis=0, tiled=True)
    gains = lax.all_gather(jnp.concatenate([gain_one, gain_two])[None], "inner", axis=0, tiled=True)
    first_gain = gains[:, :w_rows].reshape(1, dim).astype(F32)
    second_gain = gains[:, w_rows:].reshape(1, dim).astype(F32)

    order = jnp.arange(total, dtype=jnp.int32)
    place = (
        ((s ^ (order // sub % n_rep)) * part + t) * rows + (j ^ (order // rows)) * sub + order % sub
    ).astype(F32)
    inv_freq = 1.0 / THETA ** (jnp.arange(HEAD_DIM // 2, dtype=F32) * (2.0 / HEAD_DIM))
    angle = place[:, None] * inv_freq[None, :]
    cos_half, sin_half = jnp.cos(angle), jnp.sin(angle)
    cos = jnp.concatenate([cos_half] * 4, axis=1)
    sin = jnp.concatenate([-sin_half, sin_half] * 2, axis=1)

    xs = rep_gather(to_plane(tokens))
    q, kv, a_one = call(
        grouped(qkv_kernel, (n_rep,), (n_rep,) + (None,) * 7),
        [((total, width), BF16), ((total, 2 * width), BF16), ((total, dim), BF16)],
        [*xs, w_qkv, first_gain, cos, sin],
    )
    kvs = [kv] + [part_swap(kv, l) for l in range(1, part)]
    heads = width // HEAD_DIM
    stat_rows = -(-heads // 8) * 8
    o, lse = call(
        grouped(attend_kernel, (part,), (None, part) + (None,) * 4),
        [((total, width), BF16), ((stat_rows, total), F32)],
        [q, *kvs],
        [((total * part, width), BF16), ((width, total * part), BF16)],
    )
    os_ = rep_gather(o)
    c_own = to_plane(cotangent)
    cs = rep_gather(c_own)
    r_own, a_two, gated, d_hidden, c_all, o_all, da_two, gain_two_part = call(
        grouped(ff_kernel, (n_rep,), (None, n_rep, n_rep, None, None, None, n_rep) + (None,) * 12),
        [
            ((rows, dim), F32), ((total, dim), BF16), ((total, ff), BF16), ((total, 2 * ff), BF16),
            ((total, dim), BF16), ((total, dim), BF16), ((total, dim), BF16), ((1, dim), F32),
        ],
        [j_arr, *xs, *os_, w_out, w_in, w_down, *cs, second_gain],
        [((total, dim), F32), ((total, 2 * ff), F32), ((total, ff), F32)],
        n_smem=1,
    )
    das = [da_two] + [rep_swap(da_two[m * rows : (m + 1) * rows], m) for m in range(1, n_rep)]
    lo, d_in, d_down = call(
        ff_grads_kernel,
        [((total, dim), BF16), ((dim, 2 * ff), BF16), ((ff, dim), BF16)],
        [gated, w_down, c_all, a_two, d_hidden],
    )
    d_in = lax.psum_scatter(d_in, "inner", scatter_dimension=0, tiled=True)
    d_down = lax.psum_scatter(d_down, "inner", scatter_dimension=0, tiled=True)
    dr, dz = call(
        grouped(middle_kernel, (n_rep,), (n_rep,) + (None,) * 5),
        [((rows, dim), F32), ((rows, dim), BF16)],
        [*das, r_own, c_own, second_gain],
    )
    dzs = rep_gather(dz)
    los = [lo[:rows]] + [rep_swap(lo[m * rows : (m + 1) * rows], m) for m in range(1, n_rep)]
    layer_own = r_own
    for piece in los:
        layer_own = layer_own + piece.astype(F32)
    layer_out = from_plane(layer_own.astype(BF16))

    back = call(
        grouped(
            attend_back_kernel,
            (n_rep, part),
            (None, n_rep, None, None, None, part, None, None, None, None, None, part - 1, None) + (None,) * 7,
        ),
        [((total, width), BF16), ((total, 2 * width), F32)]
        + [((total, 2 * width), BF16)] * (part - 1)
        + [((total, dim), BF16)],
        [j_arr, *dzs, w_out, o, q, *kvs, lse, cos, sin],
        [
            ((total, width), BF16), ((total * part, width), BF16), ((total * part, width), BF16),
            ((width, total * part), BF16), ((stat_rows, total), F32),
            ((total * part, width), F32), ((total * part, width), F32),
        ],
        n_smem=1,
    )
    dq, dkv, sends, dz_all = back[0], back[1], back[2:-1], back[-1]
    gots = [part_swap(x, l + 1) for l, x in enumerate(sends)]
    (d_out,) = call(
        out_grad_kernel,
        [((dim, width), BF16)],
        [j_arr, o_all, dz_all],
        n_smem=1,
    )
    d_out = lax.psum_scatter(d_out, "inner", scatter_dimension=0, tiled=True)
    d_qkv, da_one, gain_one_part = call(
        grouped(qkv_back_kernel, (n_rep, part), (None, None, part - 1, None, None, None, None, n_rep) + (None,) * 4),
        [((dim, 3 * width), BF16), ((total, dim), BF16), ((1, dim), F32)],
        [dq, dkv, *gots, cos, sin, a_one, w_qkv, *xs],
        [((total, 3 * width), BF16)],
    )
    d_qkv = lax.psum_scatter(d_qkv, "inner", scatter_dimension=0, tiled=True)
    das = [da_one] + [rep_swap(da_one[m * rows : (m + 1) * rows], m) for m in range(1, n_rep)]
    (grad_own,) = call(
        grouped(last_kernel, (n_rep,), (n_rep,) + (None,) * 4),
        [((rows, dim), BF16)],
        [*das, xs[0], dr, first_gain],
    )
    input_grad = from_plane(grad_own)

    def all_quarters(x):
        got = jnp.stack(rep_gather(x))
        return jnp.stack([lax.dynamic_index_in_dim(got, j ^ a, 0, keepdims=False) for a in range(n_rep)]).astype(F32)

    g_qkv = all_quarters(d_qkv).reshape(n_rep, w_rows, 3, width).transpose(1, 2, 0, 3).reshape(w_rows, 3 * dim)
    g_out = all_quarters(d_out).transpose(1, 0, 2).reshape(w_rows, dim)
    g_in = all_quarters(d_in).reshape(n_rep, w_rows, 2 * n_inner, pitch)[..., :unit]
    g_in = g_in.transpose(1, 2, 0, 3).reshape(w_rows, 2 * n_inner, n_rep * unit)[..., :ff_shard].reshape(w_rows, -1)
    g_down = all_quarters(d_down)[:, :unit].reshape(n_rep * unit, dim)[:ff_shard]
    gain_sum = lax.psum(jnp.concatenate([gain_one_part, gain_two_part]), ("rep", "inner"))
    gain_own = lax.dynamic_slice_in_dim(gain_sum, i * w_rows, w_rows, 1)
    return (layer_out, input_grad, g_qkv, g_out, g_in, g_down, gain_own[0], gain_own[1])


def solution(mesh):
    rows = P(("rep", "inner"), None)
    weight = P("inner", None)
    return jax.shard_map(
        functools.partial(on_device, mesh.shape["rep"], mesh.shape["inner"]),
        mesh=mesh,
        in_specs=(rows, rows, weight, weight, weight, weight, P("inner"), P("inner")),
        out_specs=(rows, rows, weight, weight, weight, weight, P("inner"), P("inner")),
        check_vma=False,
    )
```

time: 849 us -> 394 us (0.46)
  waiting for transfers between devices: 616 us -> 136 us
  starting transfers between devices: 0.78 us -> 88.7 us
  matrix products: 82.5 us -> 0 us
  Pallas kernels: 0 us -> 59.7 us
  local copies, waits for them, and re-layouts: 57.7 us -> 31.5 us
  other arithmetic: 23 us -> 9.43 us
    reduce_scatter x4, waiting for transfers between devices: 267 us -> 0.06 us  [the longest x1 0.02 us: on_device(): d_down = lax.psum_scatter(d_down, 'inner', scatter_dimension=0, tiled=True)]
    all_gather x6 -> x4, waiting for transfers between devices: 246 us -> 40.2 us  [the longest x1 39.9 us: on_device(): w_in = lax.all_gather(w_in_own, 'inner', axis=0, tiled=True)]
    ppermute x0 -> x55, waiting for transfers between devices: none -> 94.1 us  [the longest x39 76.7 us: rep_swap(): return lax.ppermute(x, 'rep', [(a, a ^ m) for a in range(n_rep)])]
    ppermute x0 -> x55, starting transfers between devices: none -> 88.4 us  [the longest x39 59.8 us: rep_swap(): return lax.ppermute(x, 'rep', [(a, a ^ m) for a in range(n_rep)])]
    dot_general x26 -> x0, matrix products: 82.5 us -> none  [the longest x4 18.6 us: contract_cols(): lax.dot_general(left_mat, right_mat, (((1,), (1,)), ((), ())), preferred_...]
    pallas_call x0 -> x9, Pallas kernels: none -> 59.7 us  [call(): pl.pallas_call(body, out_shape=[jax.ShapeDtypeStruct(s, d) for s, d in ou...]
    psum x1 -> x0, waiting for transfers between devices: 52 us -> none  [on_device(): lax.psum(summed[0].astype(jnp.bfloat16), 'rep').astype(jnp.float32)]
    unnamed x15 -> x8, waiting for transfers between devices: 51.4 us -> 1.46 us
  transfers between devices with their start and end apart: 13 -> 63, of which waited for: 13 -> 30; matrix products, arithmetic and copies ran while one was open for 11% -> 4% of each run, Pallas kernels for 0% -> 7%
where the time goes in v1:
time: 394 us; the launch traced here: 393 us
  waiting for transfers between devices  136 us (35%)
  starting transfers between devices  88.7 us (23%)
  Pallas kernels  59.7 us (15%)
  blocking collectives  53.4 us (14%)
  local copies, waits for them, and re-layouts  31.5 us (8%)
  between operations  15 us (4%)
  other arithmetic  9.43 us (2%)
    ppermute x39, waiting for transfers between devices, rep_swap(): return lax.ppermute(x, 'rep', [(a, a ^ m) for a in range(n_rep)])  76.7 us
    ppermute x39, starting transfers between devices, rep_swap(): return lax.ppermute(x, 'rep', [(a, a ^ m) for a in range(n_rep)])  59.8 us
    pallas_call x9, Pallas kernels, call(): pl.pallas_call(body, out_shape=[jax.ShapeDtypeStruct(s, d) for s, d in ou...  59.7 us
    psum x1, blocking collectives, on_device(): lax.psum(jnp.concatenate([gain_one_part, gain_two_part]), ('rep', 'inner'))  40.7 us
    all_gather x1, waiting for transfers between devices, on_device(): w_in = lax.all_gather(w_in_own, 'inner', axis=0, tiled=True)  39.9 us
    unnamed x89, local copies, waits for them, and re-layouts  19.5 us
    ppermute x8, starting transfers between devices, from_plane(): got.append(lax.ppermute(block(x, s ^ j ^ k, sub), ('rep', 'inner'), pairs))  17.4 us
    all_gather x1, blocking collectives, on_device(): lax.all_gather(jnp.concatenate([gain_one, gain_two])[None], 'inner', axis...  12.7 us
  transfers between devices with their start and end apart: 63, of which 30 were waited for; matrix products, arithmetic and copies ran while one was open for 4% of the time, Pallas kernels for 7%

profile of v1, /device:TPU:0, one launch (start us, length us, event | category | flops | bytes accessed | tf_op | source)
XLA Modules:
  0.0 393.4 jit_solution(15988509878300014692)
XLA Ops:
  28.2 12.7 %all-gather.1 = bf16[8,1,256]{2,1,0:T(2,128)(2,1)S(1)} all-gather(bf16[1,1,256]{2,1,0:T(2,128)(2,1)S(1)} %reshape.158), channel_id=2, replica_groups=mesh['rep'=4,'inner'=8] {'inner'}, dimensions={0}, use_global_device_ids=true | all-gather | bytes 4608 | tf_op jit(solution)/shard_map/all_gather | solution.py:384
  48.7 8.9 %collective-permute-done.15 = bf16[32,1024]{1,0:T(8,128)(2,1)S(1)} collective-permute-done((bf16[32,1024]{1,0:T(8,128)(2,1)S(1)}, bf16[32,1024]{1,0:T(8,128)(2,1)S(1)}, u32[]{:S(2)}, u32[]{:S(2)}) %collective-permute-start.15) | collective-permute-done | bytes 65568 | tf_op jit(solution)/shard_map/ppermute | solution.py:336
  58.5 4.5 %shard_map.143 = (bf16[512,256]{1,0:T(8,128)(2,1)}, bf16[512,512]{1,0:T(8,128)(2,1)}, bf16[512,1024]{1,0:T(8,128)(2,1)}) custom-call(bf16[128,1024]{1,0:T(8,128)(2,1)} %copy-done.2, bf16[128,1024]{1,0:T(8,128)(2,1)} %copy-done.4, bf16[128,1024]{1,0:T(8,128)(2,1)} %copy-done.5, bf16[128,1024]{1,0:T(8,128)(2,1)} %copy-done.6, ...), custom_call_target="tpu_custom_call" | custom-call | tf_op jit(solution)/shard_map/pallas_call | solution.py:36
  79.5 8.3 %shard_map.144 = (bf16[512,256]{1,0:T(8,128)(2,1)}, f32[8,512]{1,0:T(8,128)}) custom-call(bf16[512,256]{1,0:T(8,128)(2,1)} %get-tuple-element.33.refs_0_.refs_7_, bf16[512,512]{1,0:T(8,128)(2,1)} %get-tuple-element.34.refs_1_.refs_8_, bf16[512,512]{1,0:T(8,128)(2,1)} %copy-done.9), custom_call_target="tpu_custom_call" | custom-call | tf_op jit(solution)/shard_map/pallas_call | solution.py:36
  91.3 5.9 %collective-permute-done.10.refs_6_ = bf16[512,256]{1,0:T(8,128)(2,1)S(1)} collective-permute-done((bf16[512,256]{1,0:T(8,128)(2,1)}, bf16[512,256]{1,0:T(8,128)(2,1)S(1)}, u32[]{:S(2)}, u32[]{:S(2)}) %collective-permute-start.10) | collective-permute-done | bytes 262176 | tf_op jit(solution)/shard_map/ppermute | solution.py:336
  97.2 4.2 %collective-permute-done.11.refs_7_ = bf16[512,256]{1,0:T(8,128)(2,1)S(1)} collective-permute-done((bf16[512,256]{1,0:T(8,128)(2,1)}, bf16[512,256]{1,0:T(8,128)(2,1)S(1)}, u32[]{:S(2)}, u32[]{:S(2)}) %collective-permute-start.11) | collective-permute-done | bytes 262176 | tf_op jit(solution)/shard_map/ppermute | solution.py:336
  101.7 39.9 %all-gather.11.cloned.1.call-done.refs_10_ = bf16[1024,1536]{1,0:T(8,128)(2,1)} async-done(((bf16[128,1536]{1,0:T(8,128)(2,1)}), bf16[1024,1536]{1,0:T(8,128)(2,1)}) %all-gather.11.cloned.1.call-update) | async-done | bytes 3145744 | tf_op jit(solution)/shard_map/all_gather | solution.py:383
  141.6 14.1 %shard_map.145 = (f32[128,1024]{1,0:T(8,128)}, bf16[512,1024]{1,0:T(8,128)(2,1)}, bf16[512,768]{1,0:T(8,128)(2,1)}, bf16[512,1536]{1,0:T(8,128)(2,1)}, bf16[512,...) custom-call(s32[1]{0:T(128)} %bitcast.refs_0_.sub_j, ...), custom_call_target="tpu_custom_call" | custom-call | tf_op jit(solution)/shard_map/pallas_call | solution.py:36
  160.4 5.7 %collective-permute-done.29.refs_1_ = bf16[128,1024]{1,0:T(8,128)(2,1)S(1)} collective-permute-done((bf16[128,1024]{1,0:T(8,128)(2,1)S(1)}, bf16[128,1024]{1,0:T(8,128)(2,1)S(1)}, u32[]{:S(2)}, u32[]{:S(2)}) %collective-permute-start.29) | collective-permute-done | bytes 262176 | tf_op jit(solution)/shard_map/ppermute | solution.py:336
  166.1 6.1 %collective-permute-done.30.refs_2_ = bf16[128,1024]{1,0:T(8,128)(2,1)S(1)} collective-permute-done((bf16[128,1024]{1,0:T(8,128)(2,1)S(1)}, bf16[128,1024]{1,0:T(8,128)(2,1)S(1)}, u32[]{:S(2)}, u32[]{:S(2)}) %collective-permute-start.30) | collective-permute-done | bytes 262176 | tf_op jit(solution)/shard_map/ppermute | solution.py:336
  179.6 6.0 %collective-permute-done.32.refs_2_ = bf16[128,1024]{1,0:T(8,128)(2,1)S(1)} collective-permute-done((bf16[128,1024]{1,0:T(8,128)(2,1)}, bf16[128,1024]{1,0:T(8,128)(2,1)S(1)}, u32[]{:S(2)}, u32[]{:S(2)}) %collective-permute-start.32) | collective-permute-done | bytes 262176 | tf_op jit(solution)/shard_map/ppermute | solution.py:336
  185.5 4.9 %collective-permute-done.33.refs_3_ = bf16[128,1024]{1,0:T(8,128)(2,1)S(1)} collective-permute-done((bf16[128,1024]{1,0:T(8,128)(2,1)}, bf16[128,1024]{1,0:T(8,128)(2,1)S(1)}, u32[]{:S(2)}, u32[]{:S(2)}) %collective-permute-start.33) | collective-permute-done | bytes 262176 | tf_op jit(solution)/shard_map/ppermute | solution.py:336
  191.2 10.4 %shard_map.148 = (bf16[512,256]{1,0:T(8,128)(2,1)}, f32[512,512]{1,0:T(8,128)}, bf16[512,512]{1,0:T(8,128)(2,1)}, bf16[512,1024]{1,0:T(8,128)(2,1)}) custom-call(s32[1]{0:T(128)} %bitcast.refs_0_.sub_j, bf16[128,1024]{1,0:T(8,128)(2,1)} %get-tuple-element.43.refs_1_, bf16[128,1024]{1,0:T(8,128)(2,1)} %copy-done.28, bf16[128,1024]{1,0:T(8,128)(2,1)} %copy-done.29, ...), custom_call_target="tpu_custom_call" | custom-call | tf_op jit(solution)/shard_map/pallas_call | solution.py:36
  204.6 7.5 %shard_map.146 = (bf16[512,1024]{1,0:T(8,128)(2,1)}, bf16[1024,1536]{1,0:T(8,128)(2,1)}, bf16[768,1024]{1,0:T(8,128)(2,1)}) custom-call(bf16[512,768]{1,0:T(8,128)(2,1)} %get-tuple-element.37.m_ref, bf16[768,1024]{1,0:T(8,128)(2,1)} %all-gather.13.cloned.1.call-done.refs_11_.wdown_ref, bf16[512,1024]{1,0:T(8,128)(2,1)} %get-tuple-element.38.c_ref, ...), custom_call_target="tpu_custom_call" | custom-call | tf_op jit(solution)/shard_map/pallas_call | solution.py:36
  215.9 6.0 %shard_map.149 = (bf16[1024,768]{1,0:T(8,128)(2,1)}, bf16[512,1024]{1,0:T(8,128)(2,1)}, f32[1,1024]{1,0:T(1,128)}) custom-call(bf16[512,256]{1,0:T(8,128)(2,1)} %get-tuple-element.45.refs_0_, f32[512,512]{1,0:T(8,128)} %get-tuple-element.46.refs_1_, bf16[512,512]{1,0:T(8,128)(2,1)} %copy-done.12, f32[512,128]{1,0:T(8,128)} %get-tuple-element.165.refs_6_.refs_11_.refs_3_, ...), custom_call_target="tpu_custom_call" | custom-call | tf_op jit(solution)/shard_map/pallas_call | solution.py:36
  227.6 5.9 %collective-permute-done.22 = bf16[128,1024]{1,0:T(8,128)(2,1)S(1)} collective-permute-done((bf16[128,1024]{1,0:T(8,128)(2,1)}, bf16[128,1024]{1,0:T(8,128)(2,1)S(1)}, u32[]{:S(2)}, u32[]{:S(2)}) %collective-permute-start.22) | collective-permute-done | bytes 262176 | tf_op jit(solution)/shard_map/ppermute | solution.py:336
  233.4 5.2 %collective-permute-done.23 = bf16[128,1024]{1,0:T(8,128)(2,1)S(1)} collective-permute-done((bf16[128,1024]{1,0:T(8,128)(2,1)}, bf16[128,1024]{1,0:T(8,128)(2,1)S(1)}, u32[]{:S(2)}, u32[]{:S(2)}) %collective-permute-start.23) | collective-permute-done | bytes 262176 | tf_op jit(solution)/shard_map/ppermute | solution.py:336
  239.6 4.2 %collective-permute-start.26 = (bf16[32,1024]{1,0:T(8,128)(2,1)S(1)}, bf16[32,1024]{1,0:T(8,128)(2,1)S(1)}, u32[]{:S(2)}, u32[]{:S(2)}) collective-permute-start(bf16[32,1024]{1,0:T(8,128)(2,1)S(1)} %get-tuple-element.140), channel_id=1, source_target_pairs={{0,2},{1,3},{2,10},{3,11},{4,18},{5,19},{6,26},{7,27},{8,0},{9,1},... | collective-permute-start | bytes 196616 | tf_op jit(solution)/shard_map/ppermute | solution.py:368
  251.2 5.8 %collective-permute-start.36 = (bf16[128,1024]{1,0:T(8,128)(2,1)S(1)}, bf16[128,1024]{1,0:T(8,128)(2,1)S(1)}, u32[]{:S(2)}, u32[]{:S(2)}) collective-permute-start(bf16[128,1024]{1,0:T(8,128)(2,1)S(1)} %get-tuple-element.104), channel_id=1, source_target_pairs={{0,8},{8,0},{16,24},{24,16},{1,9},{9,1},{17,25},{25,17},{2,10},{10... | collective-permute-start | bytes 786440 | tf_op jit(solution)/shard_map/ppermute | solution.py:336
  260.4 40.7 %psum.7 = f32[2,1024]{1,0:T(2,128)S(1)} all-reduce(f32[2,1024]{1,0:T(2,128)S(1)} %pad_maximum_fusion.19), channel_id=1, replica_groups=mesh['rep'=4,'inner'=8] {'rep','inner'}, use_global_device_ids=true, to_apply=%region_4.5 | all-reduce | flops 2048 | bytes 16384 | tf_op jit(solution)/shard_map/psum | solution.py:496
  307.1 5.0 %collective-permute-start.40 = (bf16[32,1024]{1,0:T(8,128)(2,1)S(1)}, bf16[32,1024]{1,0:T(8,128)(2,1)S(1)}, u32[]{:S(2)}, u32[]{:S(2)}) collective-permute-start(bf16[32,1024]{1,0:T(8,128)(2,1)S(1)} %get-tuple-element.132), channel_id=1, source_target_pairs={{0,2},{1,3},{2,10},{3,11},{4,18},{5,19},{6,26},{7,27},{8,0},{9,1},... | collective-permute-start | bytes 196616 | tf_op jit(solution)/shard_map/ppermute | solution.py:368
  361.7 4.9 %collective-permute-done.49 = bf16[128,1536]{1,0:T(8,128)(2,1)S(1)} collective-permute-done((bf16[128,1536]{1,0:T(8,128)(2,1)}, bf16[128,1536]{1,0:T(8,128)(2,1)S(1)}, u32[]{:S(2)}, u32[]{:S(2)}) %collective-permute-start.49) | collective-permute-done | bytes 393248 | tf_op jit(solution)/shard_map/ppermute | solution.py:336
  366.6 6.0 %collective-permute-done.50 = bf16[128,1536]{1,0:T(8,128)(2,1)S(1)} collective-permute-done((bf16[128,1536]{1,0:T(8,128)(2,1)}, bf16[128,1536]{1,0:T(8,128)(2,1)S(1)}, u32[]{:S(2)}, u32[]{:S(2)}) %collective-permute-start.50) | collective-permute-done | bytes 393248 | tf_op jit(solution)/shard_map/ppermute | solution.py:336
  380.9 5.7 %reshape.161 = f32[128,5248]{1,0:T(8,128)} reshape(f32[128,16,4,82]{3,2,1,0:T(4,128)} %copy.95) | data formatting | bytes 5373952
  (269 shorter events, 150.1 us)
Async XLA Ops:
  7.2 50.5 %all-gather.7.cloned.1.call-start = ((), (), s32[]{:S(2)}) async-start(), calls=%async_computation.4 | async-start | bytes 1769472 | tf_op jit(solution)/shard_map/all_gather | solution.py:380
  9.0 82.3 %all-gather.13.cloned.1.call-start = ((), (), s32[]{:S(2)}) async-start(), calls=%async_computation.7 | async-start | bytes 1769472 | tf_op jit(solution)/shard_map/all_gather | solution.py:382
  9.9 91.8 %all-gather.9.cloned.1.call-start = ((), (), s32[]{:S(2)}) async-start(), calls=%async_computation.5 | async-start | bytes 2359296 | tf_op jit(solution)/shard_map/all_gather | solution.py:381
  10.6 131.0 %all-gather.11.cloned.1.call-start = ((), (), s32[]{:S(2)}) async-start(), calls=%async_computation.6 | async-start | bytes 3538944 | tf_op jit(solution)/shard_map/all_gather | solution.py:383
  12.9 308.8 %reduce-scatter.7.cloned.1.call-start = ((), (), s32[]{:S(2)}) async-start(), calls=%async_computation.9 | async-start | bytes 589824 | tf_op jit(solution)/shard_map/reduce_scatter | solution.py:471
  13.1 32.0 %collective-permute-start.13 = (bf16[32,1024]{1,0:T(8,128)(2,1)S(1)}, bf16[32,1024]{1,0:T(8,128)(2,1)S(1)}, u32[]{:S(2)}, u32[]{:S(2)}) collective-permute-start(bf16[32,1024]{1,0:T(8,128)(2,1)S(1)} %get-tuple-element.147), channel_id=1, source_target_pairs={{0,8},{8,0},{16,24},{24,16},{1,9},{9,1},{17,25},{25,17},{2,10},{10... | collective-permute-start | bytes 196616 | tf_op jit(solution)/shard_map/ppermute | solution.py:336
  16.1 32.6 %collective-permute-start.14 = (bf16[32,1024]{1,0:T(8,128)(2,1)S(1)}, bf16[32,1024]{1,0:T(8,128)(2,1)S(1)}, u32[]{:S(2)}, u32[]{:S(2)}) collective-permute-start(bf16[32,1024]{1,0:T(8,128)(2,1)S(1)} %get-tuple-element.149), channel_id=1, source_target_pairs={{0,16},{8,24},{16,0},{24,8},{1,17},{9,25},{17,1},{25,9},{2,18},{10... | collective-permute-start | bytes 196616 | tf_op jit(solution)/shard_map/ppermute | solution.py:336
  23.5 17.4 %collective-permute-start.3 = (bf16[32,1024]{1,0:T(8,128)(2,1)S(1)}, bf16[32,1024]{1,0:T(8,128)(2,1)S(1)}, u32[]{:S(2)}, u32[]{:S(2)}) collective-permute-start(bf16[32,1024]{1,0:T(8,128)(2,1)S(1)} %get-tuple-element.153), channel_id=1, source_target_pairs={{0,2},{1,3},{2,0},{3,1},{4,6},{5,7},{6,4},{7,5},{8,10},{9,11},{10,... | collective-permute-start | bytes 196616 | tf_op jit(solution)/shard_map/ppermute | solution.py:340
  25.6 15.3 %collective-permute-start.4 = (bf16[32,1024]{1,0:T(8,128)(2,1)S(1)}, bf16[32,1024]{1,0:T(8,128)(2,1)S(1)}, u32[]{:S(2)}, u32[]{:S(2)}) collective-permute-start(bf16[32,1024]{1,0:T(8,128)(2,1)S(1)} %get-tuple-element.152), channel_id=1, source_target_pairs={{0,4},{1,5},{2,6},{3,7},{4,0},{5,1},{6,2},{7,3},{8,12},{9,13},{10,... | collective-permute-start | bytes 196616 | tf_op jit(solution)/shard_map/ppermute | solution.py:340
  40.9 16.7 %collective-permute-start.6 = (bf16[128,1024]{1,0:T(8,128)(2,1)S(1)}, bf16[128,1024]{1,0:T(8,128)(2,1)S(1)}, u32[]{:S(2)}, u32[]{:S(2)}) collective-permute-start(bf16[128,1024]{1,0:T(8,128)(2,1)S(1)} %pad_maximum_fusion.10.refs_0_.refs_1_.refs_7_.refs_4_), channel_id=1, source_target_pairs={{0,8},{8,0},{16,24},{24,16},{1,9},{9,1},{17,25},{25,17},{2,10},{10... | collective-permute-start | bytes 786440 | tf_op jit(solution)/shard_map/ppermute | solution.py:336
  42.3 15.3 %collective-permute-start.7 = (bf16[128,1024]{1,0:T(8,128)(2,1)S(1)}, bf16[128,1024]{1,0:T(8,128)(2,1)S(1)}, u32[]{:S(2)}, u32[]{:S(2)}) collective-permute-start(bf16[128,1024]{1,0:T(8,128)(2,1)S(1)} %pad_maximum_fusion.10.refs_0_.refs_1_.refs_7_.refs_4_), channel_id=1, source_target_pairs={{0,16},{8,24},{16,0},{24,8},{1,17},{9,25},{17,1},{25,9},{2,18},{10... | collective-permute-start | bytes 786440 | tf_op jit(solution)/shard_map/ppermute | solution.py:336
  63.0 15.6 %collective-permute-start.9 = (bf16[512,512]{1,0:T(8,128)(2,1)}, bf16[512,512]{1,0:T(8,128)(2,1)S(1)}, u32[]{:S(2)}, u32[]{:S(2)}) collective-permute-start(bf16[512,512]{1,0:T(8,128)(2,1)} %get-tuple-element.34.refs_1_.refs_8_), channel_id=1, source_target_pairs={{0,1},{1,0},{2,3},{3,2},{4,5},{5,4},{6,7},{7,6},{8,9},{9,8},{10,11... | collective-permute-start | bytes 1572872 | tf_op jit(solution)/shard_map/ppermute | solution.py:344
  75.1 14.7 %collective-permute-start.19 = (bf16[128,1024]{1,0:T(8,128)(2,1)S(1)}, bf16[128,1024]{1,0:T(8,128)(2,1)S(1)}, u32[]{:S(2)}, u32[]{:S(2)}) collective-permute-start(bf16[128,1024]{1,0:T(8,128)(2,1)S(1)} %pad_maximum_fusion.14.refs_12_.refs_5_), channel_id=1, source_target_pairs={{0,8},{8,0},{16,24},{24,16},{1,9},{9,1},{17,25},{25,17},{2,10},{10... | collective-permute-start | bytes 786440 | tf_op jit(solution)/shard_map/ppermute | solution.py:336
  76.5 14.7 %collective-permute-start.20 = (bf16[128,1024]{1,0:T(8,128)(2,1)S(1)}, bf16[128,1024]{1,0:T(8,128)(2,1)S(1)}, u32[]{:S(2)}, u32[]{:S(2)}) collective-permute-start(bf16[128,1024]{1,0:T(8,128)(2,1)S(1)} %pad_maximum_fusion.14.refs_12_.refs_5_), channel_id=1, source_target_pairs={{0,16},{8,24},{16,0},{24,8},{1,17},{9,25},{17,1},{25,9},{2,18},{10... | collective-permute-start | bytes 786440 | tf_op jit(solution)/shard_map/ppermute | solution.py:336
  77.1 14.1 %collective-permute-start.21 = (bf16[128,1024]{1,0:T(8,128)(2,1)S(1)}, bf16[128,1024]{1,0:T(8,128)(2,1)S(1)}, u32[]{:S(2)}, u32[]{:S(2)}) collective-permute-start(bf16[128,1024]{1,0:T(8,128)(2,1)S(1)} %pad_maximum_fusion.14.refs_12_.refs_5_), channel_id=1, source_target_pairs={{0,24},{8,16},{16,8},{24,0},{1,25},{9,17},{17,9},{25,1},{2,26},{10... | collective-permute-start | bytes 786440 | tf_op jit(solution)/shard_map/ppermute | solution.py:336
  204.5 131.5 %reduce-scatter.11.cloned.1.call-start = ((), (), s32[]{:S(2)}) async-start(), calls=%async_computation.11 | async-start | bytes 1769472 | tf_op jit(solution)/shard_map/reduce_scatter | solution.py:433
  212.1 134.9 %reduce-scatter.5.cloned.1.call-start = ((), (), s32[]{:S(2)}) async-start(), calls=%async_computation.8 | async-start | bytes 1769472 | tf_op jit(solution)/shard_map/reduce_scatter | solution.py:478
  221.9 130.2 %reduce-scatter.9.cloned.1.call-start = ((), (), s32[]{:S(2)}) async-start(), calls=%async_computation.10 | async-start | bytes 3538944 | tf_op jit(solution)/shard_map/reduce_scatter | solution.py:432
  251.2 49.9 %collective-permute-start.36 = (bf16[128,1024]{1,0:T(8,128)(2,1)S(1)}, bf16[128,1024]{1,0:T(8,128)(2,1)S(1)}, u32[]{:S(2)}, u32[]{:S(2)}) collective-permute-start(bf16[128,1024]{1,0:T(8,128)(2,1)S(1)} %get-tuple-element.104), channel_id=1, source_target_pairs={{0,8},{8,0},{16,24},{24,16},{1,9},{9,1},{17,25},{25,17},{2,10},{10... | collective-permute-start | bytes 786440 | tf_op jit(solution)/shard_map/ppermute | solution.py:336
  257.0 44.2 %collective-permute-start.37 = (bf16[128,1024]{1,0:T(8,128)(2,1)S(1)}, bf16[128,1024]{1,0:T(8,128)(2,1)S(1)}, u32[]{:S(2)}, u32[]{:S(2)}) collective-permute-start(bf16[128,1024]{1,0:T(8,128)(2,1)S(1)} %get-tuple-element.103), channel_id=1, source_target_pairs={{0,16},{8,24},{16,0},{24,8},{1,17},{9,25},{17,1},{25,9},{2,18},{10... | collective-permute-start | bytes 786440 | tf_op jit(solution)/shard_map/ppermute | solution.py:336
  258.3 42.9 %collective-permute-start.38 = (bf16[128,1024]{1,0:T(8,128)(2,1)S(1)}, bf16[128,1024]{1,0:T(8,128)(2,1)S(1)}, u32[]{:S(2)}, u32[]{:S(2)}) collective-permute-start(bf16[128,1024]{1,0:T(8,128)(2,1)S(1)} %get-tuple-element.102), channel_id=1, source_target_pairs={{0,24},{8,16},{16,8},{24,0},{1,25},{9,17},{17,9},{25,1},{2,26},{10... | collective-permute-start | bytes 786440 | tf_op jit(solution)/shard_map/ppermute | solution.py:336
  352.1 14.5 %collective-permute-start.49 = (bf16[128,1536]{1,0:T(8,128)(2,1)}, bf16[128,1536]{1,0:T(8,128)(2,1)S(1)}, u32[]{:S(2)}, u32[]{:S(2)}) collective-permute-start(bf16[128,1536]{1,0:T(8,128)(2,1)} %reduce-scatter.9.cloned.1.call-done), channel_id=1, source_target_pairs={{0,8},{8,0},{16,24},{24,16},{1,9},{9,1},{17,25},{25,17},{2,10},{10... | collective-permute-start | bytes 1179656 | tf_op jit(solution)/shard_map/ppermute | solution.py:336
  352.1 20.5 %collective-permute-start.50 = (bf16[128,1536]{1,0:T(8,128)(2,1)}, bf16[128,1536]{1,0:T(8,128)(2,1)S(1)}, u32[]{:S(2)}, u32[]{:S(2)}) collective-permute-start(bf16[128,1536]{1,0:T(8,128)(2,1)} %reduce-scatter.9.cloned.1.call-done), channel_id=1, source_target_pairs={{0,16},{8,24},{16,0},{24,8},{1,17},{9,25},{17,1},{25,9},{2,18},{10... | collective-permute-start | bytes 1179656 | tf_op jit(solution)/shard_map/ppermute | solution.py:336
  354.1 18.5 %collective-permute-start.51 = (bf16[128,1536]{1,0:T(8,128)(2,1)}, bf16[128,1536]{1,0:T(8,128)(2,1)S(1)}, u32[]{:S(2)}, u32[]{:S(2)}) collective-permute-start(bf16[128,1536]{1,0:T(8,128)(2,1)} %reduce-scatter.9.cloned.1.call-done), channel_id=1, source_target_pairs={{0,24},{8,16},{16,8},{24,0},{1,25},{9,17},{17,9},{25,1},{2,26},{10... | collective-permute-start | bytes 1179656 | tf_op jit(solution)/shard_map/ppermute | solution.py:336
  (77 other events, 870.3 us)
Sparse Core Ops, SparseCore 0:
  10.2 33.7 all-gather.6
  46.2 24.7 all-gather.12
  72.6 29.0 all-gather.8
  103.8 37.7 all-gather.10
  204.6 28.9 reduce-scatter.6
  236.4 33.6 reduce-scatter.10
  273.0 33.0 reduce-scatter.4
  308.6 40.4 reduce-scatter.8

commit v2 on v1

v2 whole, which is shorter than its diff:
```python
import functools

import jax
import jax.numpy as jnp
from jax import lax
from jax.experimental import pallas as pl
from jax.experimental.pallas import tpu as pltpu
from jax.sharding import PartitionSpec as P

HEAD_DIM = 64
EPSILON = 1e-05
THETA = 160000.0
F32 = jnp.float32
BF16 = jnp.bfloat16
NT = (((1,), (1,)), ((), ()))
TN = (((0,), (0,)), ((), ()))
VMEM_LIMIT = 56 * 1024 * 1024


def dot(a, b):
    return jnp.dot(a, b, preferred_element_type=F32)


def dot_nt(a, b):
    return lax.dot_general(a, b, NT, preferred_element_type=F32)


def dot_tn(a, b):
    return lax.dot_general(a, b, TN, preferred_element_type=F32)


def call(body, outs, args, scratch=(), n_smem=0, n_any=0, micros=1):
    n_vmem = len(args) - n_smem - n_any
    in_specs = (
        [pl.BlockSpec(memory_space=pltpu.SMEM)] * n_smem
        + [pl.BlockSpec(memory_space=pltpu.VMEM)] * n_vmem
        + [pl.BlockSpec(memory_space=pl.ANY)] * n_any
    )

    def without_waited(*refs):
        body(*refs[: n_smem + n_vmem], *refs[len(args) :])

    return pl.pallas_call(
        without_waited,
        out_shape=[jax.ShapeDtypeStruct(s, d) for s, d in outs],
        in_specs=in_specs,
        out_specs=[pl.BlockSpec(memory_space=pltpu.VMEM)] * len(outs),
        scratch_shapes=[pltpu.VMEM(s, d) for s, d in scratch],
        compiler_params=pltpu.CompilerParams(vmem_limit_bytes=VMEM_LIMIT),
        cost_estimate=pl.CostEstimate(
            flops=int(micros * 1e9), transcendentals=0, bytes_accessed=int(micros * 1e6)
        ),
    )(*args)


def after(value, *others):
    return lax.optimization_barrier((value, *others))[0]


def hat_of(values):
    centred = values - jnp.mean(values, axis=-1, keepdims=True)
    inv = lax.rsqrt(jnp.mean(centred * centred, axis=-1, keepdims=True) + EPSILON)
    return centred * inv, inv


def partner(x):
    width = x.shape[-1]
    half = HEAD_DIM // 2
    lane = lax.broadcasted_iota(jnp.int32, x.shape, x.ndim - 1)
    ahead = pltpu.roll(x, width - half, 1)
    behind = pltpu.roll(x, half, 1)
    return jnp.where(lane % HEAD_DIM < half, ahead, behind)


def tile_lanes(table, width):
    return jnp.concatenate([table] * (width // table.shape[-1]), axis=-1)


def head_mask(h, width):
    lane = lax.broadcasted_iota(jnp.int32, (1, width), 1)
    return ((lane >= h * HEAD_DIM) & (lane < (h + 1) * HEAD_DIM)).astype(BF16)


def pick_kernel(n_rep, at_ref, x_ref, outs):
    sub = x_ref.shape[0] // n_rep
    for m in range(n_rep):
        outs[m][...] = x_ref[pl.ds(pl.multiple_of((at_ref[0] ^ m) * sub, sub), sub), :]


def pick_plane_kernel(n_rep, at_ref, pieces, outs, scr):
    sub = pieces[0].shape[0]
    for m in range(n_rep):
        scr[m * sub : (m + 1) * sub, :] = pieces[m][...]
    for m in range(n_rep):
        block = at_ref[0] ^ at_ref[1] ^ m
        outs[m][...] = scr[pl.ds(pl.multiple_of(block * sub, sub), sub), :]


def place_kernel(n_rep, at_ref, pieces, out_ref):
    sub = pieces[0].shape[0]
    for k in range(n_rep):
        out_ref[pl.ds(pl.multiple_of((at_ref[1] ^ k) * sub, sub), sub), :] = pieces[k][...]


def send_back(n_rep, at_ref, scr, outs):
    sub = outs[0].shape[0]
    for k in range(n_rep):
        block = at_ref[0] ^ at_ref[1] ^ k
        outs[k][...] = scr[pl.ds(pl.multiple_of(block * sub, sub), sub), :].astype(BF16)


def weight_kernel(at_ref, qkv_ref, out_ref, gain_ref, pack_ref):
    rows, dim = out_ref.shape
    width = pack_ref.shape[1] // 4
    for p in range(3):
        start = pl.multiple_of(p * dim + at_ref[0] * width, width)
        pack_ref[:rows, p * width : (p + 1) * width] = qkv_ref[:, pl.ds(start, width)]
    start = pl.multiple_of(at_ref[0] * width, width)
    pack_ref[:rows, 3 * width :] = out_ref[:, pl.ds(start, width)]
    pack_ref[rows:, :] = gain_ref[...]


def packed_rows(pitch, dim, lanes):
    extra = pitch * dim // lanes
    spots = [(0, 0, 0, 0, extra, min(dim, lanes))]
    left = lanes - dim
    if left:
        rest = pitch - extra
        for c in range(dim // left):
            spots.append((c * rest, dim, extra, c * left, rest, left))
    return extra, spots


def ff_weight_kernel(n_rep, unit, pitch, at_ref, in_ref, down_ref, pack_ref, down_scr):
    rows = in_ref.shape[0]
    shard, dim = down_ref.shape
    lanes = pack_ref.shape[1]
    for jj in range(n_rep):
        size = min(unit, shard - jj * unit)

        @pl.when(at_ref[0] == jj)
        def _(jj=jj, size=size):
            pieces = []
            for p in range(in_ref.shape[1] // shard):
                first = p * shard + jj * unit
                pieces.append(in_ref[:, first : first + size])
                pieces.append(jnp.zeros((rows, pitch - size), BF16))
            pack_ref[:rows, :] = jnp.concatenate(pieces, axis=1)
            down_scr[:size, :] = down_ref[jj * unit : jj * unit + size, :]
            down_scr[size:, :] = jnp.zeros((pitch - size, dim), BF16)

    _, spots = packed_rows(pitch, dim, lanes)
    for row, lane, row_in, col_in, n, w in spots:
        pack_ref[rows + row : rows + row + n, lane : lane + w] = down_scr[row_in : row_in + n, col_in : col_in + w]


def qkv_kernel(
    n_rep, n_part, at_ref, refs_x, refs_own, refs_other, cos_ref, sin_ref,
    q_ref, kv_ref, a_ref, w_ref, gains_ref,
):
    rows = refs_x[0].shape[0]
    width = q_ref.shape[1]
    dim = a_ref.shape[1]
    lanes = 4 * width
    high = refs_own[0].shape[0]
    w_rows = high - 8
    gains = jnp.zeros((8, lanes), F32)
    for l in range(n_part):
        for m in range(n_rep):
            ref, base = (refs_own[m], 0) if l == 0 else (refs_other[l - 1], m * high)
            shard = (at_ref[1] ^ m) * n_part + (at_ref[2] ^ l)
            start = pl.multiple_of(shard * w_rows, w_rows)
            w_ref[pl.ds(start, w_rows), :] = ref[base : base + w_rows, : 3 * width]
            gains = gains + ref[base + w_rows : base + high, :].astype(F32)
    per = dim // lanes
    for g in range(2):
        gains_ref[g : g + 1, :] = jnp.concatenate(
            [gains[g * per + k : g * per + k + 1, :] for k in range(per)], axis=1
        )
    for m in range(n_rep):
        hat, _ = hat_of(refs_x[m][...].astype(F32))
        a_ref[m * rows : (m + 1) * rows, :] = (hat * gains_ref[0:1, :]).astype(BF16)
    step = 2 * rows if n_rep % 2 == 0 else rows
    for r0 in range(0, n_rep * rows, step):
        sl = slice(r0, r0 + step)
        proj = dot(a_ref[sl, :], w_ref[...])
        cos = tile_lanes(cos_ref[sl, :], width)
        sin = tile_lanes(sin_ref[sl, :], width)
        query = proj[:, :width]
        key = proj[:, width : 2 * width]
        query = (query * cos + partner(query) * sin).astype(BF16).astype(F32)
        q_ref[sl, :] = (query * HEAD_DIM**-0.5).astype(BF16)
        kv_ref[sl, :width] = (key * cos + partner(key) * sin).astype(BF16)
        kv_ref[sl, width:] = proj[:, 2 * width :].astype(BF16)


def attend_kernel(n_part, q_ref, refs_kv, o_ref, lse_ref, k_scr, vt_scr):
    rows, width = q_ref.shape
    keys = refs_kv[0].shape[0]
    for l in range(n_part):
        k_scr[l * keys : (l + 1) * keys, :] = refs_kv[l][:, :width]
        vt_scr[:, l * keys : (l + 1) * keys] = refs_kv[l][:, width:].astype(F32).T.astype(BF16)
    heads = width // HEAD_DIM
    step = min(256, rows)

    def body(c, carry):
        r0 = pl.multiple_of(c * step, step)
        for h in range(heads):
            pair = h // 2 * 128
            q = q_ref[pl.ds(r0, step), pair : pair + 128] * head_mask(h % 2, 128)
            s = dot_nt(k_scr[:, pair : pair + 128], q)
            top = jnp.max(s, axis=0, keepdims=True)
            e = jnp.exp(s - top)
            mass = jnp.sum(e, axis=0, keepdims=True)
            lse_ref[h : h + 1, pl.ds(r0, step)] = top + jnp.log(mass)
            ot = dot(vt_scr[h * HEAD_DIM : (h + 1) * HEAD_DIM, :], e.astype(BF16)) / mass
            ot_list.append(ot)
            if h % 2 == 1:
                both = jnp.concatenate(ot_list, axis=0)
                o_ref[pl.ds(r0, step), pair : pair + 128] = both.T.astype(BF16)
                ot_list.clear()
        return carry

    ot_list = []
    lax.fori_loop(0, rows // step, body, 0)


def ff_kernel(
    n_rep, n_part, pitch, at_ref, refs_x, refs_o, refs_wo, refs_wo_other, ffw_ref, refs_c, gains_ref,
    r_ref, refs_da, a_ref, m_ref, du_ref, c_ref, o_ref, wout_ref, wdown_ref, gain_ref,
    hat_scr, u_scr, dm_scr, win_scr,
):
    rows, dim = refs_x[0].shape
    total = n_rep * rows
    quarter = refs_o[0].shape[1]
    j = at_ref[0]
    n_inner = n_rep * n_part
    w_rows = dim // n_inner
    lanes = win_scr.shape[1]
    extra, spots = packed_rows(pitch, dim, lanes)
    for k in range(n_rep):
        col = pl.multiple_of((j ^ k) * quarter, quarter)
        for l in range(n_part):
            for m in range(n_rep):
                shard = (at_ref[1] ^ m) * n_part + (at_ref[2] ^ l)
                row = pl.multiple_of(shard * w_rows, w_rows)
                if l == 0:
                    piece = refs_wo[k][m * w_rows : (m + 1) * w_rows, :]
                else:
                    at = (k * n_rep + m) * w_rows
                    piece = refs_wo_other[l - 1][at : at + w_rows, :]
                wout_ref[pl.ds(row, w_rows), pl.ds(col, quarter)] = piece
    for m in range(n_rep):
        hat_scr[m * rows : (m + 1) * rows, :] = refs_x[m][...].astype(F32)
        c_ref[m * rows : (m + 1) * rows, :] = refs_c[m][...]
        col = pl.multiple_of((j ^ m) * quarter, quarter)
        for k in range(n_rep):
            at = (k ^ m) * rows
            o_ref[k * rows : (k + 1) * rows, pl.ds(col, quarter)] = refs_o[m][at : at + rows, :]
    for p in range(n_inner):
        base = p * (w_rows + extra)
        win_scr[p * w_rows : (p + 1) * w_rows, :] = ffw_ref[base : base + w_rows, :]
        for row, lane, row_in, col_in, n, w in spots:
            top = base + w_rows + row
            wdown_ref[p * pitch + row_in : p * pitch + row_in + n, col_in : col_in + w] = ffw_ref[
                top : top + n, lane : lane + w
            ]
    hat_scr[...] += dot(o_ref[...], wout_ref[...])
    r_ref[...] = hat_scr[:rows, :]
    gain = gains_ref[1:2, :]

    def norm_step(c, carry):
        r0 = pl.multiple_of(c * 64, 64)
        hat, _ = hat_of(hat_scr[pl.ds(r0, 64), :])
        hat_scr[pl.ds(r0, 64), :] = hat
        a_ref[pl.ds(r0, 64), :] = (hat * gain).astype(BF16)
        return carry

    lax.fori_loop(0, total // 64, norm_step, 0)
    u_scr[...] = dot(a_ref[...], win_scr[...])
    dm_scr[...] = dot_nt(c_ref[...], wdown_ref[...])
    width = m_ref.shape[1]

    def gate_step(c, carry):
        sl = pl.ds(pl.multiple_of(c * 32, 32), 32)
        pre = u_scr[sl, :width]
        gate = u_scr[sl, width:]
        dm = dm_scr[sl, :]
        cdf = 0.5 * (1.0 + lax.erf(pre * (0.5**0.5)))
        pdf = jnp.exp(-0.5 * pre * pre) * 0.3989422804014327
        act = pre * cdf
        m_ref[sl, :] = (act * gate).astype(BF16)
        du_ref[sl, :width] = (dm * gate * (cdf + pre * pdf)).astype(BF16)
        du_ref[sl, width:] = (dm * act).astype(BF16)
        return carry

    lax.fori_loop(0, total // 32, gate_step, 0)
    total_gain = jnp.zeros((1, dim), F32)
    for m in range(n_rep):
        sl = slice(m * rows, (m + 1) * rows)
        da = dot_nt(du_ref[sl, :], win_scr[...])
        refs_da[m][...] = da.astype(BF16)
        total_gain = total_gain + jnp.sum(da * hat_scr[sl, :], axis=0, keepdims=True)
    gain_ref[...] = total_gain


def ff_grads_kernel(n_rep, n_inner, pitch, m_ref, wdown_ref, c_ref, a_ref, du_ref, refs_lo, grad_ref, down_scr):
    rows, dim = refs_lo[0].shape
    w_rows = dim // n_inner
    lanes = du_ref.shape[1]
    extra, spots = packed_rows(pitch, dim, lanes)
    high = w_rows + extra
    down_scr[...] = dot_tn(m_ref[...], c_ref[...]).astype(BF16)
    din = dot_tn(a_ref[...], du_ref[...]).astype(BF16)
    for p in range(n_inner):
        grad_ref[p * high : p * high + w_rows, :] = din[p * w_rows : (p + 1) * w_rows, :]
        for row, lane, row_in, col_in, n, w in spots:
            top = p * high + w_rows + row
            grad_ref[top : top + n, lane : lane + w] = down_scr[
                p * pitch + row_in : p * pitch + row_in + n, col_in : col_in + w
            ]
    for m in range(n_rep):
        refs_lo[m][...] = dot(m_ref[m * rows : (m + 1) * rows, :], wdown_ref[...]).astype(BF16)


def norm_back(values, gain, grad):
    hat, inv = hat_of(values)
    dhat = grad * gain
    return inv * (
        dhat
        - jnp.mean(dhat, axis=-1, keepdims=True)
        - hat * jnp.mean(dhat * hat, axis=-1, keepdims=True)
    )


def sum_of(refs):
    total = refs[0][...].astype(F32)
    for ref in refs[1:]:
        total = total + ref[...].astype(F32)
    return total


def middle_kernel(n_rep, refs_da, r_ref, c_ref, gains_ref, dr_ref, dz_ref):
    dr = c_ref[...].astype(F32) + norm_back(r_ref[...], gains_ref[1:2, :], sum_of(refs_da))
    dr_ref[...] = dr
    dz_ref[...] = dr.astype(BF16)


def layer_out_kernel(n_rep, at_ref, refs_lo, r_ref, outs, scr):
    scr[...] = r_ref[...] + sum_of(refs_lo)
    send_back(n_rep, at_ref, scr, outs)


def last_kernel(n_rep, at_ref, refs_da, x_ref, dr_ref, gains_ref, outs, scr):
    back = norm_back(x_ref[...].astype(F32), gains_ref[0:1, :], sum_of(refs_da))
    scr[...] = dr_ref[...] + back
    send_back(n_rep, at_ref, scr, outs)


def attend_back_kernel(
    n_rep, n_part, sub_j, refs_dz, wout_ref, o_ref, q_ref, refs_kv, lse_ref, cos_ref, sin_ref,
    dq_ref, dkv_ref, refs_send, dz_ref, do_scr, k_scr, v_scr, kt_scr, delta_scr, dk_scr, dv_scr,
):
    rows, width = q_ref.shape
    keys = refs_kv[0].shape[0]
    part = refs_dz[0].shape[0]
    j = sub_j[0]
    for m in range(n_rep):
        dz_ref[m * part : (m + 1) * part, :] = refs_dz[m][...]
    start = pl.multiple_of(j * width, width)
    dout = dot_nt(dz_ref[...], wout_ref[pl.ds(start, width), :]).astype(BF16)
    do_scr[...] = dout
    prod_t = (dout.astype(F32) * o_ref[...].astype(F32)).T
    heads = width // HEAD_DIM
    for h in range(heads):
        delta_scr[h : h + 1, :] = jnp.sum(
            prod_t[h * HEAD_DIM : (h + 1) * HEAD_DIM, :], axis=0, keepdims=True
        )
    for l in range(n_part):
        sl = slice(l * keys, (l + 1) * keys)
        k_scr[sl, :] = refs_kv[l][:, :width]
        v_scr[sl, :] = refs_kv[l][:, width:]
        kt_scr[:, sl] = refs_kv[l][:, :width].astype(F32).T.astype(BF16)
    dk_scr[...] = jnp.zeros_like(dk_scr)
    dv_scr[...] = jnp.zeros_like(dv_scr)
    step = min(256, rows)

    def body(c, carry):
        r0 = pl.multiple_of(c * step, step)
        for h in range(heads):
            pair = h // 2 * 128
            lanes = slice(pair, pair + 128)
            mask = head_mask(h % 2, 128)
            q = q_ref[pl.ds(r0, step), lanes] * mask
            do = do_scr[pl.ds(r0, step), lanes] * mask
            p = jnp.exp(dot_nt(k_scr[:, lanes], q) - lse_ref[h : h + 1, pl.ds(r0, step)])
            dp = dot_nt(v_scr[:, lanes], do)
            ds = (p * (dp - delta_scr[h : h + 1, pl.ds(r0, step)])).astype(BF16)
            dv_scr[:, lanes] += dot(p.astype(BF16), do)
            dk_scr[:, lanes] += dot(ds, q)
            dq_list.append(dot(kt_scr[h * HEAD_DIM : (h + 1) * HEAD_DIM, :], ds))
            if h % 2 == 1:
                dq = jnp.concatenate(dq_list, axis=0).T * HEAD_DIM**-0.5
                dq_list.clear()
                cos = cos_ref[pl.ds(r0, step), :]
                sin = sin_ref[pl.ds(r0, step), :]
                dq_ref[pl.ds(r0, step), lanes] = (dq * cos - partner(dq) * sin).astype(BF16)
        return carry

    dq_list = []
    lax.fori_loop(0, rows // step, body, 0)
    dkv_ref[:, :width] = dk_scr[:keys, :]
    dkv_ref[:, width:] = dv_scr[:keys, :]
    for l in range(1, n_part):
        sl = slice(l * keys, (l + 1) * keys)
        refs_send[l - 1][:, :width] = dk_scr[sl, :].astype(BF16)
        refs_send[l - 1][:, width:] = dv_scr[sl, :].astype(BF16)


def out_grad_kernel(sub_j, o_ref, dz_ref, dout_ref):
    quarter = dout_ref.shape[1]
    cols = dz_ref[:, pl.ds(pl.multiple_of(sub_j[0] * quarter, quarter), quarter)]
    dout_ref[...] = dot_tn(o_ref[...], cols).astype(BF16)


def qkv_back_kernel(
    n_rep, n_part, at_ref, dq_ref, dkv_ref, refs_got, cos_ref, sin_ref, a_ref, w_ref, refs_x, dout_ref,
    gain_two_ref, keep_ref, refs_send, refs_da, dp_scr, grad_scr,
):
    width = dq_ref.shape[1]
    rows, dim = refs_x[0].shape
    lanes = 4 * width
    high = keep_ref.shape[0] // n_rep
    w_rows = high - 8
    dkv = dkv_ref[...]
    for got in refs_got:
        dkv = dkv + got[...].astype(F32)
    dk = dkv[:, :width]
    cos = tile_lanes(cos_ref[...], width)
    sin = tile_lanes(sin_ref[...], width)
    dp_scr[:, :width] = dq_ref[...]
    dp_scr[:, width : 2 * width] = (dk * cos - partner(dk) * sin).astype(BF16)
    dp_scr[:, 2 * width :] = dkv[:, width:].astype(BF16)
    grad_scr[:, : 3 * width] = dot_tn(a_ref[...], dp_scr[...])
    grad_scr[:, 3 * width :] = dout_ref[...].astype(F32)
    gain = jnp.zeros((1, dim), F32)
    for m in range(n_rep):
        da = dot_nt(dp_scr[m * rows : (m + 1) * rows, :], w_ref[...])
        refs_da[m][...] = da.astype(BF16)
        hat, _ = hat_of(refs_x[m][...].astype(F32))
        gain = gain + jnp.sum(da * hat, axis=0, keepdims=True)
    per = dim // lanes
    strips = [g[:, k * lanes : (k + 1) * lanes] for g in (gain, gain_two_ref[...]) for k in range(per)]
    strips.append(jnp.zeros((8 - len(strips), lanes), F32))
    gains = jnp.concatenate(strips, axis=0)
    for l in range(n_part):
        for m in range(n_rep):
            shard = (at_ref[1] ^ m) * n_part + (at_ref[2] ^ l)
            block = grad_scr[pl.ds(pl.multiple_of(shard * w_rows, w_rows), w_rows), :]
            ref = keep_ref if l == 0 else refs_send[l - 1]
            ref[m * high : m * high + w_rows, :] = block.astype(ref.dtype)
            ref[m * high + w_rows : (m + 1) * high, :] = gains.astype(ref.dtype)


def part_sum_kernel(n_rep, keep_ref, refs_got, own_ref, outs):
    high = own_ref.shape[0]
    for m in range(n_rep):
        sl = slice(m * high, (m + 1) * high)
        total = keep_ref[sl, :]
        for got in refs_got:
            total = total + got[sl, :].astype(F32)
        if m == 0:
            own_ref[...] = total
        else:
            outs[m - 1][...] = total.astype(BF16)


def plane_sum_kernel(own_ref, refs_got, out_ref):
    out_ref[...] = (own_ref[...] + sum_of(refs_got)).astype(BF16)


def grads_kernel(n_rep, at_ref, pieces, qkv_ref, out_ref, gains_ref):
    width = pieces[0].shape[1] // 4
    rows, dim = out_ref.shape
    for m in range(n_rep):
        for p in range(3):
            start = pl.multiple_of(p * dim + (at_ref[0] ^ m) * width, width)
            qkv_ref[:, pl.ds(start, width)] = pieces[m][:rows, p * width : (p + 1) * width].astype(F32)
        start = pl.multiple_of((at_ref[0] ^ m) * width, width)
        out_ref[:, pl.ds(start, width)] = pieces[m][:rows, 3 * width :].astype(F32)
    gains = pieces[0][rows:, :].astype(F32)
    for m in range(1, n_rep):
        gains = gains + pieces[m][rows:, :].astype(F32)
    gains_ref[...] = gains


def ff_out_kernel(n_rep, unit, pitch, at_ref, pieces, in_ref, down_ref, scr, down_scr):
    high, lanes = pieces[0].shape
    rows = in_ref.shape[0]
    shard, dim = down_ref.shape
    for m in range(n_rep):
        scr[at_ref[0] ^ m] = pieces[m][...]
    _, spots = packed_rows(pitch, dim, lanes)
    strips = []
    for jj in range(n_rep):
        size = min(unit, shard - jj * unit)
        for row, lane, row_in, col_in, n, w in spots:
            down_scr[row_in : row_in + n, col_in : col_in + w] = scr[
                jj, rows + row : rows + row + n, lane : lane + w
            ].astype(F32)
        down_ref[jj * unit : jj * unit + size, :] = down_scr[:size, :]
    for p in range(lanes // pitch):
        strips = []
        for jj in range(n_rep):
            size = min(unit, shard - jj * unit)
            strips.append(scr[jj, :rows, p * pitch : p * pitch + size].astype(F32))
        in_ref[:, p * shard : (p + 1) * shard] = jnp.concatenate(strips, axis=1)


def split_refs(counts, refs):
    out, at = [], 0
    for n in counts:
        if n is None:
            out.append(refs[at])
            at += 1
        else:
            out.append(list(refs[at : at + n]))
            at += n
    return out


def grouped(kernel, static, counts):
    def body(*refs):
        kernel(*static, *split_refs(counts, refs))

    return body


def on_device(
    n_rep, n_inner,
    tokens, cotangent, qkv_weight, out_weight, in_weight, down_weight, gain_one, gain_two,
):
    part = n_inner // n_rep
    rows, dim = tokens.shape
    sub = rows // n_rep
    w_rows = qkv_weight.shape[0]
    width = dim // n_rep
    lanes = 4 * width
    high = w_rows + 8
    ff_shard = down_weight.shape[0]
    unit = -(-ff_shard // n_rep)
    pitch = -(-unit // 16) * 16
    ff = pitch * n_inner
    ff_high = w_rows + pitch * dim // (2 * ff)
    total = n_rep * rows
    j = lax.axis_index("rep")
    i = lax.axis_index("inner")
    s = i // part
    t = i % part
    at = jnp.stack([j, s, t]).astype(jnp.int32)

    def rep_swap(x, m):
        return lax.ppermute(x, "rep", [(a, a ^ m) for a in range(n_rep)])

    def plane_swap(x, m):
        pairs = [(a * part + b, (a ^ m) * part + b) for a in range(n_rep) for b in range(part)]
        return lax.ppermute(x, "inner", pairs)

    def part_swap(x, l):
        pairs = [(a * part + b, a * part + (b ^ l)) for a in range(n_rep) for b in range(part)]
        return lax.ppermute(x, "inner", pairs)

    def rep_gather(x):
        return [x] + [rep_swap(x, m) for m in range(1, n_rep)]

    def rep_trade(pieces):
        return [pieces[0]] + [rep_swap(pieces[m], m) for m in range(1, n_rep)]

    def plane_trade(pieces):
        return [pieces[0]] + [plane_swap(pieces[m], m) for m in range(1, n_rep)]

    def send_home(pieces):
        got = []
        for k in range(n_rep):
            pairs = []
            for a in range(n_rep):
                for z in range(n_rep):
                    for b in range(part):
                        pairs.append((a * n_inner + z * part + b, z * n_inner + (a ^ k) * part + b))
            got.append(lax.ppermute(pieces[k], ("rep", "inner"), pairs))
        return got

    small = [((sub, dim), BF16)] * n_rep

    def pick(x):
        return call(grouped(pick_kernel, (n_rep,), (None, None, n_rep)), small, [at, x], n_smem=1)

    def pick_plane(pieces):
        return call(
            grouped(pick_plane_kernel, (n_rep,), (None, n_rep, n_rep, None)),
            small, [at, *pieces], [((rows, dim), BF16)], n_smem=1,
        )

    def place(pieces):
        return call(
            grouped(place_kernel, (n_rep,), (None, n_rep, None)), [((rows, dim), BF16)], [at, *pieces], n_smem=1
        )[0]

    x_first = rep_trade(pick(tokens))
    gain_rows = jnp.zeros((2, dim), BF16)
    gain_rows = lax.dynamic_update_slice(gain_rows, jnp.stack([gain_one, gain_two]), (0, i * w_rows))
    gain_rows = gain_rows.reshape(2 * dim // lanes, lanes)
    gain_rows = jnp.pad(gain_rows, ((0, 8 - gain_rows.shape[0]), (0, 0)))
    (w_pack,) = call(weight_kernel, [((high, lanes), BF16)], [at, qkv_weight, out_weight, gain_rows], n_smem=1)
    w_own = [w_pack] + [plane_swap(w_pack, m) for m in range(1, n_rep)]
    (ff_pack,) = call(
        grouped(ff_weight_kernel, (n_rep, unit, pitch), (None,) * 5),
        [((ff_high, 2 * ff), BF16)],
        [at, in_weight, down_weight],
        [((pitch, dim), BF16)],
        n_smem=1,
    )
    x_own = jnp.concatenate(plane_trade(pick_plane(x_first)), axis=0)
    w_own = [after(w, x_own) for w in w_own]
    ff_w = lax.all_gather(after(ff_pack, *w_own), "inner", axis=0, tiled=True)
    xs = rep_gather(x_own)
    c_first = rep_trade(pick(after(cotangent, *x_first)))
    c_own = jnp.concatenate(plane_trade(pick_plane([after(c, x_own) for c in c_first])), axis=0)

    w_other = [part_swap(jnp.concatenate(w_own, axis=0), l) for l in range(1, part)]
    wo_own = rep_gather(after(jnp.concatenate([w[:w_rows, 3 * width :] for w in w_own], axis=0), xs[-1]))
    wo_other = [part_swap(jnp.concatenate(wo_own, axis=0), l) for l in range(1, part)]

    order = jnp.arange(total, dtype=jnp.int32)
    spot = ((s ^ (order // sub % n_rep)) * part + t) * rows + (j ^ (order // rows)) * sub + order % sub
    inv_freq = 1.0 / THETA ** (jnp.arange(HEAD_DIM // 2, dtype=F32) * (2.0 / HEAD_DIM))
    angle = spot.astype(F32)[:, None] * inv_freq[None, :]
    cos_half, sin_half = jnp.cos(angle), jnp.sin(angle)
    cos = jnp.concatenate([cos_half] * 4, axis=1)
    sin = jnp.concatenate([-sin_half, sin_half] * 2, axis=1)

    q, kv, a_one, w_qkv, gains = call(
        grouped(qkv_kernel, (n_rep, part), (None, n_rep, n_rep, part - 1) + (None,) * 7),
        [
            ((total, width), BF16), ((total, 2 * width), BF16), ((total, dim), BF16),
            ((dim, 3 * width), BF16), ((2, dim), F32),
        ],
        [at, *xs, *w_own, *w_other, cos, sin],
        n_smem=1, micros=4,
    )
    kvs = [kv] + [part_swap(kv, l) for l in range(1, part)]
    heads = width // HEAD_DIM
    stat_rows = -(-heads // 8) * 8
    o, lse = call(
        grouped(attend_kernel, (part,), (None, part) + (None,) * 4),
        [((total, width), BF16), ((stat_rows, total), F32)],
        [q, *kvs],
        [((total * part, width), BF16), ((width, total * part), BF16)],
        micros=8,
    )
    os_ = rep_gather(o)
    cs = rep_gather(after(c_own, xs[-1]))
    ff_out = call(
        grouped(
            ff_kernel, (n_rep, part, pitch),
            (None, n_rep, n_rep, n_rep, part - 1, None, n_rep, None, None, n_rep) + (None,) * 12,
        ),
        [((rows, dim), F32)]
        + [((rows, dim), BF16)] * n_rep
        + [
            ((total, dim), BF16), ((total, ff), BF16), ((total, 2 * ff), BF16), ((total, dim), BF16),
            ((total, dim), BF16), ((dim, dim), BF16), ((ff, dim), BF16), ((1, dim), F32),
        ],
        [at, *xs, *os_, *wo_own, *wo_other, ff_w, *cs, gains],
        [((total, dim), F32), ((total, 2 * ff), F32), ((total, ff), F32), ((dim, 2 * ff), BF16)],
        n_smem=1, micros=14,
    )
    r_own, da_two = ff_out[0], ff_out[1 : 1 + n_rep]
    a_two, gated, d_hidden, c_all, o_all, w_out, w_down, gain_two_part = ff_out[1 + n_rep :]
    das = rep_trade(da_two)
    ff_back = call(
        grouped(ff_grads_kernel, (n_rep, n_inner, pitch), (None,) * 5 + (n_rep, None, None)),
        [((rows, dim), BF16)] * n_rep + [((n_inner * ff_high, 2 * ff), BF16)],
        [gated, w_down, c_all, a_two, d_hidden],
        [((ff, dim), BF16)],
        micros=7,
    )
    lo, ff_grad = ff_back[:-1], ff_back[-1]
    dr, dz = call(
        grouped(middle_kernel, (n_rep,), (n_rep,) + (None,) * 5),
        [((rows, dim), F32), ((rows, dim), BF16)],
        [*das, r_own, c_own, gains, ff_grad],
        n_any=1, micros=2,
    )
    ff_grad = lax.psum_scatter(ff_grad, "inner", scatter_dimension=0, tiled=True)
    dzs = rep_gather(dz)

    back = call(
        grouped(
            attend_back_kernel,
            (n_rep, part),
            (None, n_rep, None, None, None, part, None, None, None, None, None, part - 1, None) + (None,) * 7,
        ),
        [((total, width), BF16), ((total, 2 * width), F32)]
        + [((total, 2 * width), BF16)] * (part - 1)
        + [((total, dim), BF16)],
        [at, *dzs, w_out, o, q, *kvs, lse, cos, sin],
        [
            ((total, width), BF16), ((total * part, width), BF16), ((total * part, width), BF16),
            ((width, total * part), BF16), ((stat_rows, total), F32),
            ((total * part, width), F32), ((total * part, width), F32),
        ],
        n_smem=1, micros=10,
    )
    dq, dkv, sends, dz_all = back[0], back[1], back[2:-1], back[-1]
    gots = [part_swap(x, l + 1) for l, x in enumerate(sends)]
    (d_out,) = call(
        out_grad_kernel, [((dim, width), BF16)], [at, o_all, dz_all], n_smem=1, micros=2,
    )
    los = rep_trade([after(x, dzs[-1]) for x in lo])
    parts = call(
        grouped(layer_out_kernel, (n_rep,), (None, n_rep, None, n_rep, None)),
        small, [at, *los, r_own, dq], [((rows, dim), F32)], n_smem=1, n_any=1,
    )
    layer_out = place(send_home(parts))

    qkv_out = call(
        grouped(
            qkv_back_kernel, (n_rep, part),
            (None, None, None, part - 1, None, None, None, None, n_rep, None, None, None, part - 1, n_rep, None, None),
        ),
        [((n_rep * high, lanes), F32)]
        + [((n_rep * high, lanes), BF16)] * (part - 1)
        + [((rows, dim), BF16)] * n_rep,
        [at, dq, dkv, *gots, cos, sin, a_one, w_qkv, *xs, d_out, gain_two_part],
        [((total, 3 * width), BF16), ((dim, lanes), F32)],
        n_smem=1, micros=6,
    )
    keep, sends, da_one = qkv_out[0], qkv_out[1:part], qkv_out[part:]
    gots = [part_swap(x, l + 1) for l, x in enumerate(sends)]
    summed = call(
        grouped(part_sum_kernel, (n_rep,), (None, part - 1, None, n_rep - 1)),
        [((high, lanes), F32)] + [((high, lanes), BF16)] * (n_rep - 1),
        [keep, *gots],
    )
    gots = [plane_swap(x, m + 1) for m, x in enumerate(summed[1:])]
    das = rep_trade(da_one)
    parts = call(
        grouped(last_kernel, (n_rep,), (None, n_rep, None, None, None, n_rep, None)),
        small, [at, *das, xs[0], dr, gains], [((rows, dim), F32)], n_smem=1, micros=2,
    )
    input_grad = place(send_home(parts))
    (quarter,) = call(
        grouped(plane_sum_kernel, (), (None, n_rep - 1, None)), [((high, lanes), BF16)], [summed[0], *gots]
    )
    g_qkv, g_out, g_gains = call(
        grouped(grads_kernel, (n_rep,), (None, n_rep, None, None, None)),
        [((w_rows, 3 * dim), F32), ((w_rows, dim), F32), ((8, lanes), F32)],
        [at, *rep_gather(quarter)],
        n_smem=1, micros=2,
    )
    g_in, g_down = call(
        grouped(ff_out_kernel, (n_rep, unit, pitch), (None, n_rep, None, None, None, None)),
        [((w_rows, 2 * n_inner * ff_shard), F32), ((ff_shard, dim), F32)],
        [at, *rep_gather(ff_grad)],
        [((n_rep, ff_high, 2 * ff), BF16), ((pitch, dim), F32)],
        n_smem=1, micros=4,
    )
    gain_grads = g_gains[: 2 * dim // lanes].reshape(2, dim)
    gain_grads = lax.dynamic_slice_in_dim(gain_grads, i * w_rows, w_rows, 1)
    return (layer_out, input_grad, g_qkv, g_out, g_in, g_down, gain_grads[0], gain_grads[1])


def solution(mesh):
    rows = P(("rep", "inner"), None)
    weight = P("inner", None)
    return jax.shard_map(
        functools.partial(on_device, mesh.shape["rep"], mesh.shape["inner"]),
        mesh=mesh,
        in_specs=(rows, rows, weight, weight, weight, weight, P("inner"), P("inner")),
        out_specs=(rows, rows, weight, weight, weight, weight, P("inner"), P("inner")),
        check_vma=False,
    )
```

time: 394 us -> 303 us (0.77)
  blocking collectives: 53.4 us -> 0 us
  waiting for transfers between devices: 136 us -> 83.8 us
  Pallas kernels: 59.7 us -> 96.3 us
  local copies, waits for them, and re-layouts: 31.5 us -> 13.8 us
  other arithmetic: 9.43 us -> 3.76 us
    psum x1 -> x0, blocking collectives: 40.7 us -> none  [on_device(): lax.psum(jnp.concatenate([gain_one_part, gain_two_part]), ('rep', 'inner'))]
    all_gather x4 -> x1, waiting for transfers between devices: 40.2 us -> 0.01 us  [on_device(): ff_w = lax.all_gather(after(ff_pack, *w_own), 'inner', axis=0, tiled=True)]
    pallas_call x9 -> x22, Pallas kernels: 59.7 us -> 96.3 us  [call(): pl.pallas_call(without_waited, out_shape=[jax.ShapeDtypeStruct(s, d) for...]
    ppermute x39 -> x36, starting transfers between devices: 59.8 us -> 42.6 us  [rep_swap(): return lax.ppermute(x, 'rep', [(a, a ^ m) for a in range(n_rep)])]
    ppermute x39 -> x36, waiting for transfers between devices: 76.7 us -> 62.8 us  [rep_swap(): return lax.ppermute(x, 'rep', [(a, a ^ m) for a in range(n_rep)])]
    ppermute x6 -> x12, waiting for transfers between devices: 5.5 us -> 18.6 us  [plane_swap(): return lax.ppermute(x, 'inner', pairs)]
    all_gather x1 -> x0, blocking collectives: 12.7 us -> none  [on_device(): lax.all_gather(jnp.concatenate([gain_one, gain_two])[None], 'inner', axis...]
    ppermute x8, waiting for transfers between devices: 9.98 us -> 0.02 us  [send_home(): got.append(lax.ppermute(pieces[k], ('rep', 'inner'), pairs))]
  transfers between devices with their start and end apart: 63 -> 63, of which waited for: 30 -> 21; matrix products, arithmetic and copies ran while one was open for 4% -> 2% of each run, Pallas kernels for 7% -> 21%
where the time goes in v2:
time: 303 us; the launch traced here: 302 us
  Pallas kernels  96.3 us (32%)
  starting transfers between devices  89.9 us (30%)
  waiting for transfers between devices  83.8 us (28%)
  between operations  14.6 us (5%)
  local copies, waits for them, and re-layouts  13.8 us (5%)
  other arithmetic  3.76 us (1%)
    pallas_call x22, Pallas kernels, call(): pl.pallas_call(without_waited, out_shape=[jax.ShapeDtypeStruct(s, d) for...  96.3 us
    ppermute x36, waiting for transfers between devices, rep_swap(): return lax.ppermute(x, 'rep', [(a, a ^ m) for a in range(n_rep)])  62.8 us
    ppermute x36, starting transfers between devices, rep_swap(): return lax.ppermute(x, 'rep', [(a, a ^ m) for a in range(n_rep)])  42.6 us
    ppermute x8, starting transfers between devices, send_home(): got.append(lax.ppermute(pieces[k], ('rep', 'inner'), pairs))  25.2 us
    ppermute x12, starting transfers between devices, plane_swap(): return lax.ppermute(x, 'inner', pairs)  21 us
    ppermute x12, waiting for transfers between devices, plane_swap(): return lax.ppermute(x, 'inner', pairs)  18.6 us
    unnamed x148, local copies, waits for them, and re-layouts  11.9 us
  transfers between devices with their start and end apart: 63, of which 21 were waited for; matrix products, arithmetic and copies ran while one was open for 2% of the time, Pallas kernels for 21%

profile of v2, /device:TPU:0, one launch (start us, length us, event | category | flops | bytes accessed | tf_op | source)
XLA Modules:
  0.0 302.1 jit_solution(15899232912571152050)
XLA Ops:
  11.1 5.0 %collective-permute-start.11 = (bf16[136,1024]{1,0:T(8,128)(2,1)}, bf16[136,1024]{1,0:T(8,128)(2,1)S(1)}, u32[]{:S(2)}, u32[]{:S(2)}) collective-permute-start(bf16[136,1024]{1,0:T(8,128)(2,1)} %shard_map.145.refs_5_), channel_id=1, source_target_pairs={{0,6},{1,7},{2,4},{3,5},{4,2},{5,3},{6,0},{7,1},{8,14},{9,15},{10,... | collective-permute-start | bytes 835592 | tf_op jit(solution)/shard_map/ppermute | solution.py:567
  32.3 4.6 %collective-permute-done.3 = bf16[32,1024]{1,0:T(8,128)(2,1)S(1)} collective-permute-done((bf16[32,1024]{1,0:T(8,128)(2,1)}, bf16[32,1024]{1,0:T(8,128)(2,1)S(1)}, u32[]{:S(2)}, u32[]{:S(2)}) %collective-permute-start.3) | collective-permute-done | bytes 65568 | tf_op jit(solution)/shard_map/ppermute | solution.py:567
  36.9 8.1 %collective-permute-done.4 = bf16[32,1024]{1,0:T(8,128)(2,1)S(1)} collective-permute-done((bf16[32,1024]{1,0:T(8,128)(2,1)}, bf16[32,1024]{1,0:T(8,128)(2,1)S(1)}, u32[]{:S(2)}, u32[]{:S(2)}) %collective-permute-start.4) | collective-permute-done | bytes 65568 | tf_op jit(solution)/shard_map/ppermute | solution.py:567
  71.2 4.8 %shard_map.146 = (bf16[512,256]{1,0:T(8,128)(2,1)}, bf16[512,512]{1,0:T(8,128)(2,1)}, bf16[512,1024]{1,0:T(8,128)(2,1)}, bf16[1024,768]{1,0:T(8,128)(2,1)}, f32[2,1024]{1,0:T(2,128)}) custom-call(s32[3]{0:T(128)} %pad_add_fusion.refs_0_, bf16[128,1024]{1,0:T(8,128)(2,1)} %copy-done.9, bf16[128,1024]{1,0:T(8,128)(2,1)} %copy-done.26, ...), custom_call_target="tpu_custom_call" | custom-call | flops 4000000000 | bytes 4000000 | tf_op jit(solution)/shard_map/pallas_call | solution.py:43
  78.7 3.8 %collective-permute-done.18.refs_11_ = bf16[512,256]{1,0:T(8,128)(2,1)S(1)} collective-permute-done((bf16[512,256]{1,0:T(8,128)(2,1)S(1)}, bf16[512,256]{1,0:T(8,128)(2,1)S(1)}, u32[]{:S(2)}, u32[]{:S(2)}) %collective-permute-start.18) | collective-permute-done | bytes 262176 | tf_op jit(solution)/shard_map/ppermute | solution.py:563
  88.5 8.1 %shard_map.147 = (bf16[512,256]{1,0:T(8,128)(2,1)}, f32[8,512]{1,0:T(8,128)}) custom-call(bf16[512,256]{1,0:T(8,128)(2,1)} %get-tuple-element.106.refs_0_.refs_7_, bf16[512,512]{1,0:T(8,128)(2,1)} %get-tuple-element.107.refs_1_.refs_8_, bf16[512,512]{1,0:T(8,128)(2,1)} %copy-done.16), custom_call_target="tpu_custom_call" | custom-call | flops 8000000000 | bytes 8000000 | tf_op jit(solution)/shard_map/pallas_call | solution.py:43
  100.2 6.9 %collective-permute-done.16.refs_8_ = bf16[512,256]{1,0:T(8,128)(2,1)S(1)} collective-permute-done((bf16[512,256]{1,0:T(8,128)(2,1)}, bf16[512,256]{1,0:T(8,128)(2,1)S(1)}, u32[]{:S(2)}, u32[]{:S(2)}) %collective-permute-start.16) | collective-permute-done | bytes 262176 | tf_op jit(solution)/shard_map/ppermute | solution.py:563
  111.2 17.0 %shard_map.151 = (f32[128,1024]{1,0:T(8,128)}, bf16[128,1024]{1,0:T(8,128)(2,1)}, bf16[128,1024]{1,0:T(8,128)(2,1)}, bf16[128,1024]{1,0:T(8,128)(2,1)}, bf16[128...) custom-call(s32[3]{0:T(128)} %pad_add_fusion.refs_0_, ...), custom_call_target="tpu_custom_call" | custom-call | flops 14000000000 | bytes 14000000 | tf_op jit(solution)/shard_map/pallas_call | solution.py:43
  128.2 8.5 %shard_map.152 = (bf16[128,1024]{1,0:T(8,128)(2,1)}, bf16[128,1024]{1,0:T(8,128)(2,1)}, bf16[128,1024]{1,0:T(8,128)(2,1)}, bf16[128,1024]{1,0:T(8,128)(2,1)}, bf16[1536,1536]{1,0:T(8,128)(2,1)}) custom-call(bf16[512,768]{1,0:T(8,128)(2,1)} %get-tuple-element.126.refs_0_, bf16[768,1024]{1,0:T(8,128)(2,1)} %get-tuple-element.127.refs_1_, ...), custom_call_target="tpu_custom_call" | custom-call | flops 7000000000 | bytes 7000000 | tf_op jit(solution)/shard_map/pallas_call | solution.py:43
  141.1 5.7 %collective-permute-done.30.refs_1_ = bf16[128,1024]{1,0:T(8,128)(2,1)S(1)} collective-permute-done((bf16[128,1024]{1,0:T(8,128)(2,1)S(1)}, bf16[128,1024]{1,0:T(8,128)(2,1)S(1)}, u32[]{:S(2)}, u32[]{:S(2)}) %collective-permute-start.30) | collective-permute-done | bytes 262176 | tf_op jit(solution)/shard_map/ppermute | solution.py:563
  147.7 4.6 %collective-permute-done.32.refs_3_ = bf16[128,1024]{1,0:T(8,128)(2,1)S(1)} collective-permute-done((bf16[128,1024]{1,0:T(8,128)(2,1)S(1)}, bf16[128,1024]{1,0:T(8,128)(2,1)S(1)}, u32[]{:S(2)}, u32[]{:S(2)}) %collective-permute-start.32) | collective-permute-done | bytes 262176 | tf_op jit(solution)/shard_map/ppermute | solution.py:563
  159.4 5.1 %collective-permute-done.38.refs_3_ = bf16[128,1024]{1,0:T(8,128)(2,1)S(1)} collective-permute-done((bf16[128,1024]{1,0:T(8,128)(2,1)}, bf16[128,1024]{1,0:T(8,128)(2,1)S(1)}, u32[]{:S(2)}, u32[]{:S(2)}) %collective-permute-start.38) | collective-permute-done | bytes 262176 | tf_op jit(solution)/shard_map/ppermute | solution.py:563
  166.4 4.0 %collective-permute-done.33.refs_4_ = bf16[128,1024]{1,0:T(8,128)(2,1)S(1)} collective-permute-done((bf16[128,1024]{1,0:T(8,128)(2,1)}, bf16[128,1024]{1,0:T(8,128)(2,1)S(1)}, u32[]{:S(2)}, u32[]{:S(2)}) %collective-permute-start.33) | collective-permute-done | bytes 262176 | tf_op jit(solution)/shard_map/ppermute | solution.py:563
  171.1 10.8 %shard_map.154 = (bf16[512,256]{1,0:T(8,128)(2,1)}, f32[512,512]{1,0:T(8,128)}, bf16[512,512]{1,0:T(8,128)(2,1)}, bf16[512,1024]{1,0:T(8,128)(2,1)}) custom-call(s32[3]{0:T(128)} %pad_add_fusion.refs_0_, bf16[128,1024]{1,0:T(8,128)(2,1)} %get-tuple-element.138.refs_1_, bf16[128,1024]{1,0:T(8,128)(2,1)} %copy-done.49, bf16[128,1024]{1,0:T(8,128)(2,1)} %copy-done.48, ...), custom_call_target="tpu_custom_call" | custom-call | flops 10000000000 | bytes 10000000 | tf_op jit(solution)/shard_map/pallas_call | solution.py:43
  185.5 8.1 %shard_map.158 = (f32[544,1024]{1,0:T(8,128)}, bf16[544,1024]{1,0:T(8,128)(2,1)}, bf16[128,1024]{1,0:T(8,128)(2,1)}, bf16[128,1024]{1,0:T(8,128)(2,1)}, bf16[128...) custom-call(s32[3]{0:T(128)} %pad_add_fusion.refs_0_, bf16[512,256]{1,0:T(8,128)(2,1)} %get-tuple-element.148.refs_6_.refs_1_, ...), custom_call_target="tpu_custom_call" | custom-call | flops 6000000000 | bytes 6000000 | tf_op jit(solution)/shard_map/pallas_call | solution.py:43
  200.9 3.8 %collective-permute-start.52 = (bf16[136,1024]{1,0:T(8,128)(2,1)}, bf16[136,1024]{1,0:T(8,128)(2,1)S(1)}, u32[]{:S(2)}, u32[]{:S(2)}) collective-permute-start(bf16[136,1024]{1,0:T(8,128)(2,1)} %get-tuple-element.172), channel_id=1, source_target_pairs={{0,2},{1,3},{2,0},{3,1},{4,6},{5,7},{6,4},{7,5},{8,10},{9,11},{10,... | collective-permute-start | bytes 835592 | tf_op jit(solution)/shard_map/ppermute | solution.py:567
  209.1 9.6 %collective-permute-done.35.refs_3_ = bf16[128,1024]{1,0:T(8,128)(2,1)S(1)} collective-permute-done((bf16[128,1024]{1,0:T(8,128)(2,1)S(1)}, bf16[128,1024]{1,0:T(8,128)(2,1)S(1)}, u32[]{:S(2)}, u32[]{:S(2)}) %collective-permute-start.35) | collective-permute-done | bytes 262176 | tf_op jit(solution)/shard_map/ppermute | solution.py:563
  224.7 4.6 %collective-permute-done.53.refs_2_ = bf16[136,1024]{1,0:T(8,128)(2,1)S(1)} collective-permute-done((bf16[136,1024]{1,0:T(8,128)(2,1)}, bf16[136,1024]{1,0:T(8,128)(2,1)S(1)}, u32[]{:S(2)}, u32[]{:S(2)}) %collective-permute-start.53) | collective-permute-done | bytes 278560 | tf_op jit(solution)/shard_map/ppermute | solution.py:567
  230.8 5.0 %collective-permute-start.40 = (bf16[32,1024]{1,0:T(8,128)(2,1)}, bf16[32,1024]{1,0:T(8,128)(2,1)S(1)}, u32[]{:S(2)}, u32[]{:S(2)}) collective-permute-start(bf16[32,1024]{1,0:T(8,128)(2,1)} %get-tuple-element.150), channel_id=1, source_target_pairs={{0,2},{1,3},{2,10},{3,11},{4,18},{5,19},{6,26},{7,27},{8,0},{9,1},... | collective-permute-start | bytes 196616 | tf_op jit(solution)/shard_map/ppermute | solution.py:590
  239.0 4.6 %collective-permute-start.42 = (bf16[32,1024]{1,0:T(8,128)(2,1)S(1)}, bf16[32,1024]{1,0:T(8,128)(2,1)S(1)}, u32[]{:S(2)}, u32[]{:S(2)}) collective-permute-start(bf16[32,1024]{1,0:T(8,128)(2,1)S(1)} %copy-done.57), channel_id=1, source_target_pairs={{0,6},{1,7},{2,14},{3,15},{4,22},{5,23},{6,30},{7,31},{8,4},{9,5},... | collective-permute-start | bytes 196616 | tf_op jit(solution)/shard_map/ppermute | solution.py:590
  253.9 5.6 %collective-permute-start.49 = (bf16[32,1024]{1,0:T(8,128)(2,1)}, bf16[32,1024]{1,0:T(8,128)(2,1)S(1)}, u32[]{:S(2)}, u32[]{:S(2)}) collective-permute-start(bf16[32,1024]{1,0:T(8,128)(2,1)} %get-tuple-element.167), channel_id=1, source_target_pairs={{0,4},{1,5},{2,12},{3,13},{4,20},{5,21},{6,28},{7,29},{8,6},{9,7},... | collective-permute-start | bytes 196616 | tf_op jit(solution)/shard_map/ppermute | solution.py:590
  277.3 5.0 %collective-permute-done.60.refs_4_ = bf16[192,1536]{1,0:T(8,128)(2,1)S(1)} collective-permute-done((bf16[192,1536]{1,0:T(8,128)(2,1)}, bf16[192,1536]{1,0:T(8,128)(2,1)S(1)}, u32[]{:S(2)}, u32[]{:S(2)}) %collective-permute-start.60) | collective-permute-done | bytes 589856 | tf_op jit(solution)/shard_map/ppermute | solution.py:563
  282.3 5.5 %collective-permute-done.59.refs_3_ = bf16[192,1536]{1,0:T(8,128)(2,1)S(1)} collective-permute-done((bf16[192,1536]{1,0:T(8,128)(2,1)}, bf16[192,1536]{1,0:T(8,128)(2,1)S(1)}, u32[]{:S(2)}, u32[]{:S(2)}) %collective-permute-start.59) | collective-permute-done | bytes 589856 | tf_op jit(solution)/shard_map/ppermute | solution.py:563
  289.4 5.8 %shard_map.164 = (f32[128,5248]{1,0:T(8,128)}, f32[328,1024]{1,0:T(8,128)}) custom-call(s32[3]{0:T(128)} %pad_add_fusion.refs_0_, bf16[192,1536]{1,0:T(8,128)(2,1)} %reduce-scatter.2.cloned.1.call-done.refs_1_, bf16[192,1536]{1,0:T(8,128)(2,1)} %copy-done.15, bf16[192,1536]{1,0:T(8,128)(2,1)} %copy-done.14, bf16[192,1536]{1,0:T(8,128)(2,1)} %copy-done.13), custom_call_target="tpu_custom_call" | custom-call | flops 4000000000 | bytes 4000000 | tf_op jit(solution)/shard_map/pallas_call | solution.py:43
  (294 shorter events, 133.0 us)
Async XLA Ops:
  7.2 103.3 %all-gather.2.cloned.1.call-start = ((), (), s32[]{:S(2)}) async-start(), calls=%async_computation.1 | async-start | bytes 5308416 | tf_op jit(solution)/shard_map/all_gather | solution.py:625
  11.1 33.9 %collective-permute-start.11 = (bf16[136,1024]{1,0:T(8,128)(2,1)}, bf16[136,1024]{1,0:T(8,128)(2,1)S(1)}, u32[]{:S(2)}, u32[]{:S(2)}) collective-permute-start(bf16[136,1024]{1,0:T(8,128)(2,1)} %shard_map.145.refs_5_), channel_id=1, source_target_pairs={{0,6},{1,7},{2,4},{3,5},{4,2},{5,3},{6,0},{7,1},{8,14},{9,15},{10,... | collective-permute-start | bytes 835592 | tf_op jit(solution)/shard_map/ppermute | solution.py:567
  16.2 28.9 %collective-permute-start.10 = (bf16[136,1024]{1,0:T(8,128)(2,1)}, bf16[136,1024]{1,0:T(8,128)(2,1)S(1)}, u32[]{:S(2)}, u32[]{:S(2)}) collective-permute-start(bf16[136,1024]{1,0:T(8,128)(2,1)} %shard_map.145.refs_5_), channel_id=1, source_target_pairs={{0,4},{1,5},{2,6},{3,7},{4,0},{5,1},{6,2},{7,3},{8,12},{9,13},{10,... | collective-permute-start | bytes 835592 | tf_op jit(solution)/shard_map/ppermute | solution.py:567
  24.0 21.1 %collective-permute-start.9 = (bf16[136,1024]{1,0:T(8,128)(2,1)S(1)}, bf16[136,1024]{1,0:T(8,128)(2,1)S(1)}, u32[]{:S(2)}, u32[]{:S(2)}) collective-permute-start(bf16[136,1024]{1,0:T(8,128)(2,1)S(1)} %copy-done.1), channel_id=1, source_target_pairs={{0,2},{1,3},{2,0},{3,1},{4,6},{5,7},{6,4},{7,5},{8,10},{9,11},{10,... | collective-permute-start | bytes 835592 | tf_op jit(solution)/shard_map/ppermute | solution.py:567
  29.3 15.7 %collective-permute-start.4 = (bf16[32,1024]{1,0:T(8,128)(2,1)}, bf16[32,1024]{1,0:T(8,128)(2,1)S(1)}, u32[]{:S(2)}, u32[]{:S(2)}) collective-permute-start(bf16[32,1024]{1,0:T(8,128)(2,1)} %get-tuple-element.100), channel_id=1, source_target_pairs={{0,4},{1,5},{2,6},{3,7},{4,0},{5,1},{6,2},{7,3},{8,12},{9,13},{10,... | collective-permute-start | bytes 196616 | tf_op jit(solution)/shard_map/ppermute | solution.py:567
  45.1 219.3 %reduce-scatter.2.cloned.1.call-start = ((), (), s32[]{:S(2)}) async-start(), calls=%async_computation.2 | async-start | bytes 5308416 | tf_op jit(solution)/shard_map/reduce_scatter | solution.py:695
  45.3 24.9 %collective-permute-start.12 = (bf16[544,1024]{1,0:T(8,128)(2,1)S(1)}, bf16[544,1024]{1,0:T(8,128)(2,1)S(1)}, u32[]{:S(2)}, u32[]{:S(2)}) collective-permute-start(bf16[544,1024]{1,0:T(8,128)(2,1)S(1)} %pad_maximum_fusion), channel_id=1, source_target_pairs={{0,1},{1,0},{2,3},{3,2},{4,5},{5,4},{6,7},{7,6},{8,9},{9,8},{10,11... | collective-permute-start | bytes 3342344 | tf_op jit(solution)/shard_map/ppermute | solution.py:571
  59.9 16.1 %collective-permute-start.24 = (bf16[32,1024]{1,0:T(8,128)(2,1)}, bf16[32,1024]{1,0:T(8,128)(2,1)S(1)}, u32[]{:S(2)}, u32[]{:S(2)}) collective-permute-start(bf16[32,1024]{1,0:T(8,128)(2,1)} %get-tuple-element.121), channel_id=1, source_target_pairs={{0,2},{1,3},{2,0},{3,1},{4,6},{5,7},{6,4},{7,5},{8,10},{9,11},{10,... | collective-permute-start | bytes 196616 | tf_op jit(solution)/shard_map/ppermute | solution.py:567
  82.6 17.5 %collective-permute-start.20 = (bf16[2048,256]{1,0:T(8,128)(2,1)S(1)}, bf16[2048,256]{1,0:T(8,128)(2,1)S(1)}, u32[]{:S(2)}, u32[]{:S(2)}) collective-permute-start(bf16[2048,256]{1,0:T(8,128)(2,1)S(1)} %pad_maximum_fusion.1), channel_id=1, source_target_pairs={{0,1},{1,0},{2,3},{3,2},{4,5},{5,4},{6,7},{7,6},{8,9},{9,8},{10,11... | collective-permute-start | bytes 3145736 | tf_op jit(solution)/shard_map/ppermute | solution.py:571
  84.2 14.5 %collective-permute-start.29 = (bf16[128,1024]{1,0:T(8,128)(2,1)S(1)}, bf16[128,1024]{1,0:T(8,128)(2,1)S(1)}, u32[]{:S(2)}, u32[]{:S(2)}) collective-permute-start(bf16[128,1024]{1,0:T(8,128)(2,1)S(1)} %constant_dynamic-update-slice_fusion.4.refs_15_.refs_5_), channel_id=1, source_target_pairs={{0,24},{8,16},{16,8},{24,0},{1,25},{9,17},{17,9},{25,1},{2,26},{10... | collective-permute-start | bytes 786440 | tf_op jit(solution)/shard_map/ppermute | solution.py:563
  200.9 19.7 %collective-permute-start.52 = (bf16[136,1024]{1,0:T(8,128)(2,1)}, bf16[136,1024]{1,0:T(8,128)(2,1)S(1)}, u32[]{:S(2)}, u32[]{:S(2)}) collective-permute-start(bf16[136,1024]{1,0:T(8,128)(2,1)} %get-tuple-element.172), channel_id=1, source_target_pairs={{0,2},{1,3},{2,0},{3,1},{4,6},{5,7},{6,4},{7,5},{8,10},{9,11},{10,... | collective-permute-start | bytes 835592 | tf_op jit(solution)/shard_map/ppermute | solution.py:567
  204.8 13.9 %collective-permute-start.35 = (bf16[128,1024]{1,0:T(8,128)(2,1)S(1)}, bf16[128,1024]{1,0:T(8,128)(2,1)S(1)}, u32[]{:S(2)}, u32[]{:S(2)}) collective-permute-start(bf16[128,1024]{1,0:T(8,128)(2,1)S(1)} %copy-done.28), channel_id=1, source_target_pairs={{0,16},{8,24},{16,0},{24,8},{1,17},{9,25},{17,1},{25,9},{2,18},{10... | collective-permute-start | bytes 786440 | tf_op jit(solution)/shard_map/ppermute | solution.py:563
  205.6 13.5 %collective-permute-start.36 = (bf16[128,1024]{1,0:T(8,128)(2,1)S(1)}, bf16[128,1024]{1,0:T(8,128)(2,1)S(1)}, u32[]{:S(2)}, u32[]{:S(2)}) collective-permute-start(bf16[128,1024]{1,0:T(8,128)(2,1)S(1)} %copy-done.27), channel_id=1, source_target_pairs={{0,24},{8,16},{16,8},{24,0},{1,25},{9,17},{17,9},{25,1},{2,26},{10... | collective-permute-start | bytes 786440 | tf_op jit(solution)/shard_map/ppermute | solution.py:563
  206.6 22.6 %collective-permute-start.53 = (bf16[136,1024]{1,0:T(8,128)(2,1)}, bf16[136,1024]{1,0:T(8,128)(2,1)S(1)}, u32[]{:S(2)}, u32[]{:S(2)}) collective-permute-start(bf16[136,1024]{1,0:T(8,128)(2,1)} %get-tuple-element.173), channel_id=1, source_target_pairs={{0,4},{1,5},{2,6},{3,7},{4,0},{5,1},{6,2},{7,3},{8,12},{9,13},{10,... | collective-permute-start | bytes 835592 | tf_op jit(solution)/shard_map/ppermute | solution.py:567
  206.6 24.1 %collective-permute-start.54 = (bf16[136,1024]{1,0:T(8,128)(2,1)}, bf16[136,1024]{1,0:T(8,128)(2,1)S(1)}, u32[]{:S(2)}, u32[]{:S(2)}) collective-permute-start(bf16[136,1024]{1,0:T(8,128)(2,1)} %get-tuple-element.174), channel_id=1, source_target_pairs={{0,6},{1,7},{2,4},{3,5},{4,2},{5,3},{6,0},{7,1},{8,14},{9,15},{10,... | collective-permute-start | bytes 835592 | tf_op jit(solution)/shard_map/ppermute | solution.py:567
  218.7 24.9 %collective-permute-start.44 = (bf16[128,1024]{1,0:T(8,128)(2,1)S(1)}, bf16[128,1024]{1,0:T(8,128)(2,1)S(1)}, u32[]{:S(2)}, u32[]{:S(2)}) collective-permute-start(bf16[128,1024]{1,0:T(8,128)(2,1)S(1)} %copy-done.32), channel_id=1, source_target_pairs={{0,8},{8,0},{16,24},{24,16},{1,9},{9,1},{17,25},{25,17},{2,10},{10... | collective-permute-start | bytes 786440 | tf_op jit(solution)/shard_map/ppermute | solution.py:563
  219.1 25.1 %collective-permute-start.45 = (bf16[128,1024]{1,0:T(8,128)(2,1)S(1)}, bf16[128,1024]{1,0:T(8,128)(2,1)S(1)}, u32[]{:S(2)}, u32[]{:S(2)}) collective-permute-start(bf16[128,1024]{1,0:T(8,128)(2,1)S(1)} %copy-done.31), channel_id=1, source_target_pairs={{0,16},{8,24},{16,0},{24,8},{1,17},{9,25},{17,1},{25,9},{2,18},{10... | collective-permute-start | bytes 786440 | tf_op jit(solution)/shard_map/ppermute | solution.py:563
  220.7 24.6 %collective-permute-start.46 = (bf16[128,1024]{1,0:T(8,128)(2,1)S(1)}, bf16[128,1024]{1,0:T(8,128)(2,1)S(1)}, u32[]{:S(2)}, u32[]{:S(2)}) collective-permute-start(bf16[128,1024]{1,0:T(8,128)(2,1)S(1)} %copy-done.30), channel_id=1, source_target_pairs={{0,24},{8,16},{16,8},{24,0},{1,25},{9,17},{17,9},{25,1},{2,26},{10... | collective-permute-start | bytes 786440 | tf_op jit(solution)/shard_map/ppermute | solution.py:563
  243.6 24.8 %collective-permute-start.57 = (bf16[136,1024]{1,0:T(8,128)(2,1)}, bf16[136,1024]{1,0:T(8,128)(2,1)S(1)}, u32[]{:S(2)}, u32[]{:S(2)}) collective-permute-start(bf16[136,1024]{1,0:T(8,128)(2,1)} %shard_map.162.refs_1_), channel_id=1, source_target_pairs={{0,24},{8,16},{16,8},{24,0},{1,25},{9,17},{17,9},{25,1},{2,26},{10... | collective-permute-start | bytes 835592 | tf_op jit(solution)/shard_map/ppermute | solution.py:563
  244.2 27.7 %collective-permute-start.56 = (bf16[136,1024]{1,0:T(8,128)(2,1)}, bf16[136,1024]{1,0:T(8,128)(2,1)S(1)}, u32[]{:S(2)}, u32[]{:S(2)}) collective-permute-start(bf16[136,1024]{1,0:T(8,128)(2,1)} %shard_map.162.refs_1_), channel_id=1, source_target_pairs={{0,16},{8,24},{16,0},{24,8},{1,17},{9,25},{17,1},{25,9},{2,18},{10... | collective-permute-start | bytes 835592 | tf_op jit(solution)/shard_map/ppermute | solution.py:563
  245.2 26.7 %collective-permute-start.55 = (bf16[136,1024]{1,0:T(8,128)(2,1)}, bf16[136,1024]{1,0:T(8,128)(2,1)S(1)}, u32[]{:S(2)}, u32[]{:S(2)}) collective-permute-start(bf16[136,1024]{1,0:T(8,128)(2,1)} %shard_map.162.refs_1_), channel_id=1, source_target_pairs={{0,8},{8,0},{16,24},{24,16},{1,9},{9,1},{17,25},{25,17},{2,10},{10... | collective-permute-start | bytes 835592 | tf_op jit(solution)/shard_map/ppermute | solution.py:563
  264.5 17.8 %collective-permute-start.60 = (bf16[192,1536]{1,0:T(8,128)(2,1)}, bf16[192,1536]{1,0:T(8,128)(2,1)S(1)}, u32[]{:S(2)}, u32[]{:S(2)}) collective-permute-start(bf16[192,1536]{1,0:T(8,128)(2,1)} %reduce-scatter.2.cloned.1.call-done.refs_1_), channel_id=1, source_target_pairs={{0,24},{8,16},{16,8},{24,0},{1,25},{9,17},{17,9},{25,1},{2,26},{10... | collective-permute-start | bytes 1769480 | tf_op jit(solution)/shard_map/ppermute | solution.py:563
  268.0 19.8 %collective-permute-start.59 = (bf16[192,1536]{1,0:T(8,128)(2,1)}, bf16[192,1536]{1,0:T(8,128)(2,1)S(1)}, u32[]{:S(2)}, u32[]{:S(2)}) collective-permute-start(bf16[192,1536]{1,0:T(8,128)(2,1)} %reduce-scatter.2.cloned.1.call-done.refs_1_), channel_id=1, source_target_pairs={{0,16},{8,24},{16,0},{24,8},{1,17},{9,25},{17,1},{25,9},{2,18},{10... | collective-permute-start | bytes 1769480 | tf_op jit(solution)/shard_map/ppermute | solution.py:563
  268.4 19.4 %collective-permute-start.58 = (bf16[192,1536]{1,0:T(8,128)(2,1)}, bf16[192,1536]{1,0:T(8,128)(2,1)S(1)}, u32[]{:S(2)}, u32[]{:S(2)}) collective-permute-start(bf16[192,1536]{1,0:T(8,128)(2,1)} %reduce-scatter.2.cloned.1.call-done.refs_1_), channel_id=1, source_target_pairs={{0,8},{8,0},{16,24},{24,16},{1,9},{9,1},{17,25},{25,17},{2,10},{10... | collective-permute-start | bytes 1769480 | tf_op jit(solution)/shard_map/ppermute | solution.py:563
  (110 other events, 936.7 us)
Sparse Core Ops, SparseCore 0:
  45.3 57.2 all-gather.1
  136.9 55.9 reduce-scatter.1

commit v3 on v2

--- a/solution.py
+++ b/solution.py
@@ -81,43 +81,36 @@
     return ((lane >= h * HEAD_DIM) & (lane < (h + 1) * HEAD_DIM)).astype(BF16)
 
 
-def pick_kernel(n_rep, at_ref, x_ref, outs):
-    sub = x_ref.shape[0] // n_rep
-    for m in range(n_rep):
-        outs[m][...] = x_ref[pl.ds(pl.multiple_of((at_ref[0] ^ m) * sub, sub), sub), :]
-
-
-def pick_plane_kernel(n_rep, at_ref, pieces, outs, scr):
-    sub = pieces[0].shape[0]
-    for m in range(n_rep):
-        scr[m * sub : (m + 1) * sub, :] = pieces[m][...]
-    for m in range(n_rep):
-        block = at_ref[0] ^ at_ref[1] ^ m
-        outs[m][...] = scr[pl.ds(pl.multiple_of(block * sub, sub), sub), :]
-
-
-def place_kernel(n_rep, at_ref, pieces, out_ref):
-    sub = pieces[0].shape[0]
+def place_kernel(n_rep, at_ref, pieces, first_ref, second_ref):
+    sub = pieces[0].shape[0] // 2
     for k in range(n_rep):
-        out_ref[pl.ds(pl.multiple_of((at_ref[1] ^ k) * sub, sub), sub), :] = pieces[k][...]
-
-
-def send_back(n_rep, at_ref, scr, outs):
-    sub = outs[0].shape[0]
+        spot = pl.ds(pl.multiple_of((at_ref[1] ^ k) * sub, sub), sub)
+        first_ref[spot, :] = pieces[k][:sub, :]
+        second_ref[spot, :] = pieces[k][sub:, :]
+
+
+def send_back(n_rep, at_ref, scr, outs, first):
+    sub = outs[0].shape[0] // 2
     for k in range(n_rep):
-        block = at_ref[0] ^ at_ref[1] ^ k
-        outs[k][...] = scr[pl.ds(pl.multiple_of(block * sub, sub), sub), :].astype(BF16)
-
-
-def weight_kernel(at_ref, qkv_ref, out_ref, gain_ref, pack_ref):
+        block = at_ref[0] ^ k
+        outs[k][first : first + sub, :] = scr[pl.ds(pl.multiple_of(block * sub, sub), sub), :].astype(BF16)
+
+
+def weight_kernel(n_inner, n_part, at_ref, qkv_ref, out_ref, gains_ref, pack_ref):
     rows, dim = out_ref.shape
-    width = pack_ref.shape[1] // 4
+    lanes = pack_ref.shape[1]
+    width = lanes // 4
     for p in range(3):
         start = pl.multiple_of(p * dim + at_ref[0] * width, width)
         pack_ref[:rows, p * width : (p + 1) * width] = qkv_ref[:, pl.ds(start, width)]
     start = pl.multiple_of(at_ref[0] * width, width)
     pack_ref[:rows, 3 * width :] = out_ref[:, pl.ds(start, width)]
-    pack_ref[rows:, :] = gain_ref[...]
+    shard = lax.broadcasted_iota(jnp.int32, (2, dim), 1) // rows
+    own = jnp.concatenate([gains_ref[...].astype(F32)] * n_inner, axis=1)
+    own = jnp.where(shard == at_ref[1] * n_part + at_ref[2], own, 0.0)
+    strips = [own[g : g + 1, k * lanes : (k + 1) * lanes] for g in range(2) for k in range(dim // lanes)]
+    strips.append(jnp.zeros((8 - len(strips), lanes), F32))
+    pack_ref[rows:, :] = jnp.concatenate(strips, axis=0).astype(BF16)
 
 
 def packed_rows(pitch, dim, lanes):
@@ -155,23 +148,21 @@
 
 
 def qkv_kernel(
-    n_rep, n_part, at_ref, refs_x, refs_own, refs_other, cos_ref, sin_ref,
+    n_rep, n_part, refs_x, pack_ref, cos_ref, sin_ref,
     q_ref, kv_ref, a_ref, w_ref, gains_ref,
 ):
     rows = refs_x[0].shape[0]
     width = q_ref.shape[1]
     dim = a_ref.shape[1]
     lanes = 4 * width
-    high = refs_own[0].shape[0]
+    n_inner = n_rep * n_part
+    high = pack_ref.shape[0] // n_inner
     w_rows = high - 8
     gains = jnp.zeros((8, lanes), F32)
-    for l in range(n_part):
-        for m in range(n_rep):
-            ref, base = (refs_own[m], 0) if l == 0 else (refs_other[l - 1], m * high)
-            shard = (at_ref[1] ^ m) * n_part + (at_ref[2] ^ l)
-            start = pl.multiple_of(shard * w_rows, w_rows)
-            w_ref[pl.ds(start, w_rows), :] = ref[base : base + w_rows, : 3 * width]
-            gains = gains + ref[base + w_rows : base + high, :].astype(F32)
+    for p in range(n_inner):
+        base = p * high
+        w_ref[p * w_rows : (p + 1) * w_rows, :] = pack_ref[base : base + w_rows, : 3 * width]
+        gains = gains + pack_ref[base + w_rows : base + high, :].astype(F32)
     per = dim // lanes
     for g in range(2):
         gains_ref[g : g + 1, :] = jnp.concatenate(
@@ -242,8 +233,7 @@
         col = pl.multiple_of((j ^ k) * quarter, quarter)
         for l in range(n_part):
             for m in range(n_rep):
-                shard = (at_ref[1] ^ m) * n_part + (at_ref[2] ^ l)
-                row = pl.multiple_of(shard * w_rows, w_rows)
+                row = pl.multiple_of((m * n_part + (at_ref[2] ^ l)) * w_rows, w_rows)
                 if l == 0:
                     piece = refs_wo[k][m * w_rows : (m + 1) * w_rows, :]
                 else:
@@ -346,15 +336,14 @@
     dz_ref[...] = dr.astype(BF16)
 
 
-def layer_out_kernel(n_rep, at_ref, refs_lo, r_ref, outs, scr):
+def last_kernel(n_rep, at_ref, refs_da, refs_lo, x_ref, dr_ref, r_ref, gains_ref, outs, scr):
+    rows = x_ref.shape[0]
+    sub = rows // n_rep
     scr[...] = r_ref[...] + sum_of(refs_lo)
-    send_back(n_rep, at_ref, scr, outs)
-
-
-def last_kernel(n_rep, at_ref, refs_da, x_ref, dr_ref, gains_ref, outs, scr):
+    send_back(n_rep, at_ref, scr, outs, sub)
     back = norm_back(x_ref[...].astype(F32), gains_ref[0:1, :], sum_of(refs_da))
     scr[...] = dr_ref[...] + back
-    send_back(n_rep, at_ref, scr, outs)
+    send_back(n_rep, at_ref, scr, outs, 0)
 
 
 def attend_back_kernel(
@@ -424,13 +413,13 @@
 
 
 def qkv_back_kernel(
-    n_rep, n_part, at_ref, dq_ref, dkv_ref, refs_got, cos_ref, sin_ref, a_ref, w_ref, refs_x, dout_ref,
-    gain_two_ref, keep_ref, refs_send, refs_da, dp_scr, grad_scr,
+    n_rep, n_inner, dq_ref, dkv_ref, refs_got, cos_ref, sin_ref, a_ref, w_ref, refs_x, dout_ref,
+    gain_two_ref, grad_ref, refs_da, dp_scr,
 ):
     width = dq_ref.shape[1]
     rows, dim = refs_x[0].shape
     lanes = 4 * width
-    high = keep_ref.shape[0] // n_rep
+    high = grad_ref.shape[0] // n_inner
     w_rows = high - 8
     dkv = dkv_ref[...]
     for got in refs_got:
@@ -441,8 +430,7 @@
     dp_scr[:, :width] = dq_ref[...]
     dp_scr[:, width : 2 * width] = (dk * cos - partner(dk) * sin).astype(BF16)
     dp_scr[:, 2 * width :] = dkv[:, width:].astype(BF16)
-    grad_scr[:, : 3 * width] = dot_tn(a_ref[...], dp_scr[...])
-    grad_scr[:, 3 * width :] = dout_ref[...].astype(F32)
+    grad = dot_tn(a_ref[...], dp_scr[...]).astype(BF16)
     gain = jnp.zeros((1, dim), F32)
     for m in range(n_rep):
         da = dot_nt(dp_scr[m * rows : (m + 1) * rows, :], w_ref[...])
@@ -452,31 +440,12 @@
     per = dim // lanes
     strips = [g[:, k * lanes : (k + 1) * lanes] for g in (gain, gain_two_ref[...]) for k in range(per)]
     strips.append(jnp.zeros((8 - len(strips), lanes), F32))
-    gains = jnp.concatenate(strips, axis=0)
-    for l in range(n_part):
-        for m in range(n_rep):
-            shard = (at_ref[1] ^ m) * n_part + (at_ref[2] ^ l)
-            block = grad_scr[pl.ds(pl.multiple_of(shard * w_rows, w_rows), w_rows), :]
-            ref = keep_ref if l == 0 else refs_send[l - 1]
-            ref[m * high : m * high + w_rows, :] = block.astype(ref.dtype)
-            ref[m * high + w_rows : (m + 1) * high, :] = gains.astype(ref.dtype)
-
-
-def part_sum_kernel(n_rep, keep_ref, refs_got, own_ref, outs):
-    high = own_ref.shape[0]
-    for m in range(n_rep):
-        sl = slice(m * high, (m + 1) * high)
-        total = keep_ref[sl, :]
-        for got in refs_got:
-            total = total + got[sl, :].astype(F32)
-        if m == 0:
-            own_ref[...] = total
-        else:
-            outs[m - 1][...] = total.astype(BF16)
-
-
-def plane_sum_kernel(own_ref, refs_got, out_ref):
-    out_ref[...] = (own_ref[...] + sum_of(refs_got)).astype(BF16)
+    gains = jnp.concatenate(strips, axis=0).astype(BF16)
+    for p in range(n_inner):
+        sl = slice(p * w_rows, (p + 1) * w_rows)
+        grad_ref[p * high : p * high + w_rows, : 3 * width] = grad[sl, :]
+        grad_ref[p * high : p * high + w_rows, 3 * width :] = dout_ref[sl, :]
+        grad_ref[p * high + w_rows : (p + 1) * high, :] = gains
 
 
 def grads_kernel(n_rep, at_ref, pieces, qkv_ref, out_ref, gains_ref):
@@ -494,12 +463,10 @@
     gains_ref[...] = gains
 
 
-def ff_out_kernel(n_rep, unit, pitch, at_ref, pieces, in_ref, down_ref, scr, down_scr):
-    high, lanes = pieces[0].shape
+def ff_out_kernel(n_rep, unit, pitch, scr, in_ref, down_ref, down_scr):
+    _, high, lanes = scr.shape
     rows = in_ref.shape[0]
     shard, dim = down_ref.shape
-    for m in range(n_rep):
-        scr[at_ref[0] ^ m] = pieces[m][...]
     _, spots = packed_rows(pitch, dim, lanes)
     strips = []
     for jj in range(n_rep):
@@ -590,49 +557,37 @@
             got.append(lax.ppermute(pieces[k], ("rep", "inner"), pairs))
         return got
 
-    small = [((sub, dim), BF16)] * n_rep
-
-    def pick(x):
-        return call(grouped(pick_kernel, (n_rep,), (None, None, n_rep)), small, [at, x], n_smem=1)
-
-    def pick_plane(pieces):
-        return call(
-            grouped(pick_plane_kernel, (n_rep,), (None, n_rep, n_rep, None)),
-            small, [at, *pieces], [((rows, dim), BF16)], n_smem=1,
-        )
-
-    def place(pieces):
-        return call(
-            grouped(place_kernel, (n_rep,), (None, n_rep, None)), [((rows, dim), BF16)], [at, *pieces], n_smem=1
-        )[0]
-
-    x_first = rep_trade(pick(tokens))
-    gain_rows = jnp.zeros((2, dim), BF16)
-    gain_rows = lax.dynamic_update_slice(gain_rows, jnp.stack([gain_one, gain_two]), (0, i * w_rows))
-    gain_rows = gain_rows.reshape(2 * dim // lanes, lanes)
-    gain_rows = jnp.pad(gain_rows, ((0, 8 - gain_rows.shape[0]), (0, 0)))
-    (w_pack,) = call(weight_kernel, [((high, lanes), BF16)], [at, qkv_weight, out_weight, gain_rows], n_smem=1)
-    w_own = [w_pack] + [plane_swap(w_pack, m) for m in range(1, n_rep)]
+    home = [((2 * sub, dim), BF16)] * n_rep
+    planes = [[z * part + b for z in range(n_rep)] for b in range(part)]
+
+    (w_pack,) = call(
+        functools.partial(weight_kernel, n_inner, part), [((high, lanes), BF16)],
+        [at, qkv_weight, out_weight, jnp.stack([gain_one, gain_two])], n_smem=1,
+    )
+    w_all = lax.all_gather(w_pack, "inner", axis=0, tiled=True)
+    x_first = lax.all_to_all(after(tokens, w_pack), "rep", 0, 0, tiled=True)
+    in_late = after(in_weight, x_first)
+    x_own = lax.all_to_all(x_first, "inner", 0, 0, axis_index_groups=planes, tiled=True)
+    c_first = lax.all_to_all(after(cotangent, x_first), "rep", 0, 0, tiled=True)
+    x_own = after(x_own, c_first)
+    c_own = lax.all_to_all(after(c_first, x_own), "inner", 0, 0, axis_index_groups=planes, tiled=True)
+    xs = rep_gather(x_own)
     (ff_pack,) = call(
         grouped(ff_weight_kernel, (n_rep, unit, pitch), (None,) * 5),
         [((ff_high, 2 * ff), BF16)],
-        [at, in_weight, down_weight],
+        [at, in_late, down_weight, w_pack],
         [((pitch, dim), BF16)],
-        n_smem=1,
-    )
-    x_own = jnp.concatenate(plane_trade(pick_plane(x_first)), axis=0)
-    w_own = [after(w, x_own) for w in w_own]
-    ff_w = lax.all_gather(after(ff_pack, *w_own), "inner", axis=0, tiled=True)
-    xs = rep_gather(x_own)
-    c_first = rep_trade(pick(after(cotangent, *x_first)))
-    c_own = jnp.concatenate(plane_trade(pick_plane([after(c, x_own) for c in c_first])), axis=0)
-
-    w_other = [part_swap(jnp.concatenate(w_own, axis=0), l) for l in range(1, part)]
-    wo_own = rep_gather(after(jnp.concatenate([w[:w_rows, 3 * width :] for w in w_own], axis=0), xs[-1]))
+        n_smem=1, n_any=1,
+    )
+    ff_w = lax.all_gather(ff_pack, "inner", axis=0, tiled=True)
+
+    own = w_all.reshape(n_rep, part, high, lanes)
+    own = lax.dynamic_slice_in_dim(own, t, 1, 1)[:, 0, :w_rows, 3 * width :].reshape(n_rep * w_rows, width)
+    wo_own = rep_gather(after(own, xs[-1]))
     wo_other = [part_swap(jnp.concatenate(wo_own, axis=0), l) for l in range(1, part)]
 
     order = jnp.arange(total, dtype=jnp.int32)
-    spot = ((s ^ (order // sub % n_rep)) * part + t) * rows + (j ^ (order // rows)) * sub + order % sub
+    spot = ((order // sub % n_rep) * part + t) * rows + (j ^ (order // rows)) * sub + order % sub
     inv_freq = 1.0 / THETA ** (jnp.arange(HEAD_DIM // 2, dtype=F32) * (2.0 / HEAD_DIM))
     angle = spot.astype(F32)[:, None] * inv_freq[None, :]
     cos_half, sin_half = jnp.cos(angle), jnp.sin(angle)
@@ -640,13 +595,13 @@
     sin = jnp.concatenate([-sin_half, sin_half] * 2, axis=1)
 
     q, kv, a_one, w_qkv, gains = call(
-        grouped(qkv_kernel, (n_rep, part), (None, n_rep, n_rep, part - 1) + (None,) * 7),
+        grouped(qkv_kernel, (n_rep, part), (n_rep,) + (None,) * 8),
         [
             ((total, width), BF16), ((total, 2 * width), BF16), ((total, dim), BF16),
             ((dim, 3 * width), BF16), ((2, dim), F32),
         ],
-        [at, *xs, *w_own, *w_other, cos, sin],
-        n_smem=1, micros=4,
+        [*xs, w_all, cos, sin, c_own],
+        n_any=1, micros=4,
     )
     kvs = [kv] + [part_swap(kv, l) for l in range(1, part)]
     heads = width // HEAD_DIM
@@ -683,7 +638,7 @@
         [((rows, dim), BF16)] * n_rep + [((n_inner * ff_high, 2 * ff), BF16)],
         [gated, w_down, c_all, a_two, d_hidden],
         [((ff, dim), BF16)],
-        micros=7,
+        micros=30,
     )
     lo, ff_grad = ff_back[:-1], ff_back[-1]
     dr, dz = call(
@@ -692,7 +647,7 @@
         [*das, r_own, c_own, gains, ff_grad],
         n_any=1, micros=2,
     )
-    ff_grad = lax.psum_scatter(ff_grad, "inner", scatter_dimension=0, tiled=True)
+    ff_grad = lax.psum_scatter(after(ff_grad, *das[1:]), "inner", scatter_dimension=0, tiled=True)
     dzs = rep_gather(dz)
 
     back = call(
@@ -713,45 +668,32 @@
         n_smem=1, micros=10,
     )
     dq, dkv, sends, dz_all = back[0], back[1], back[2:-1], back[-1]
-    gots = [part_swap(x, l + 1) for l, x in enumerate(sends)]
+    los = rep_trade([after(x, dzs[-1]) for x in lo])
+    gots = [part_swap(after(x, *los[1:]), l + 1) for l, x in enumerate(sends)]
     (d_out,) = call(
         out_grad_kernel, [((dim, width), BF16)], [at, o_all, dz_all], n_smem=1, micros=2,
     )
-    los = rep_trade([after(x, dzs[-1]) for x in lo])
+    qkv_out = call(
+        grouped(qkv_back_kernel, (n_rep, n_inner), (None, None, part - 1) + (None,) * 4 + (n_rep,) + (None,) * 3 + (n_rep, None)),
+        [((n_inner * high, lanes), BF16)] + [((rows, dim), BF16)] * n_rep,
+        [dq, dkv, *gots, cos, sin, a_one, w_qkv, *xs, d_out, gain_two_part],
+        [((total, 3 * width), BF16)],
+        micros=6,
+    )
+    das = rep_trade(qkv_out[1:])
+    ff_grad = after(ff_grad, *das[1:])
+    d_pack = lax.psum_scatter(after(qkv_out[0], ff_grad), "inner", scatter_dimension=0, tiled=True)
     parts = call(
-        grouped(layer_out_kernel, (n_rep,), (None, n_rep, None, n_rep, None)),
-        small, [at, *los, r_own, dq], [((rows, dim), F32)], n_smem=1, n_any=1,
-    )
-    layer_out = place(send_home(parts))
-
-    qkv_out = call(
-        grouped(
-            qkv_back_kernel, (n_rep, part),
-            (None, None, None, part - 1, None, None, None, None, n_rep, None, None, None, part - 1, n_rep, None, None),
-        ),
-        [((n_rep * high, lanes), F32)]
-        + [((n_rep * high, lanes), BF16)] * (part - 1)
-        + [((rows, dim), BF16)] * n_rep,
-        [at, dq, dkv, *gots, cos, sin, a_one, w_qkv, *xs, d_out, gain_two_part],
-        [((total, 3 * width), BF16), ((dim, lanes), F32)],
-        n_smem=1, micros=6,
-    )
-    keep, sends, da_one = qkv_out[0], qkv_out[1:part], qkv_out[part:]
-    gots = [part_swap(x, l + 1) for l, x in enumerate(sends)]
-    summed = call(
-        grouped(part_sum_kernel, (n_rep,), (None, part - 1, None, n_rep - 1)),
-        [((high, lanes), F32)] + [((high, lanes), BF16)] * (n_rep - 1),
-        [keep, *gots],
-    )
-    gots = [plane_swap(x, m + 1) for m, x in enumerate(summed[1:])]
-    das = rep_trade(da_one)
-    parts = call(
-        grouped(last_kernel, (n_rep,), (None, n_rep, None, None, None, n_rep, None)),
-        small, [at, *das, xs[0], dr, gains], [((rows, dim), F32)], n_smem=1, micros=2,
-    )
-    input_grad = place(send_home(parts))
-    (quarter,) = call(
-        grouped(plane_sum_kernel, (), (None, n_rep - 1, None)), [((high, lanes), BF16)], [summed[0], *gots]
+        grouped(last_kernel, (n_rep,), (None, n_rep, n_rep, None, None, None, None, n_rep, None)),
+        home, [at, *das, *los, xs[0], dr, r_own, gains], [((rows, dim), F32)], n_smem=1, micros=2,
+    )
+    ff_grads = jnp.concatenate([after(ff_grad, *das[1:])] * n_rep, axis=0)
+    ff_grads = lax.all_to_all(ff_grads, "rep", 0, 0, tiled=True).reshape(n_rep, ff_high, 2 * ff)
+    back_home = send_home(parts)
+    quarter = after(d_pack, *back_home)
+    input_grad, layer_out = call(
+        grouped(place_kernel, (n_rep,), (None, n_rep, None, None)),
+        [((rows, dim), BF16)] * 2, [at, *back_home, d_pack], n_smem=1, n_any=1,
     )
     g_qkv, g_out, g_gains = call(
         grouped(grads_kernel, (n_rep,), (None, n_rep, None, None, None)),
@@ -760,11 +702,11 @@
         n_smem=1, micros=2,
     )
     g_in, g_down = call(
-        grouped(ff_out_kernel, (n_rep, unit, pitch), (None, n_rep, None, None, None, None)),
+        grouped(ff_out_kernel, (n_rep, unit, pitch), (None,) * 4),
         [((w_rows, 2 * n_inner * ff_shard), F32), ((ff_shard, dim), F32)],
-        [at, *rep_gather(ff_grad)],
-        [((n_rep, ff_high, 2 * ff), BF16), ((pitch, dim), F32)],
-        n_smem=1, micros=4,
+        [ff_grads, d_pack],
+        [((pitch, dim), F32)],
+        n_any=1, micros=4,
     )
     gain_grads = g_gains[: 2 * dim // lanes].reshape(2, dim)
     gain_grads = lax.dynamic_slice_in_dim(gain_grads, i * w_rows, w_rows, 1)

time: 303 us -> 265 us (0.87)
  starting transfers between devices: 89.9 us -> 54.4 us
  blocking collectives: 0 us -> 19.7 us
  Pallas kernels: 96.3 us -> 81 us
  waiting for transfers between devices: 83.8 us -> 75.8 us
    ppermute x36 -> x27, waiting for transfers between devices: 62.8 us -> 39.1 us  [rep_swap(): return lax.ppermute(x, 'rep', [(a, a ^ m) for a in range(n_rep)])]
    ppermute x12 -> x0, starting transfers between devices: 21 us -> none  [plane_swap(): return lax.ppermute(x, 'inner', pairs)]
    ppermute x8 -> x4, waiting for transfers between devices: 0.02 us -> 20.5 us  [send_home(): got.append(lax.ppermute(pieces[k], ('rep', 'inner'), pairs))]
    all_to_all x0 -> x2, blocking collectives: none -> 19.7 us  [the longest x1 10.9 us: on_device(): x_first = lax.all_to_all(after(tokens, w_pack), 'rep', 0, 0, tiled=True)]
    ppermute x12 -> x0, waiting for transfers between devices: 18.6 us -> none  [plane_swap(): return lax.ppermute(x, 'inner', pairs)]
    ppermute x8 -> x4, starting transfers between devices: 25.2 us -> 9.74 us  [send_home(): got.append(lax.ppermute(pieces[k], ('rep', 'inner'), pairs))]
    pallas_call x22 -> x14, Pallas kernels: 96.3 us -> 81 us  [call(): pl.pallas_call(without_waited, out_shape=[jax.ShapeDtypeStruct(s, d) for...]
    all_to_all x0 -> x3, waiting for transfers between devices: none -> 14.2 us  [the longest x1 10.3 us: on_device(): lax.all_to_all(x_first, 'inner', 0, 0, axis_index_groups=planes, tiled=True)]
  transfers between devices with their start and end apart: 63 -> 41, of which waited for: 21 -> 16; matrix products, arithmetic and copies ran while one was open for 2% -> 2% of each run, Pallas kernels for 21% -> 23%
where the time goes in v3:
time: 265 us; the launch traced here: 262 us
  Pallas kernels  81 us (31%)
  waiting for transfers between devices  75.8 us (29%)
  starting transfers between devices  54.4 us (21%)
  blocking collectives  19.7 us (7%)
  between operations  14.1 us (5%)
  local copies, waits for them, and re-layouts  11.4 us (4%)
  other arithmetic  5.83 us (2%)
    pallas_call x14, Pallas kernels, call(): pl.pallas_call(without_waited, out_shape=[jax.ShapeDtypeStruct(s, d) for...  81 us
    ppermute x27, waiting for transfers between devices, rep_swap(): return lax.ppermute(x, 'rep', [(a, a ^ m) for a in range(n_rep)])  39.1 us
    ppermute x27, starting transfers between devices, rep_swap(): return lax.ppermute(x, 'rep', [(a, a ^ m) for a in range(n_rep)])  32.2 us
    ppermute x4, waiting for transfers between devices, send_home(): got.append(lax.ppermute(pieces[k], ('rep', 'inner'), pairs))  20.5 us
    all_to_all x1, blocking collectives, on_device(): x_first = lax.all_to_all(after(tokens, w_pack), 'rep', 0, 0, tiled=True)  10.9 us
    all_to_all x1, waiting for transfers between devices, on_device(): lax.all_to_all(x_first, 'inner', 0, 0, axis_index_groups=planes, tiled=True)  10.3 us
    ppermute x4, starting transfers between devices, send_home(): got.append(lax.ppermute(pieces[k], ('rep', 'inner'), pairs))  9.74 us
    unnamed x88, local copies, waits for them, and re-layouts  9.17 us
  transfers between devices with their start and end apart: 41, of which 16 were waited for; matrix products, arithmetic and copies ran while one was open for 2% of the time, Pallas kernels for 23%

profile of v3, /device:TPU:0, one launch (start us, length us, event | category | flops | bytes accessed | tf_op | source)
XLA Modules:
  0.0 262.3 jit_solution(18245657001284260063)
XLA Ops:
  11.2 10.9 %all_to_all.53 = bf16[4,32,1024]{2,1,0:T(8,128)(2,1)} all-to-all(bf16[4,32,1024]{2,1,0:T(8,128)(2,1)S(1)} %bitcast.27), channel_id=1, replica_groups=mesh['rep'=4,'inner'=8] {'rep'}, dimensions={0} | all-to-all | bytes 524288 | tf_op jit(solution)/shard_map/all_to_all | solution.py:568
  24.8 8.8 %all_to_all.54 = bf16[4,32,1024]{2,1,0:T(8,128)(2,1)} all-to-all(bf16[4,32,1024]{2,1,0:T(8,128)(2,1)S(1)} %bitcast.28), channel_id=1, replica_groups=mesh['rep'=4,'inner'=8] {'rep'}, dimensions={0} | all-to-all | bytes 524288 | tf_op jit(solution)/shard_map/all_to_all | solution.py:571
  33.6 4.9 %all-to-all-start.1 = ((bf16[4,32,1024]{2,1,0:T(8,128)(2,1)}), bf16[4,32,1024]{2,1,0:T(8,128)(2,1)S(1)}, u32[]{:S(2)}, u32[]{:S(2)}) async-start(bf16[4,32,1024]{2,1,0:T(8,128)(2,1)} %all_to_all.53), calls=%async_computation.1 | async-start | bytes 524288 | tf_op jit(solution)/shard_map/all_to_all | solution.py:570
  38.5 10.3 %all-to-all-done.1 = bf16[4,32,1024]{2,1,0:T(8,128)(2,1)S(1)} async-done(((bf16[4,32,1024]{2,1,0:T(8,128)(2,1)}), bf16[4,32,1024]{2,1,0:T(8,128)(2,1)S(1)}, u32[]{:S(2)}, u32[]{:S(2)}) %all-to-all-start.1) | async-done | bytes 262176 | tf_op jit(solution)/shard_map/all_to_all | solution.py:570
  52.3 3.4 %all-to-all-start.3 = ((bf16[4,32,1024]{2,1,0:T(8,128)(2,1)}), bf16[4,32,1024]{2,1,0:T(8,128)(2,1)S(1)}, u32[]{:S(2)}, u32[]{:S(2)}) async-start(bf16[4,32,1024]{2,1,0:T(8,128)(2,1)} %bitcast.10), calls=%async_computation.3 | async-start | bytes 524288 | tf_op jit(solution)/shard_map/all_to_all | solution.py:573
  64.6 3.9 %all-to-all-done.3 = bf16[4,32,1024]{2,1,0:T(8,128)(2,1)S(1)} async-done(((bf16[4,32,1024]{2,1,0:T(8,128)(2,1)}), bf16[4,32,1024]{2,1,0:T(8,128)(2,1)S(1)}, u32[]{:S(2)}, u32[]{:S(2)}) %all-to-all-start.3) | async-done | bytes 262176 | tf_op jit(solution)/shard_map/all_to_all | solution.py:573
  69.3 4.8 %shard_map.144 = (bf16[512,256]{1,0:T(8,128)(2,1)}, bf16[512,512]{1,0:T(8,128)(2,1)}, bf16[512,1024]{1,0:T(8,128)(2,1)}, bf16[1024,768]{1,0:T(8,128)(2,1)}, f32[2,1024]{1,0:T(2,128)}) custom-call(bf16[128,1024]{1,0:T(8,128)(2,1)} %bitcast.32, bf16[128,1024]{1,0:T(8,128)(2,1)} %copy-done.18, bf16[128,1024]{1,0:T(8,128)(2,1)} %copy-done.17, ...), custom_call_target="tpu_custom_call" | custom-call | flops 4000000000 | bytes 4000000 | tf_op jit(solution)/shard_map/pallas_call | solution.py:43
  79.1 8.3 %shard_map.145 = (bf16[512,256]{1,0:T(8,128)(2,1)}, f32[8,512]{1,0:T(8,128)}) custom-call(bf16[512,256]{1,0:T(8,128)(2,1)} %get-tuple-element.76.refs_0_.refs_7_, bf16[512,512]{1,0:T(8,128)(2,1)} %get-tuple-element.77.refs_1_.refs_8_, bf16[512,512]{1,0:T(8,128)(2,1)} %copy-done.11), custom_call_target="tpu_custom_call" | custom-call | flops 8000000000 | bytes 8000000 | tf_op jit(solution)/shard_map/pallas_call | solution.py:43
  91.6 6.2 %collective-permute-done.6.refs_8_ = bf16[512,256]{1,0:T(8,128)(2,1)S(1)} collective-permute-done((bf16[512,256]{1,0:T(8,128)(2,1)}, bf16[512,256]{1,0:T(8,128)(2,1)S(1)}, u32[]{:S(2)}, u32[]{:S(2)}) %collective-permute-start.6) | collective-permute-done | bytes 262176 | tf_op jit(solution)/shard_map/ppermute | solution.py:530
  97.8 4.1 %collective-permute-done.5.refs_7_ = bf16[512,256]{1,0:T(8,128)(2,1)S(1)} collective-permute-done((bf16[512,256]{1,0:T(8,128)(2,1)}, bf16[512,256]{1,0:T(8,128)(2,1)S(1)}, u32[]{:S(2)}, u32[]{:S(2)}) %collective-permute-start.5) | collective-permute-done | bytes 262176 | tf_op jit(solution)/shard_map/ppermute | solution.py:530
  103.8 16.7 %shard_map.147 = (f32[128,1024]{1,0:T(8,128)}, bf16[128,1024]{1,0:T(8,128)(2,1)}, bf16[128,1024]{1,0:T(8,128)(2,1)}, bf16[128,1024]{1,0:T(8,128)(2,1)}, bf16[128...) custom-call(s32[3]{0:T(128)} %pad_add_fusion.refs_0_, ...), custom_call_target="tpu_custom_call" | custom-call | flops 14000000000 | bytes 14000000 | tf_op jit(solution)/shard_map/pallas_call | solution.py:43
  124.1 8.5 %shard_map.148 = (bf16[128,1024]{1,0:T(8,128)(2,1)}, bf16[128,1024]{1,0:T(8,128)(2,1)}, bf16[128,1024]{1,0:T(8,128)(2,1)}, bf16[128,1024]{1,0:T(8,128)(2,1)}, bf16[1536,1536]{1,0:T(8,128)(2,1)}) custom-call(bf16[512,768]{1,0:T(8,128)(2,1)} %get-tuple-element.88.refs_0_, bf16[768,1024]{1,0:T(8,128)(2,1)} %get-tuple-element.89.refs_1_, ...), custom_call_target="tpu_custom_call" | custom-call | flops 30000001024 | bytes 30000000 | tf_op jit(solution)/shard_map/pallas_call | solution.py:43
  132.6 3.5 %collective-permute-done.15.refs_2_ = bf16[128,1024]{1,0:T(8,128)(2,1)S(1)} collective-permute-done((bf16[128,1024]{1,0:T(8,128)(2,1)}, bf16[128,1024]{1,0:T(8,128)(2,1)S(1)}, u32[]{:S(2)}, u32[]{:S(2)}) %collective-permute-start.15) | collective-permute-done | bytes 262176 | tf_op jit(solution)/shard_map/ppermute | solution.py:530
  143.3 6.9 %collective-permute-done.19.refs_4_ = bf16[128,1024]{1,0:T(8,128)(2,1)S(1)} collective-permute-done((bf16[128,1024]{1,0:T(8,128)(2,1)}, bf16[128,1024]{1,0:T(8,128)(2,1)S(1)}, u32[]{:S(2)}, u32[]{:S(2)}) %collective-permute-start.19) | collective-permute-done | bytes 262176 | tf_op jit(solution)/shard_map/ppermute | solution.py:530
  156.5 10.6 %shard_map.150 = (bf16[512,256]{1,0:T(8,128)(2,1)}, f32[512,512]{1,0:T(8,128)}, bf16[512,512]{1,0:T(8,128)(2,1)}, bf16[512,1024]{1,0:T(8,128)(2,1)}) custom-call(s32[3]{0:T(128)} %pad_add_fusion.refs_0_, bf16[128,1024]{1,0:T(8,128)(2,1)} %get-tuple-element.94.refs_1_, bf16[128,1024]{1,0:T(8,128)(2,1)} %copy-done.39, bf16[128,1024]{1,0:T(8,128)(2,1)} %copy-done.38, ...), custom_call_target="tpu_custom_call" | custom-call | flops 10000000000 | bytes 10000000 | tf_op jit(solution)/shard_map/pallas_call | solution.py:43
  171.2 7.6 %shard_map.152 = (bf16[1088,1024]{1,0:T(8,128)(2,1)}, bf16[128,1024]{1,0:T(8,128)(2,1)}, bf16[128,1024]{1,0:T(8,128)(2,1)}, bf16[128,1024]{1,0:T(8,128)(2,1)}, bf16[128,1024]{1,0:T(8,128)(2,1)}) custom-call(bf16[512,256]{1,0:T(8,128)(2,1)} %get-tuple-element.97.refs_0_, f32[512,512]{1,0:T(8,128)} %get-tuple-element.98.refs_1_, bf16[512,512]{1,0:T(8,128)(2,1)} %copy-done.12, ...), custom_call_target="tpu_custom_call" | custom-call | flops 6000000000 | bytes 6000000 | tf_op jit(solution)/shard_map/pallas_call | solution.py:43
  182.3 5.8 %collective-permute-done.24.refs_2_ = bf16[128,1024]{1,0:T(8,128)(2,1)S(1)} collective-permute-done((bf16[128,1024]{1,0:T(8,128)(2,1)}, bf16[128,1024]{1,0:T(8,128)(2,1)S(1)}, u32[]{:S(2)}, u32[]{:S(2)}) %collective-permute-start.24) | collective-permute-done | bytes 262176 | tf_op jit(solution)/shard_map/ppermute | solution.py:530
  188.1 5.3 %collective-permute-done.25.refs_3_ = bf16[128,1024]{1,0:T(8,128)(2,1)S(1)} collective-permute-done((bf16[128,1024]{1,0:T(8,128)(2,1)}, bf16[128,1024]{1,0:T(8,128)(2,1)S(1)}, u32[]{:S(2)}, u32[]{:S(2)}) %collective-permute-start.25) | collective-permute-done | bytes 262176 | tf_op jit(solution)/shard_map/ppermute | solution.py:530
  196.3 3.7 %all-to-all-start.4 = ((bf16[4,192,1536]{2,1,0:T(8,128)(2,1)}), bf16[4,192,1536]{2,1,0:T(8,128)(2,1)S(1)}, u32[]{:S(2)}, u32[]{:S(2)}) async-start(bf16[4,192,1536]{2,1,0:T(8,128)(2,1)} %bitcast.14), calls=%async_computation.6 | async-start | bytes 4718592 | tf_op jit(solution)/shard_map/all_to_all | solution.py:691
  200.0 3.5 %shard_map.153 = (bf16[64,1024]{1,0:T(8,128)(2,1)}, bf16[64,1024]{1,0:T(8,128)(2,1)}, bf16[64,1024]{1,0:T(8,128)(2,1)}, bf16[64,1024]{1,0:T(8,128)(2,1)}) custom-call(s32[3]{0:T(128)} %pad_add_fusion.refs_0_, bf16[128,1024]{1,0:T(8,128)(2,1)} %get-tuple-element.112.refs_1_, bf16[128,1024]{1,0:T(8,128)(2,1)} %copy-done.29, bf16[128,1024]{1,0:T(8,128)(2,1)} %copy-done.30, ...), custom_call_target="tpu_custom_call" | custom-call | flops 2000000000 | bytes 2000000 | tf_op jit(solution)/shard_map/pallas_call | solution.py:43
  205.1 3.8 %collective-permute-start.28 = (bf16[64,1024]{1,0:T(8,128)(2,1)}, bf16[64,1024]{1,0:T(8,128)(2,1)S(1)}, u32[]{:S(2)}, u32[]{:S(2)}) collective-permute-start(bf16[64,1024]{1,0:T(8,128)(2,1)} %get-tuple-element.120), channel_id=1, source_target_pairs={{0,2},{1,3},{2,10},{3,11},{4,18},{5,19},{6,26},{7,27},{8,0},{9,1},... | collective-permute-start | bytes 393224 | tf_op jit(solution)/shard_map/ppermute | solution.py:557
  210.1 3.1 %collective-permute-start.30 = (bf16[64,1024]{1,0:T(8,128)(2,1)}, bf16[64,1024]{1,0:T(8,128)(2,1)S(1)}, u32[]{:S(2)}, u32[]{:S(2)}) collective-permute-start(bf16[64,1024]{1,0:T(8,128)(2,1)} %get-tuple-element.122), channel_id=1, source_target_pairs={{0,6},{1,7},{2,14},{3,15},{4,22},{5,23},{6,30},{7,31},{8,4},{9,5},... | collective-permute-start | bytes 393224 | tf_op jit(solution)/shard_map/ppermute | solution.py:557
  213.3 20.5 %collective-permute-done.28.refs_2_ = bf16[64,1024]{1,0:T(8,128)(2,1)S(1)} collective-permute-done((bf16[64,1024]{1,0:T(8,128)(2,1)}, bf16[64,1024]{1,0:T(8,128)(2,1)S(1)}, u32[]{:S(2)}, u32[]{:S(2)}) %collective-permute-start.28) | collective-permute-done | bytes 131104 | tf_op jit(solution)/shard_map/ppermute | solution.py:557
  241.9 5.7 %shard_map.156 = (f32[128,5248]{1,0:T(8,128)}, f32[328,1024]{1,0:T(8,128)}) custom-call(bf16[4,192,1536]{2,1,0:T(8,128)(2,1)} %copy-done, bf16[136,1024]{1,0:T(8,128)(2,1)} %reduce-scatter.5.cloned.1.call-done.refs_5_.refs_1_), custom_call_target="tpu_custom_call" | custom-call | flops 4000000000 | bytes 4000000 | tf_op jit(solution)/shard_map/pallas_call | solution.py:43
  (178 shorter events, 77.2 us)
Async XLA Ops:
  7.2 50.9 %all-gather.3.cloned.1.call-start = ((), (), s32[]{:S(2)}) async-start(), calls=%async_computation.7 | async-start | bytes 2506752 | tf_op jit(solution)/shard_map/all_gather | solution.py:567
  11.1 92.7 %all-gather.5.cloned.1.call-start = ((), (), s32[]{:S(2)}) async-start(), calls=%async_computation.8 | async-start | bytes 5308416 | tf_op jit(solution)/shard_map/all_gather | solution.py:582
  33.6 15.2 %all-to-all-start.1 = ((bf16[4,32,1024]{2,1,0:T(8,128)(2,1)}), bf16[4,32,1024]{2,1,0:T(8,128)(2,1)S(1)}, u32[]{:S(2)}, u32[]{:S(2)}) async-start(bf16[4,32,1024]{2,1,0:T(8,128)(2,1)} %all_to_all.53), calls=%async_computation.1 | async-start | bytes 524288 | tf_op jit(solution)/shard_map/all_to_all | solution.py:570
  51.2 13.5 %collective-permute-start.1 = (bf16[128,1024]{1,0:T(8,128)(2,1)S(1)}, bf16[128,1024]{1,0:T(8,128)(2,1)S(1)}, u32[]{:S(2)}, u32[]{:S(2)}) collective-permute-start(bf16[128,1024]{1,0:T(8,128)(2,1)S(1)} %bitcast.30), channel_id=1, source_target_pairs={{0,16},{8,24},{16,0},{24,8},{1,17},{9,25},{17,1},{25,9},{2,18},{10... | collective-permute-start | bytes 786440 | tf_op jit(solution)/shard_map/ppermute | solution.py:530
  52.3 16.3 %all-to-all-start.3 = ((bf16[4,32,1024]{2,1,0:T(8,128)(2,1)}), bf16[4,32,1024]{2,1,0:T(8,128)(2,1)S(1)}, u32[]{:S(2)}, u32[]{:S(2)}) async-start(bf16[4,32,1024]{2,1,0:T(8,128)(2,1)} %bitcast.10), calls=%async_computation.3 | async-start | bytes 524288 | tf_op jit(solution)/shard_map/all_to_all | solution.py:573
  55.7 137.8 %reduce-scatter.3.cloned.1.call-start = ((), (), s32[]{:S(2)}) async-start(), calls=%async_computation.9 | async-start | bytes 5308416 | tf_op jit(solution)/shard_map/reduce_scatter | solution.py:650
  59.1 15.1 %collective-permute-start.9 = (bf16[512,256]{1,0:T(8,128)(2,1)S(1)}, bf16[512,256]{1,0:T(8,128)(2,1)S(1)}, u32[]{:S(2)}, u32[]{:S(2)}) collective-permute-start(bf16[512,256]{1,0:T(8,128)(2,1)S(1)} %bitcast.22), channel_id=1, source_target_pairs={{0,24},{8,16},{16,8},{24,0},{1,25},{9,17},{17,9},{25,1},{2,26},{10... | collective-permute-start | bytes 786440 | tf_op jit(solution)/shard_map/ppermute | solution.py:530
  74.6 27.3 %collective-permute-start.10 = (bf16[2048,256]{1,0:T(8,128)(2,1)S(1)}, bf16[2048,256]{1,0:T(8,128)(2,1)S(1)}, u32[]{:S(2)}, u32[]{:S(2)}) collective-permute-start(bf16[2048,256]{1,0:T(8,128)(2,1)S(1)} %pad_maximum_fusion.1), channel_id=1, source_target_pairs={{0,1},{1,0},{2,3},{3,2},{4,5},{5,4},{6,7},{7,6},{8,9},{9,8},{10,11... | collective-permute-start | bytes 3145736 | tf_op jit(solution)/shard_map/ppermute | solution.py:538
  74.8 15.0 %collective-permute-start.13 = (bf16[128,1024]{1,0:T(8,128)(2,1)}, bf16[128,1024]{1,0:T(8,128)(2,1)S(1)}, u32[]{:S(2)}, u32[]{:S(2)}) collective-permute-start(bf16[128,1024]{1,0:T(8,128)(2,1)} %bitcast.37), channel_id=1, source_target_pairs={{0,24},{8,16},{16,8},{24,0},{1,25},{9,17},{17,9},{25,1},{2,26},{10... | collective-permute-start | bytes 786440 | tf_op jit(solution)/shard_map/ppermute | solution.py:530
  77.2 13.2 %collective-permute-start.12 = (bf16[128,1024]{1,0:T(8,128)(2,1)}, bf16[128,1024]{1,0:T(8,128)(2,1)S(1)}, u32[]{:S(2)}, u32[]{:S(2)}) collective-permute-start(bf16[128,1024]{1,0:T(8,128)(2,1)} %bitcast.38), channel_id=1, source_target_pairs={{0,16},{8,24},{16,0},{24,8},{1,17},{9,25},{17,1},{25,9},{2,18},{10... | collective-permute-start | bytes 786440 | tf_op jit(solution)/shard_map/ppermute | solution.py:530
  77.8 13.8 %collective-permute-start.11 = (bf16[128,1024]{1,0:T(8,128)(2,1)}, bf16[128,1024]{1,0:T(8,128)(2,1)S(1)}, u32[]{:S(2)}, u32[]{:S(2)}) collective-permute-start(bf16[128,1024]{1,0:T(8,128)(2,1)} %bitcast.39), channel_id=1, source_target_pairs={{0,8},{8,0},{16,24},{24,16},{1,9},{9,1},{17,25},{25,17},{2,10},{10... | collective-permute-start | bytes 786440 | tf_op jit(solution)/shard_map/ppermute | solution.py:530
  122.1 14.0 %collective-permute-start.15 = (bf16[128,1024]{1,0:T(8,128)(2,1)}, bf16[128,1024]{1,0:T(8,128)(2,1)S(1)}, u32[]{:S(2)}, u32[]{:S(2)}) collective-permute-start(bf16[128,1024]{1,0:T(8,128)(2,1)} %get-tuple-element.85), channel_id=1, source_target_pairs={{0,16},{8,24},{16,0},{24,8},{1,17},{9,25},{17,1},{25,9},{2,18},{10... | collective-permute-start | bytes 786440 | tf_op jit(solution)/shard_map/ppermute | solution.py:530
  136.9 98.2 %reduce-scatter.5.cloned.1.call-start = ((), (), s32[]{:S(2)}) async-start(), calls=%async_computation.10 | async-start | bytes 2506752 | tf_op jit(solution)/shard_map/reduce_scatter | solution.py:685
  142.4 13.4 %collective-permute-start.17 = (bf16[128,1024]{1,0:T(8,128)(2,1)}, bf16[128,1024]{1,0:T(8,128)(2,1)S(1)}, u32[]{:S(2)}, u32[]{:S(2)}) collective-permute-start(bf16[128,1024]{1,0:T(8,128)(2,1)} %get-tuple-element.94.refs_1_), channel_id=1, source_target_pairs={{0,8},{8,0},{16,24},{24,16},{1,9},{9,1},{17,25},{25,17},{2,10},{10... | collective-permute-start | bytes 786440 | tf_op jit(solution)/shard_map/ppermute | solution.py:530
  150.2 16.9 %collective-permute-start.20 = (bf16[128,1024]{1,0:T(8,128)(2,1)S(1)}, bf16[128,1024]{1,0:T(8,128)(2,1)S(1)}, u32[]{:S(2)}, u32[]{:S(2)}) collective-permute-start(bf16[128,1024]{1,0:T(8,128)(2,1)S(1)} %copy-done.24), channel_id=1, source_target_pairs={{0,8},{8,0},{16,24},{24,16},{1,9},{9,1},{17,25},{25,17},{2,10},{10... | collective-permute-start | bytes 786440 | tf_op jit(solution)/shard_map/ppermute | solution.py:530
  151.3 15.8 %collective-permute-start.21 = (bf16[128,1024]{1,0:T(8,128)(2,1)S(1)}, bf16[128,1024]{1,0:T(8,128)(2,1)S(1)}, u32[]{:S(2)}, u32[]{:S(2)}) collective-permute-start(bf16[128,1024]{1,0:T(8,128)(2,1)S(1)} %copy-done.23), channel_id=1, source_target_pairs={{0,16},{8,24},{16,0},{24,8},{1,17},{9,25},{17,1},{25,9},{2,18},{10... | collective-permute-start | bytes 786440 | tf_op jit(solution)/shard_map/ppermute | solution.py:530
  152.2 14.9 %collective-permute-start.22 = (bf16[128,1024]{1,0:T(8,128)(2,1)S(1)}, bf16[128,1024]{1,0:T(8,128)(2,1)S(1)}, u32[]{:S(2)}, u32[]{:S(2)}) collective-permute-start(bf16[128,1024]{1,0:T(8,128)(2,1)S(1)} %copy-done.22), channel_id=1, source_target_pairs={{0,24},{8,16},{16,8},{24,0},{1,25},{9,17},{17,9},{25,1},{2,26},{10... | collective-permute-start | bytes 786440 | tf_op jit(solution)/shard_map/ppermute | solution.py:530
  179.4 14.1 %collective-permute-start.25 = (bf16[128,1024]{1,0:T(8,128)(2,1)}, bf16[128,1024]{1,0:T(8,128)(2,1)S(1)}, u32[]{:S(2)}, u32[]{:S(2)}) collective-permute-start(bf16[128,1024]{1,0:T(8,128)(2,1)} %get-tuple-element.114), channel_id=1, source_target_pairs={{0,16},{8,24},{16,0},{24,8},{1,17},{9,25},{17,1},{25,9},{2,18},{10... | collective-permute-start | bytes 786440 | tf_op jit(solution)/shard_map/ppermute | solution.py:530
  196.3 44.2 %all-to-all-start.4 = ((bf16[4,192,1536]{2,1,0:T(8,128)(2,1)}), bf16[4,192,1536]{2,1,0:T(8,128)(2,1)S(1)}, u32[]{:S(2)}, u32[]{:S(2)}) async-start(bf16[4,192,1536]{2,1,0:T(8,128)(2,1)} %bitcast.14), calls=%async_computation.6 | async-start | bytes 4718592 | tf_op jit(solution)/shard_map/all_to_all | solution.py:691
  205.1 28.7 %collective-permute-start.28 = (bf16[64,1024]{1,0:T(8,128)(2,1)}, bf16[64,1024]{1,0:T(8,128)(2,1)S(1)}, u32[]{:S(2)}, u32[]{:S(2)}) collective-permute-start(bf16[64,1024]{1,0:T(8,128)(2,1)} %get-tuple-element.120), channel_id=1, source_target_pairs={{0,2},{1,3},{2,10},{3,11},{4,18},{5,19},{6,26},{7,27},{8,0},{9,1},... | collective-permute-start | bytes 393224 | tf_op jit(solution)/shard_map/ppermute | solution.py:557
  208.9 24.8 %collective-permute-start.29 = (bf16[64,1024]{1,0:T(8,128)(2,1)}, bf16[64,1024]{1,0:T(8,128)(2,1)S(1)}, u32[]{:S(2)}, u32[]{:S(2)}) collective-permute-start(bf16[64,1024]{1,0:T(8,128)(2,1)} %get-tuple-element.121), channel_id=1, source_target_pairs={{0,4},{1,5},{2,12},{3,13},{4,20},{5,21},{6,28},{7,29},{8,6},{9,7},... | collective-permute-start | bytes 393224 | tf_op jit(solution)/shard_map/ppermute | solution.py:557
  210.1 23.7 %collective-permute-start.30 = (bf16[64,1024]{1,0:T(8,128)(2,1)}, bf16[64,1024]{1,0:T(8,128)(2,1)S(1)}, u32[]{:S(2)}, u32[]{:S(2)}) collective-permute-start(bf16[64,1024]{1,0:T(8,128)(2,1)} %get-tuple-element.122), channel_id=1, source_target_pairs={{0,6},{1,7},{2,14},{3,15},{4,22},{5,23},{6,30},{7,31},{8,4},{9,5},... | collective-permute-start | bytes 393224 | tf_op jit(solution)/shard_map/ppermute | solution.py:557
  236.3 14.1 %collective-permute-start.32 = (bf16[136,1024]{1,0:T(8,128)(2,1)}, bf16[136,1024]{1,0:T(8,128)(2,1)S(1)}, u32[]{:S(2)}, u32[]{:S(2)}) collective-permute-start(bf16[136,1024]{1,0:T(8,128)(2,1)} %reduce-scatter.5.cloned.1.call-done.refs_5_.refs_1_), channel_id=1, source_target_pairs={{0,16},{8,24},{16,0},{24,8},{1,17},{9,25},{17,1},{25,9},{2,18},{10... | collective-permute-start | bytes 835592 | tf_op jit(solution)/shard_map/ppermute | solution.py:530
  237.1 13.3 %collective-permute-start.31 = (bf16[136,1024]{1,0:T(8,128)(2,1)}, bf16[136,1024]{1,0:T(8,128)(2,1)S(1)}, u32[]{:S(2)}, u32[]{:S(2)}) collective-permute-start(bf16[136,1024]{1,0:T(8,128)(2,1)} %reduce-scatter.5.cloned.1.call-done.refs_5_.refs_1_), channel_id=1, source_target_pairs={{0,8},{8,0},{16,24},{24,16},{1,9},{9,1},{17,25},{25,17},{2,10},{10... | collective-permute-start | bytes 835592 | tf_op jit(solution)/shard_map/ppermute | solution.py:530
  (61 other events, 463.0 us)
Sparse Core Ops, SparseCore 0:
  11.2 36.0 all-gather.2
  49.5 54.2 all-gather.4
  136.2 54.2 reduce-scatter.2
  193.6 41.0 reduce-scatter.4

commit v4 on v3

--- a/solution.py
+++ b/solution.py
@@ -1,4 +1,5 @@
 import functools
+import math
 
 import jax
 import jax.numpy as jnp
@@ -14,7 +15,8 @@
 BF16 = jnp.bfloat16
 NT = (((1,), (1,)), ((), ()))
 TN = (((0,), (0,)), ((), ()))
-VMEM_LIMIT = 56 * 1024 * 1024
+VMEM_SPARE = 8 * 1024 * 1024
+VMEM_WHOLE = 60 * 1024 * 1024
 
 
 def dot(a, b):
@@ -29,30 +31,47 @@
     return lax.dot_general(a, b, TN, preferred_element_type=F32)
 
 
-def call(body, outs, args, scratch=(), n_smem=0, n_any=0, micros=1):
-    n_vmem = len(args) - n_smem - n_any
-    in_specs = (
-        [pl.BlockSpec(memory_space=pltpu.SMEM)] * n_smem
-        + [pl.BlockSpec(memory_space=pltpu.VMEM)] * n_vmem
-        + [pl.BlockSpec(memory_space=pl.ANY)] * n_any
-    )
+def call(body, outs, args, scratch=(), n_smem=0, n_any=0, far=(), far_outs=(), n_sems=0, whole=False, micros=1):
+    n_passed = len(args) - n_any
+    spaces = [pltpu.SMEM] * n_smem + [pltpu.VMEM] * (n_passed - n_smem) + [pltpu.HBM] * n_any
+    for k in far:
+        spaces[k] = pltpu.HBM
+    held = sum(math.prod(s) * jnp.dtype(d).itemsize for s, d in scratch)
 
     def without_waited(*refs):
-        body(*refs[: n_smem + n_vmem], *refs[len(args) :])
+        body(*refs[:n_passed], *refs[len(args) :])
 
     return pl.pallas_call(
         without_waited,
         out_shape=[jax.ShapeDtypeStruct(s, d) for s, d in outs],
-        in_specs=in_specs,
-        out_specs=[pl.BlockSpec(memory_space=pltpu.VMEM)] * len(outs),
-        scratch_shapes=[pltpu.VMEM(s, d) for s, d in scratch],
-        compiler_params=pltpu.CompilerParams(vmem_limit_bytes=VMEM_LIMIT),
+        in_specs=[pl.BlockSpec(memory_space=space) for space in spaces],
+        out_specs=[pl.BlockSpec(memory_space=pltpu.HBM if k in far_outs else pltpu.VMEM) for k in range(len(outs))],
+        scratch_shapes=[pltpu.VMEM(s, d) for s, d in scratch]
+        + ([pltpu.SemaphoreType.DMA((n_sems,))] if n_sems else []),
+        compiler_params=pltpu.CompilerParams(vmem_limit_bytes=VMEM_WHOLE if whole else held + VMEM_SPARE),
         cost_estimate=pl.CostEstimate(
             flops=int(micros * 1e9), transcendentals=0, bytes_accessed=int(micros * 1e6)
         ),
     )(*args)
 
 
+class Copies:
+    def __init__(self, sems):
+        self.sems = sems
+        self.used = 0
+
+    def start(self, source, target):
+        copy = pltpu.make_async_copy(source, target, self.sems.at[self.used])
+        self.used += 1
+        copy.start()
+        return copy
+
+
+def wait_all(copies):
+    for copy in copies:
+        copy.wait()
+
+
 def after(value, *others):
     return lax.optimization_barrier((value, *others))[0]
 
@@ -61,6 +80,10 @@
     centred = values - jnp.mean(values, axis=-1, keepdims=True)
     inv = lax.rsqrt(jnp.mean(centred * centred, axis=-1, keepdims=True) + EPSILON)
     return centred * inv, inv
+
+
+def spot(block, size):
+    return pl.ds(pl.multiple_of(block * size, size), size)
 
 
 def partner(x):
@@ -148,21 +171,22 @@
 
 
 def qkv_kernel(
-    n_rep, n_part, refs_x, pack_ref, cos_ref, sin_ref,
-    q_ref, kv_ref, a_ref, w_ref, gains_ref,
+    n_rep, at_ref, refs_x, pack_ref, cos_ref, sin_ref, q_ref, kv_ref, a_out, w_out, gains_ref,
+    a_ref, w_ref, rows_scr, sems,
 ):
     rows = refs_x[0].shape[0]
     width = q_ref.shape[1]
     dim = a_ref.shape[1]
     lanes = 4 * width
-    n_inner = n_rep * n_part
-    high = pack_ref.shape[0] // n_inner
+    n_inner, high, _ = pack_ref.shape
     w_rows = high - 8
-    gains = jnp.zeros((8, lanes), F32)
-    for p in range(n_inner):
-        base = p * high
-        w_ref[p * w_rows : (p + 1) * w_rows, :] = pack_ref[base : base + w_rows, : 3 * width]
-        gains = gains + pack_ref[base + w_rows : base + high, :].astype(F32)
+    copies = Copies(sems)
+    gains_in = copies.start(pack_ref.at[:, w_rows:, :], rows_scr)
+    weights_in = copies.start(pack_ref.at[:, :w_rows, : 3 * width], w_ref)
+    gains_in.wait()
+    gains = rows_scr[0].astype(F32)
+    for p in range(1, n_inner):
+        gains = gains + rows_scr[p].astype(F32)
     per = dim // lanes
     for g in range(2):
         gains_ref[g : g + 1, :] = jnp.concatenate(
@@ -170,11 +194,14 @@
         )
     for m in range(n_rep):
         hat, _ = hat_of(refs_x[m][...].astype(F32))
-        a_ref[m * rows : (m + 1) * rows, :] = (hat * gains_ref[0:1, :]).astype(BF16)
+        a_ref[spot(at_ref[0] ^ m, rows), :] = (hat * gains_ref[0:1, :]).astype(BF16)
+    weights_in.wait()
+    done = [copies.start(a_ref, a_out), copies.start(w_ref, w_out)]
+    weights = w_ref[...].reshape(dim, 3 * width)
     step = 2 * rows if n_rep % 2 == 0 else rows
     for r0 in range(0, n_rep * rows, step):
         sl = slice(r0, r0 + step)
-        proj = dot(a_ref[sl, :], w_ref[...])
+        proj = dot(a_ref[sl, :], weights)
         cos = tile_lanes(cos_ref[sl, :], width)
         sin = tile_lanes(sin_ref[sl, :], width)
         query = proj[:, :width]
@@ -183,6 +210,7 @@
         q_ref[sl, :] = (query * HEAD_DIM**-0.5).astype(BF16)
         kv_ref[sl, :width] = (key * cos + partner(key) * sin).astype(BF16)
         kv_ref[sl, width:] = proj[:, 2 * width :].astype(BF16)
+    wait_all(done)
 
 
 def attend_kernel(n_part, q_ref, refs_kv, o_ref, lse_ref, k_scr, vt_scr):
@@ -217,46 +245,36 @@
 
 
 def ff_kernel(
-    n_rep, n_part, pitch, at_ref, refs_x, refs_o, refs_wo, refs_wo_other, ffw_ref, refs_c, gains_ref,
-    r_ref, refs_da, a_ref, m_ref, du_ref, c_ref, o_ref, wout_ref, wdown_ref, gain_ref,
-    hat_scr, u_scr, dm_scr, win_scr,
+    n_rep, n_part, at_ref, refs_x, refs_o, refs_wo, refs_wo_other, ffw_ref, refs_c, gains_ref,
+    r_ref, refs_da, a_ref, m_ref, du_ref, o_out, wout_out, gain_ref,
+    hat_scr, u_scr, dm_scr, win_scr, wdown_scr, x_scr, c_scr, o_scr, wout_scr, sems,
 ):
     rows, dim = refs_x[0].shape
     total = n_rep * rows
     quarter = refs_o[0].shape[1]
-    j = at_ref[0]
-    n_inner = n_rep * n_part
-    w_rows = dim // n_inner
-    lanes = win_scr.shape[1]
-    extra, spots = packed_rows(pitch, dim, lanes)
-    for k in range(n_rep):
-        col = pl.multiple_of((j ^ k) * quarter, quarter)
-        for l in range(n_part):
-            for m in range(n_rep):
-                row = pl.multiple_of((m * n_part + (at_ref[2] ^ l)) * w_rows, w_rows)
-                if l == 0:
-                    piece = refs_wo[k][m * w_rows : (m + 1) * w_rows, :]
-                else:
-                    at = (k * n_rep + m) * w_rows
-                    piece = refs_wo_other[l - 1][at : at + w_rows, :]
-                wout_ref[pl.ds(row, w_rows), pl.ds(col, quarter)] = piece
+    j, t = at_ref[0], at_ref[2]
+    _, w_rows, lanes = win_scr.shape
+    copies = Copies(sems)
+    first = []
     for m in range(n_rep):
-        hat_scr[m * rows : (m + 1) * rows, :] = refs_x[m][...].astype(F32)
-        c_ref[m * rows : (m + 1) * rows, :] = refs_c[m][...]
-        col = pl.multiple_of((j ^ m) * quarter, quarter)
-        for k in range(n_rep):
-            at = (k ^ m) * rows
-            o_ref[k * rows : (k + 1) * rows, pl.ds(col, quarter)] = refs_o[m][at : at + rows, :]
-    for p in range(n_inner):
-        base = p * (w_rows + extra)
-        win_scr[p * w_rows : (p + 1) * w_rows, :] = ffw_ref[base : base + w_rows, :]
-        for row, lane, row_in, col_in, n, w in spots:
-            top = base + w_rows + row
-            wdown_ref[p * pitch + row_in : p * pitch + row_in + n, col_in : col_in + w] = ffw_ref[
-                top : top + n, lane : lane + w
-            ]
-    hat_scr[...] += dot(o_ref[...], wout_ref[...])
-    r_ref[...] = hat_scr[:rows, :]
+        cols = spot(j ^ m, quarter)
+        first.append(copies.start(refs_wo[m], wout_scr.at[:, t, :, cols]))
+        for l in range(1, n_part):
+            first.append(copies.start(refs_wo_other[l - 1].at[m], wout_scr.at[:, t ^ l, :, cols]))
+        first.append(copies.start(refs_o[m], o_scr.at[:, cols]))
+        first.append(copies.start(refs_x[m], x_scr.at[spot(j ^ m, rows), :]))
+    second = copies.start(ffw_ref.at[:, :w_rows, :], win_scr)
+    third = [copies.start(refs_c[m], c_scr.at[spot(j ^ m, rows), :]) for m in range(n_rep)]
+    third += copy_down(copies, w_rows, ffw_ref, wdown_scr)
+    wait_all(first)
+    weights = wout_scr[...].reshape(dim, dim)
+    last = [copies.start(o_scr, o_out)]
+    hat_scr[...] = x_scr[...].astype(F32) + dot(o_scr[...], weights)
+    r_ref[...] = hat_scr[spot(j, rows), :]
+    per = quarter // w_rows // n_part
+    for k in range(per):
+        block = wout_scr.at[pl.ds(j * per + k, 1)]
+        last.append(copies.start(block, wout_out.at[pl.ds(k, 1)]))
     gain = gains_ref[1:2, :]
 
     def norm_step(c, carry):
@@ -267,8 +285,11 @@
         return carry
 
     lax.fori_loop(0, total // 64, norm_step, 0)
-    u_scr[...] = dot(a_ref[...], win_scr[...])
-    dm_scr[...] = dot_nt(c_ref[...], wdown_ref[...])
+    second.wait()
+    weights = win_scr[...].reshape(dim, lanes)
+    u_scr[...] = dot(a_ref[...], weights)
+    wait_all(third)
+    dm_scr[...] = dot_nt(c_scr[...], wdown_scr[...].reshape(m_ref.shape[1], dim))
     width = m_ref.shape[1]
 
     def gate_step(c, carry):
@@ -285,32 +306,51 @@
         return carry
 
     lax.fori_loop(0, total // 32, gate_step, 0)
+    u_scr[:, :dim] = dot_nt(du_ref[...], win_scr[...].reshape(dim, lanes))
     total_gain = jnp.zeros((1, dim), F32)
     for m in range(n_rep):
-        sl = slice(m * rows, (m + 1) * rows)
-        da = dot_nt(du_ref[sl, :], win_scr[...])
+        sl = spot(j ^ m, rows)
+        da = u_scr[sl, :dim]
         refs_da[m][...] = da.astype(BF16)
         total_gain = total_gain + jnp.sum(da * hat_scr[sl, :], axis=0, keepdims=True)
     gain_ref[...] = total_gain
-
-
-def ff_grads_kernel(n_rep, n_inner, pitch, m_ref, wdown_ref, c_ref, a_ref, du_ref, refs_lo, grad_ref, down_scr):
+    wait_all(last)
+
+
+def copy_down(copies, w_rows, ffw_ref, wdown_scr):
+    _, pitch, dim = wdown_scr.shape
+    _, spots = packed_rows(pitch, dim, ffw_ref.shape[2])
+    started = []
+    for row, lane, row_in, col_in, n, w in spots:
+        source = ffw_ref.at[:, w_rows + row : w_rows + row + n, lane : lane + w]
+        started.append(copies.start(source, wdown_scr.at[:, row_in : row_in + n, col_in : col_in + w]))
+    return started
+
+
+def ff_grads_kernel(
+    n_rep, at_ref, m_ref, ffw_ref, refs_c, a_ref, du_ref, refs_lo, grad_out,
+    down_scr, wdown_scr, c_scr, din_scr, sems,
+):
     rows, dim = refs_lo[0].shape
-    w_rows = dim // n_inner
-    lanes = du_ref.shape[1]
-    extra, spots = packed_rows(pitch, dim, lanes)
-    high = w_rows + extra
-    down_scr[...] = dot_tn(m_ref[...], c_ref[...]).astype(BF16)
-    din = dot_tn(a_ref[...], du_ref[...]).astype(BF16)
-    for p in range(n_inner):
-        grad_ref[p * high : p * high + w_rows, :] = din[p * w_rows : (p + 1) * w_rows, :]
-        for row, lane, row_in, col_in, n, w in spots:
-            top = p * high + w_rows + row
-            grad_ref[top : top + n, lane : lane + w] = down_scr[
-                p * pitch + row_in : p * pitch + row_in + n, col_in : col_in + w
-            ]
+    n_inner, w_rows, lanes = din_scr.shape
+    pitch = down_scr.shape[1]
+    j = at_ref[0]
+    copies = Copies(sems)
+    early = [copies.start(refs_c[m], c_scr.at[spot(j ^ m, rows), :]) for m in range(n_rep)]
+    late = copy_down(copies, w_rows, ffw_ref, wdown_scr)
+    din_scr[...] = dot_tn(a_ref[...], du_ref[...]).astype(BF16).reshape(n_inner, w_rows, lanes)
+    sent = [copies.start(din_scr, grad_out.at[:, :w_rows, :])]
+    wait_all(early)
+    down_scr[...] = dot_tn(m_ref[...], c_scr[...]).astype(BF16).reshape(n_inner, pitch, dim)
+    for row, lane, row_in, col_in, n, w in packed_rows(pitch, dim, lanes)[1]:
+        source = down_scr.at[:, row_in : row_in + n, col_in : col_in + w]
+        sent.append(copies.start(source, grad_out.at[:, w_rows + row : w_rows + row + n, lane : lane + w]))
+    wait_all(late)
+    down_scr_all = wdown_scr[...].reshape(n_inner * pitch, dim)
+    c_scr[...] = dot(m_ref[...], down_scr_all).astype(BF16)
     for m in range(n_rep):
-        refs_lo[m][...] = dot(m_ref[m * rows : (m + 1) * rows, :], wdown_ref[...]).astype(BF16)
+        refs_lo[m][...] = c_scr[spot(j ^ m, rows), :]
+    wait_all(sent)
 
 
 def norm_back(values, gain, grad):
@@ -353,11 +393,9 @@
     rows, width = q_ref.shape
     keys = refs_kv[0].shape[0]
     part = refs_dz[0].shape[0]
-    j = sub_j[0]
     for m in range(n_rep):
-        dz_ref[m * part : (m + 1) * part, :] = refs_dz[m][...]
-    start = pl.multiple_of(j * width, width)
-    dout = dot_nt(dz_ref[...], wout_ref[pl.ds(start, width), :]).astype(BF16)
+        dz_ref[spot(sub_j[0] ^ m, part), :] = refs_dz[m][...]
+    dout = dot_nt(dz_ref[...], wout_ref[...].reshape(width, dz_ref.shape[1])).astype(BF16)
     do_scr[...] = dout
     prod_t = (dout.astype(F32) * o_ref[...].astype(F32)).T
     heads = width // HEAD_DIM
@@ -413,13 +451,13 @@
 
 
 def qkv_back_kernel(
-    n_rep, n_inner, dq_ref, dkv_ref, refs_got, cos_ref, sin_ref, a_ref, w_ref, refs_x, dout_ref,
-    gain_two_ref, grad_ref, refs_da, dp_scr,
+    n_rep, n_part, at_ref, dq_ref, dkv_ref, refs_got, cos_ref, sin_ref, a_ref, w_ref, refs_x, dout_ref,
+    gain_two_ref, keep_ref, refs_send, refs_da, dp_scr, da_scr, grad_scr,
 ):
     width = dq_ref.shape[1]
     rows, dim = refs_x[0].shape
     lanes = 4 * width
-    high = grad_ref.shape[0] // n_inner
+    high = keep_ref.shape[0] // n_rep
     w_rows = high - 8
     dkv = dkv_ref[...]
     for got in refs_got:
@@ -430,10 +468,12 @@
     dp_scr[:, :width] = dq_ref[...]
     dp_scr[:, width : 2 * width] = (dk * cos - partner(dk) * sin).astype(BF16)
     dp_scr[:, 2 * width :] = dkv[:, width:].astype(BF16)
-    grad = dot_tn(a_ref[...], dp_scr[...]).astype(BF16)
+    grad_scr[:, : 3 * width] = dot_tn(a_ref[...], dp_scr[...]).astype(BF16)
+    grad_scr[:, 3 * width :] = dout_ref[...]
+    da_scr[...] = dot_nt(dp_scr[...], w_ref[...].reshape(dim, 3 * width))
     gain = jnp.zeros((1, dim), F32)
     for m in range(n_rep):
-        da = dot_nt(dp_scr[m * rows : (m + 1) * rows, :], w_ref[...])
+        da = da_scr[spot(at_ref[0] ^ m, rows), :]
         refs_da[m][...] = da.astype(BF16)
         hat, _ = hat_of(refs_x[m][...].astype(F32))
         gain = gain + jnp.sum(da * hat, axis=0, keepdims=True)
@@ -441,11 +481,19 @@
     strips = [g[:, k * lanes : (k + 1) * lanes] for g in (gain, gain_two_ref[...]) for k in range(per)]
     strips.append(jnp.zeros((8 - len(strips), lanes), F32))
     gains = jnp.concatenate(strips, axis=0).astype(BF16)
-    for p in range(n_inner):
-        sl = slice(p * w_rows, (p + 1) * w_rows)
-        grad_ref[p * high : p * high + w_rows, : 3 * width] = grad[sl, :]
-        grad_ref[p * high : p * high + w_rows, 3 * width :] = dout_ref[sl, :]
-        grad_ref[p * high + w_rows : (p + 1) * high, :] = gains
+    for l in range(n_part):
+        ref = keep_ref if l == 0 else refs_send[l - 1]
+        for m in range(n_rep):
+            shard = m * n_part + (at_ref[2] ^ l)
+            ref[m * high : m * high + w_rows, :] = grad_scr[spot(shard, w_rows), :]
+            ref[m * high + w_rows : (m + 1) * high, :] = gains
+
+
+def part_sum_kernel(keep_ref, refs_got, out_ref):
+    total = keep_ref[...].astype(F32)
+    for got in refs_got:
+        total = total + got[...].astype(F32)
+    out_ref[...] = total.astype(BF16)
 
 
 def grads_kernel(n_rep, at_ref, pieces, qkv_ref, out_ref, gains_ref):
@@ -564,7 +612,7 @@
         functools.partial(weight_kernel, n_inner, part), [((high, lanes), BF16)],
         [at, qkv_weight, out_weight, jnp.stack([gain_one, gain_two])], n_smem=1,
     )
-    w_all = lax.all_gather(w_pack, "inner", axis=0, tiled=True)
+    w_all = lax.all_gather(w_pack, "inner")
     x_first = lax.all_to_all(after(tokens, w_pack), "rep", 0, 0, tiled=True)
     in_late = after(in_weight, x_first)
     x_own = lax.all_to_all(x_first, "inner", 0, 0, axis_index_groups=planes, tiled=True)
@@ -579,29 +627,30 @@
         [((pitch, dim), BF16)],
         n_smem=1, n_any=1,
     )
-    ff_w = lax.all_gather(ff_pack, "inner", axis=0, tiled=True)
+    ff_w = lax.all_gather(ff_pack, "inner")
 
     own = w_all.reshape(n_rep, part, high, lanes)
     own = lax.dynamic_slice_in_dim(own, t, 1, 1)[:, 0, :w_rows, 3 * width :].reshape(n_rep * w_rows, width)
-    wo_own = rep_gather(after(own, xs[-1]))
-    wo_other = [part_swap(jnp.concatenate(wo_own, axis=0), l) for l in range(1, part)]
+    wo_own = rep_gather(after(own.reshape(n_rep, w_rows, width), xs[-1]))
+    wo_other = [part_swap(jnp.stack(wo_own), l) for l in range(1, part)]
 
     order = jnp.arange(total, dtype=jnp.int32)
-    spot = ((order // sub % n_rep) * part + t) * rows + (j ^ (order // rows)) * sub + order % sub
+    place = ((order // sub % n_rep) * part + t) * rows + (order // rows) * sub + order % sub
     inv_freq = 1.0 / THETA ** (jnp.arange(HEAD_DIM // 2, dtype=F32) * (2.0 / HEAD_DIM))
-    angle = spot.astype(F32)[:, None] * inv_freq[None, :]
+    angle = place.astype(F32)[:, None] * inv_freq[None, :]
     cos_half, sin_half = jnp.cos(angle), jnp.sin(angle)
     cos = jnp.concatenate([cos_half] * 4, axis=1)
     sin = jnp.concatenate([-sin_half, sin_half] * 2, axis=1)
 
     q, kv, a_one, w_qkv, gains = call(
-        grouped(qkv_kernel, (n_rep, part), (n_rep,) + (None,) * 8),
+        grouped(qkv_kernel, (n_rep,), (None, n_rep) + (None,) * 12),
         [
             ((total, width), BF16), ((total, 2 * width), BF16), ((total, dim), BF16),
-            ((dim, 3 * width), BF16), ((2, dim), F32),
+            ((n_inner, w_rows, 3 * width), BF16), ((2, dim), F32),
         ],
-        [*xs, w_all, cos, sin, c_own],
-        n_any=1, micros=4,
+        [at, *xs, w_all, cos, sin, c_own],
+        [((total, dim), BF16), ((n_inner, w_rows, 3 * width), BF16), ((n_inner, 8, lanes), BF16)],
+        n_smem=1, n_any=1, far=(1 + n_rep,), far_outs=(2, 3), n_sems=4, whole=True, micros=2,
     )
     kvs = [kv] + [part_swap(kv, l) for l in range(1, part)]
     heads = width // HEAD_DIM
@@ -609,36 +658,46 @@
     o, lse = call(
         grouped(attend_kernel, (part,), (None, part) + (None,) * 4),
         [((total, width), BF16), ((stat_rows, total), F32)],
-        [q, *kvs],
+        [q, *kvs, *wo_own[1:]],
         [((total * part, width), BF16), ((width, total * part), BF16)],
-        micros=8,
+        n_any=n_rep - 1, micros=6,
     )
     os_ = rep_gather(o)
     cs = rep_gather(after(c_own, xs[-1]))
+    n_spots = len(packed_rows(pitch, dim, 2 * ff)[1])
+    per = width // (part * w_rows)
     ff_out = call(
         grouped(
-            ff_kernel, (n_rep, part, pitch),
-            (None, n_rep, n_rep, n_rep, part - 1, None, n_rep, None, None, n_rep) + (None,) * 12,
+            ff_kernel, (n_rep, part),
+            (None, n_rep, n_rep, n_rep, part - 1, None, n_rep, None, None, n_rep) + (None,) * 16,
         ),
         [((rows, dim), F32)]
         + [((rows, dim), BF16)] * n_rep
         + [
-            ((total, dim), BF16), ((total, ff), BF16), ((total, 2 * ff), BF16), ((total, dim), BF16),
-            ((total, dim), BF16), ((dim, dim), BF16), ((ff, dim), BF16), ((1, dim), F32),
+            ((total, dim), BF16), ((total, ff), BF16), ((total, 2 * ff), BF16),
+            ((total, dim), BF16), ((per, part, w_rows, dim), BF16), ((1, dim), F32),
         ],
         [at, *xs, *os_, *wo_own, *wo_other, ff_w, *cs, gains],
-        [((total, dim), F32), ((total, 2 * ff), F32), ((total, ff), F32), ((dim, 2 * ff), BF16)],
-        n_smem=1, micros=14,
+        [
+            ((total, dim), F32), ((total, 2 * ff), F32), ((total, ff), F32), ((n_inner, w_rows, 2 * ff), BF16),
+            ((n_inner, pitch, dim), BF16), ((total, dim), BF16), ((total, dim), BF16), ((total, dim), BF16),
+            ((n_rep, part, w_rows, dim), BF16),
+        ],
+        n_smem=1, far=range(1, 1 + 4 * n_rep + part), far_outs=(4 + n_rep, 5 + n_rep),
+        n_sems=n_rep * (part + 3) + 1 + n_spots + 1 + per, whole=True, micros=11,
     )
     r_own, da_two = ff_out[0], ff_out[1 : 1 + n_rep]
-    a_two, gated, d_hidden, c_all, o_all, w_out, w_down, gain_two_part = ff_out[1 + n_rep :]
+    a_two, gated, d_hidden, o_all, w_out, gain_two_part = ff_out[1 + n_rep :]
     das = rep_trade(da_two)
     ff_back = call(
-        grouped(ff_grads_kernel, (n_rep, n_inner, pitch), (None,) * 5 + (n_rep, None, None)),
-        [((rows, dim), BF16)] * n_rep + [((n_inner * ff_high, 2 * ff), BF16)],
-        [gated, w_down, c_all, a_two, d_hidden],
-        [((ff, dim), BF16)],
-        micros=30,
+        grouped(ff_grads_kernel, (n_rep,), (None, None, None, n_rep, None, None, n_rep) + (None,) * 6),
+        [((rows, dim), BF16)] * n_rep + [((n_inner, ff_high, 2 * ff), BF16)],
+        [at, gated, ff_w, *cs, a_two, d_hidden],
+        [
+            ((n_inner, pitch, dim), BF16), ((n_inner, pitch, dim), BF16), ((total, dim), BF16),
+            ((n_inner, w_rows, 2 * ff), BF16),
+        ],
+        n_smem=1, far=range(2, 3 + n_rep), far_outs=(n_rep,), n_sems=n_rep + 2 * n_spots + 1, whole=True, micros=5,
     )
     lo, ff_grad = ff_back[:-1], ff_back[-1]
     dr, dz = call(
@@ -647,7 +706,7 @@
         [*das, r_own, c_own, gains, ff_grad],
         n_any=1, micros=2,
     )
-    ff_grad = lax.psum_scatter(after(ff_grad, *das[1:]), "inner", scatter_dimension=0, tiled=True)
+    ff_grad = lax.psum_scatter(after(ff_grad, *das[1:]), "inner", scatter_dimension=0)
     dzs = rep_gather(dz)
 
     back = call(
@@ -674,20 +733,30 @@
         out_grad_kernel, [((dim, width), BF16)], [at, o_all, dz_all], n_smem=1, micros=2,
     )
     qkv_out = call(
-        grouped(qkv_back_kernel, (n_rep, n_inner), (None, None, part - 1) + (None,) * 4 + (n_rep,) + (None,) * 3 + (n_rep, None)),
-        [((n_inner * high, lanes), BF16)] + [((rows, dim), BF16)] * n_rep,
-        [dq, dkv, *gots, cos, sin, a_one, w_qkv, *xs, d_out, gain_two_part],
-        [((total, 3 * width), BF16)],
-        micros=6,
-    )
-    das = rep_trade(qkv_out[1:])
+        grouped(
+            qkv_back_kernel, (n_rep, part),
+            (None, None, None, part - 1, None, None, None, None, n_rep, None, None, None, part - 1, n_rep) + (None,) * 3,
+        ),
+        [((n_rep * high, lanes), BF16)] * part + [((rows, dim), BF16)] * n_rep,
+        [at, dq, dkv, *gots, cos, sin, a_one, w_qkv, *xs, d_out, gain_two_part],
+        [((total, 3 * width), BF16), ((total, dim), F32), ((dim, lanes), BF16)],
+        n_smem=1, micros=4,
+    )
+    keep, sends, da_one = qkv_out[0], qkv_out[1:part], qkv_out[part:]
+    gots = [part_swap(x, l + 1) for l, x in enumerate(sends)]
+    (summed,) = call(
+        grouped(part_sum_kernel, (), (None, part - 1, None)), [((n_rep * high, lanes), BF16)], [keep, *gots]
+    )
+    das = rep_trade(da_one)
     ff_grad = after(ff_grad, *das[1:])
-    d_pack = lax.psum_scatter(after(qkv_out[0], ff_grad), "inner", scatter_dimension=0, tiled=True)
+    d_pack = lax.psum_scatter(
+        after(summed, ff_grad), "inner", scatter_dimension=0, axis_index_groups=planes, tiled=True
+    )
     parts = call(
         grouped(last_kernel, (n_rep,), (None, n_rep, n_rep, None, None, None, None, n_rep, None)),
-        home, [at, *das, *los, xs[0], dr, r_own, gains], [((rows, dim), F32)], n_smem=1, micros=2,
-    )
-    ff_grads = jnp.concatenate([after(ff_grad, *das[1:])] * n_rep, axis=0)
+        home, [at, *das, *los, xs[0], dr, r_own, gains], [((rows, dim), F32)], n_smem=1, whole=True, micros=2,
+    )
+    ff_grads = jnp.concatenate([ff_grad] * n_rep, axis=0)
     ff_grads = lax.all_to_all(ff_grads, "rep", 0, 0, tiled=True).reshape(n_rep, ff_high, 2 * ff)
     back_home = send_home(parts)
     quarter = after(d_pack, *back_home)

time: 265 us -> 256 us (0.966)
  Pallas kernels: 81 us -> 62.2 us
  local copies, waits for them, and re-layouts: 11.4 us -> 17.9 us
  waiting for transfers between devices: 75.8 us -> 79.1 us
    pallas_call x14 -> x15, Pallas kernels: 81 us -> 62.2 us  [call(): pl.pallas_call(without_waited, out_shape=[jax.ShapeDtypeStruct(s, d) for...]
    unnamed x88 -> x136, local copies, waits for them, and re-layouts: 9.17 us -> 16.4 us
    ppermute x27, waiting for transfers between devices: 39.1 us -> 43.6 us  [rep_swap(): return lax.ppermute(x, 'rep', [(a, a ^ m) for a in range(n_rep)])]
    reduce_scatter x2, waiting for transfers between devices: 0.02 us -> 2.78 us  [the longest x1 2.78 us: on_device(): lax.psum_scatter(after(ff_grad, *das[1:]), 'inner', scatter_dimension=0)]
    all_to_all x1, waiting for transfers between devices: 3.9 us -> 1.15 us  [on_device(): lax.all_to_all(after(c_first, x_own), 'inner', 0, 0, axis_index_groups=pl...]
  transfers between devices with their start and end apart: 41 -> 42, of which waited for: 16 -> 25; matrix products, arithmetic and copies ran while one was open for 2% -> 3% of each run, Pallas kernels for 23% -> 17%
where the time goes in v4:
time: 256 us; the launch traced here: 255 us
  waiting for transfers between devices  79.1 us (31%)
  Pallas kernels  62.2 us (24%)
  starting transfers between devices  55.5 us (22%)
  blocking collectives  19.7 us (8%)
  local copies, waits for them, and re-layouts  17.9 us (7%)
  between operations  14.4 us (6%)
  other arithmetic  6.64 us (3%)
    pallas_call x15, Pallas kernels, call(): pl.pallas_call(without_waited, out_shape=[jax.ShapeDtypeStruct(s, d) for...  62.2 us
    ppermute x27, waiting for transfers between devices, rep_swap(): return lax.ppermute(x, 'rep', [(a, a ^ m) for a in range(n_rep)])  43.6 us
    ppermute x27, starting transfers between devices, rep_swap(): return lax.ppermute(x, 'rep', [(a, a ^ m) for a in range(n_rep)])  34.1 us
    ppermute x4, waiting for transfers between devices, send_home(): got.append(lax.ppermute(pieces[k], ('rep', 'inner'), pairs))  17.9 us
    unnamed x136, local copies, waits for them, and re-layouts  16.4 us
    all_to_all x1, waiting for transfers between devices, on_device(): lax.all_to_all(x_first, 'inner', 0, 0, axis_index_groups=planes, tiled=True)  11.3 us
    all_to_all x1, blocking collectives, on_device(): x_first = lax.all_to_all(after(tokens, w_pack), 'rep', 0, 0, tiled=True)  10.9 us
    all_to_all x1, blocking collectives, on_device(): c_first = lax.all_to_all(after(cotangent, x_first), 'rep', 0, 0, tiled=True)  8.78 us
  transfers between devices with their start and end apart: 42, of which 25 were waited for; matrix products, arithmetic and copies ran while one was open for 3% of the time, Pallas kernels for 17%

profile of v4, /device:TPU:0, one launch (start us, length us, event | category | flops | bytes accessed | tf_op | source)
XLA Modules:
  0.0 255.3 jit_solution(10808879149422705971)
XLA Ops:
  11.6 10.9 %all_to_all.53 = bf16[4,32,1024]{2,1,0:T(8,128)(2,1)} all-to-all(bf16[4,32,1024]{2,1,0:T(8,128)(2,1)S(1)} %bitcast.50), channel_id=1, replica_groups=mesh['rep'=4,'inner'=8] {'rep'}, dimensions={0} | all-to-all | bytes 524288 | tf_op jit(solution)/shard_map/all_to_all | solution.py:616
  24.2 8.8 %all_to_all.54 = bf16[4,32,1024]{2,1,0:T(8,128)(2,1)} all-to-all(bf16[4,32,1024]{2,1,0:T(8,128)(2,1)S(1)} %bitcast.51), channel_id=1, replica_groups=mesh['rep'=4,'inner'=8] {'rep'}, dimensions={0} | all-to-all | bytes 524288 | tf_op jit(solution)/shard_map/all_to_all | solution.py:619
  33.0 4.9 %all-to-all-start.1 = ((bf16[4,32,1024]{2,1,0:T(8,128)(2,1)}), bf16[4,32,1024]{2,1,0:T(8,128)(2,1)S(1)}, u32[]{:S(2)}, u32[]{:S(2)}) async-start(bf16[4,32,1024]{2,1,0:T(8,128)(2,1)} %all_to_all.53), calls=%async_computation.1 | async-start | bytes 524288 | tf_op jit(solution)/shard_map/all_to_all | solution.py:618
  37.9 11.3 %all-to-all-done.1 = bf16[4,32,1024]{2,1,0:T(8,128)(2,1)S(1)} async-done(((bf16[4,32,1024]{2,1,0:T(8,128)(2,1)}), bf16[4,32,1024]{2,1,0:T(8,128)(2,1)S(1)}, u32[]{:S(2)}, u32[]{:S(2)}) %all-to-all-start.1) | async-done | bytes 262176 | tf_op jit(solution)/shard_map/all_to_all | solution.py:618
  52.7 3.4 %all-to-all-start.3 = ((bf16[4,32,1024]{2,1,0:T(8,128)(2,1)}), bf16[4,32,1024]{2,1,0:T(8,128)(2,1)S(1)}, u32[]{:S(2)}, u32[]{:S(2)}) async-start(bf16[4,32,1024]{2,1,0:T(8,128)(2,1)} %bitcast.11), calls=%async_computation.3 | async-start | bytes 524288 | tf_op jit(solution)/shard_map/all_to_all | solution.py:621
  66.8 6.4 %shard_map.144 = (bf16[512,256]{1,0:T(8,128)(2,1)}, bf16[512,512]{1,0:T(8,128)(2,1)}, bf16[512,1024]{1,0:T(8,128)(2,1)}, bf16[8,128,768]{2,1,0:T(8,128)(2,1)}, f32[2,1024]{1,0:T(2,128)}) custom-call(s32[3]{0:T(128)} %copy-done.10, bf16[128,1024]{1,0:T(8,128)(2,1)} %bitcast.33, bf16[128,1024]{1,0:T(8,128)(2,1)} %copy-done.25, bf16[128,1024]{1,0:T(8,128)(2,1)} %copy-done.23, ...), custom_call_target="tpu_custom_call" | custom-call | flops 2000000000 | bytes 2000000 | tf_op jit(solution)/shard_map/pallas_call | solution.py:44
  81.1 6.2 %shard_map.145 = (bf16[512,256]{1,0:T(8,128)(2,1)S(1)}, f32[8,512]{1,0:T(8,128)S(1)}) custom-call(bf16[512,256]{1,0:T(8,128)(2,1)S(1)} %copy-done.43, bf16[512,512]{1,0:T(8,128)(2,1)S(1)} %copy-done.16, bf16[512,512]{1,0:T(8,128)(2,1)S(1)} %collective-permute-done.3.refs_2_.refs_9_, bf16[4,128,256]{2,1,0:T(8,128)(2,1)S(1)} %collective-permute-done.4.refs_3_.refs_10_, ...), custom_call_target="tpu_custom_call" | custom-call | flops 6000000000 | bytes 6000000 | tf_op jit(solution)/shard_map/pallas_call | solution.py:44
  92.1 5.5 %collective-permute-done.9.refs_8_ = bf16[512,256]{1,0:T(8,128)(2,1)S(1)} collective-permute-done((bf16[512,256]{1,0:T(8,128)(2,1)S(1)}, bf16[512,256]{1,0:T(8,128)(2,1)S(1)}, u32[]{:S(2)}, u32[]{:S(2)}) %collective-permute-start.9) | collective-permute-done | bytes 262176 | tf_op jit(solution)/shard_map/ppermute | solution.py:578
  97.6 4.2 %collective-permute-done.8.refs_7_ = bf16[512,256]{1,0:T(8,128)(2,1)S(1)} collective-permute-done((bf16[512,256]{1,0:T(8,128)(2,1)S(1)}, bf16[512,256]{1,0:T(8,128)(2,1)S(1)}, u32[]{:S(2)}, u32[]{:S(2)}) %collective-permute-start.8) | collective-permute-done | bytes 262176 | tf_op jit(solution)/shard_map/ppermute | solution.py:578
  104.1 14.9 %shard_map.147 = (f32[128,1024]{1,0:T(8,128)}, bf16[128,1024]{1,0:T(8,128)(2,1)}, bf16[128,1024]{1,0:T(8,128)(2,1)}, bf16[128,1024]{1,0:T(8,128)(2,1)}, bf16[128...) custom-call(s32[3]{0:T(128)} %copy-done.10, ...), custom_call_target="tpu_custom_call" | custom-call | flops 11000000512 | bytes 11000000 | tf_op jit(solution)/shard_map/pallas_call | solution.py:44
  122.6 7.1 %shard_map.148 = (bf16[128,1024]{1,0:T(8,128)(2,1)}, bf16[128,1024]{1,0:T(8,128)(2,1)}, bf16[128,1024]{1,0:T(8,128)(2,1)}, bf16[128,1024]{1,0:T(8,128)(2,1)}, bf16[8,192,1536]{2,1,0:T(8,128)(2,1)}) custom-call(s32[3]{0:T(128)} %copy-done.10, bf16[512,768]{1,0:T(8,128)(2,1)} %get-tuple-element.86.refs_1_, bf16[8,192,1536]{2,1,0:T(8,128)(2,1)} %bitcast.55, ...), custom_call_target="tpu_custom_call" | custom-call | flops 5000000000 | bytes 5000000 | tf_op jit(solution)/shard_map/pallas_call | solution.py:44
  129.8 3.9 %collective-permute-done.15.refs_2_ = bf16[128,1024]{1,0:T(8,128)(2,1)S(1)} collective-permute-done((bf16[128,1024]{1,0:T(8,128)(2,1)}, bf16[128,1024]{1,0:T(8,128)(2,1)S(1)}, u32[]{:S(2)}, u32[]{:S(2)}) %collective-permute-start.15) | collective-permute-done | bytes 262176 | tf_op jit(solution)/shard_map/ppermute | solution.py:578
  142.1 6.7 %collective-permute-done.19.refs_4_ = bf16[128,1024]{1,0:T(8,128)(2,1)S(1)} collective-permute-done((bf16[128,1024]{1,0:T(8,128)(2,1)S(1)}, bf16[128,1024]{1,0:T(8,128)(2,1)S(1)}, u32[]{:S(2)}, u32[]{:S(2)}) %collective-permute-start.19) | collective-permute-done | bytes 262176 | tf_op jit(solution)/shard_map/ppermute | solution.py:578
  154.6 7.1 %shard_map.150 = (bf16[512,256]{1,0:T(8,128)(2,1)S(1)}, f32[512,512]{1,0:T(8,128)S(1)}, bf16[512,512]{1,0:T(8,128)(2,1)S(1)}, bf16[512,1024]{1,0:T(8,128)(2,1)S(1)}) custom-call(s32[3]{0:T(128)S(1)} %copy-done.11, bf16[128,1024]{1,0:T(8,128)(2,1)S(1)} %get-tuple-element.90.refs_1_, bf16[128,1024]{1,0:T(8,128)(2,1)S(1)} %collective-permute-done.17.refs_2_, ...), custom_call_target="tpu_custom_call" | custom-call | flops 10000000000 | bytes 10000000 | tf_op jit(solution)/shard_map/pallas_call | solution.py:44
  166.2 3.6 %shard_map.152 = (bf16[544,1024]{1,0:T(8,128)(2,1)S(1)}, bf16[544,1024]{1,0:T(8,128)(2,1)S(1)}, bf16[128,1024]{1,0:T(8,128)(2,1)S(1)}, bf16[128,1024]{1,0:T(8,12...) custom-call(s32[3]{0:T(128)S(1)} %copy-done.11, ...), custom_call_target="tpu_custom_call" | custom-call | flops 4000000000 | bytes 4000000 | tf_op jit(solution)/shard_map/pallas_call | solution.py:44
  175.6 4.4 %collective-permute-done.24.refs_2_ = bf16[128,1024]{1,0:T(8,128)(2,1)S(1)} collective-permute-done((bf16[128,1024]{1,0:T(8,128)(2,1)S(1)}, bf16[128,1024]{1,0:T(8,128)(2,1)S(1)}, u32[]{:S(2)}, u32[]{:S(2)}) %collective-permute-start.24) | collective-permute-done | bytes 262176 | tf_op jit(solution)/shard_map/ppermute | solution.py:578
  180.1 5.8 %collective-permute-done.25.refs_3_ = bf16[128,1024]{1,0:T(8,128)(2,1)S(1)} collective-permute-done((bf16[128,1024]{1,0:T(8,128)(2,1)S(1)}, bf16[128,1024]{1,0:T(8,128)(2,1)S(1)}, u32[]{:S(2)}, u32[]{:S(2)}) %collective-permute-start.25) | collective-permute-done | bytes 262176 | tf_op jit(solution)/shard_map/ppermute | solution.py:578
  188.7 3.3 %pad_maximum_fusion = bf16[768,1536]{1,0:T(8,128)(2,1)} fusion(bf16[192,1536]{1,0:T(8,128)(2,1)} %bitcast.49), kind=kLoop, calls=%fused_computation | loop fusion | flops 9437184 | bytes 2949120 | tf_op jit(solution)/shard_map/concatenate | solution.py:759
  192.0 3.7 %all-to-all-start.4 = ((bf16[4,192,1536]{2,1,0:T(8,128)(2,1)}), bf16[4,192,1536]{2,1,0:T(8,128)(2,1)S(1)}, u32[]{:S(2)}, u32[]{:S(2)}) async-start(bf16[4,192,1536]{2,1,0:T(8,128)(2,1)} %bitcast.47), calls=%async_computation.6 | async-start | bytes 4718592 | tf_op jit(solution)/shard_map/all_to_all | solution.py:760
  195.7 3.5 %shard_map.153 = (bf16[64,1024]{1,0:T(8,128)(2,1)}, bf16[64,1024]{1,0:T(8,128)(2,1)}, bf16[64,1024]{1,0:T(8,128)(2,1)}, bf16[64,1024]{1,0:T(8,128)(2,1)}) custom-call(s32[3]{0:T(128)} %copy-done.10, bf16[128,1024]{1,0:T(8,128)(2,1)} %copy-done.45, bf16[128,1024]{1,0:T(8,128)(2,1)} %copy-done.62, bf16[128,1024]{1,0:T(8,128)(2,1)} %copy-done.63, ...), custom_call_target="tpu_custom_call" | custom-call | flops 2000000000 | bytes 2000000 | tf_op jit(solution)/shard_map/pallas_call | solution.py:44
  200.8 3.9 %collective-permute-start.28 = (bf16[64,1024]{1,0:T(8,128)(2,1)}, bf16[64,1024]{1,0:T(8,128)(2,1)S(1)}, u32[]{:S(2)}, u32[]{:S(2)}) collective-permute-start(bf16[64,1024]{1,0:T(8,128)(2,1)} %get-tuple-element.116), channel_id=1, source_target_pairs={{0,2},{1,3},{2,10},{3,11},{4,18},{5,19},{6,26},{7,27},{8,0},{9,1},... | collective-permute-start | bytes 393224 | tf_op jit(solution)/shard_map/ppermute | solution.py:605
  208.4 17.6 %collective-permute-done.28.refs_2_ = bf16[64,1024]{1,0:T(8,128)(2,1)S(1)} collective-permute-done((bf16[64,1024]{1,0:T(8,128)(2,1)}, bf16[64,1024]{1,0:T(8,128)(2,1)S(1)}, u32[]{:S(2)}, u32[]{:S(2)}) %collective-permute-start.28) | collective-permute-done | bytes 131104 | tf_op jit(solution)/shard_map/ppermute | solution.py:605
  228.8 3.2 %collective-permute-start.33 = (bf16[136,1024]{1,0:T(8,128)(2,1)}, bf16[136,1024]{1,0:T(8,128)(2,1)S(1)}, u32[]{:S(2)}, u32[]{:S(2)}) collective-permute-start(bf16[136,1024]{1,0:T(8,128)(2,1)} %reduce-scatter.5.cloned.1.call-done.refs_5_.refs_1_), channel_id=1, source_target_pairs={{0,16},{8,24},{16,0},{24,8},{1,17},{9,25},{17,1},{25,9},{2,18},{10... | collective-permute-start | bytes 835592 | tf_op jit(solution)/shard_map/ppermute | solution.py:578
  239.4 4.0 %shard_map.157 = (f32[128,5248]{1,0:T(8,128)}, f32[328,1024]{1,0:T(8,128)}) custom-call(bf16[4,192,1536]{2,1,0:T(8,128)(2,1)S(1)} %all-to-all-done.4.refs_0_, bf16[136,1024]{1,0:T(8,128)(2,1)S(1)} %copy-done.19), custom_call_target="tpu_custom_call" | custom-call | flops 4000000000 | bytes 4000000 | tf_op jit(solution)/shard_map/pallas_call | solution.py:44
  (229 shorter events, 86.5 us)
Async XLA Ops:
  7.2 51.3 %all-gather.5.cloned.1.call-start = ((), (), s32[]{:S(2)}) async-start(), calls=%async_computation.9 | async-start | bytes 2506752 | tf_op jit(solution)/shard_map/all_gather | solution.py:615
  11.5 92.6 %all-gather.7.cloned.1.call-start = ((), (), s32[]{:S(2)}) async-start(), calls=%async_computation.10 | async-start | bytes 5308416 | tf_op jit(solution)/shard_map/all_gather | solution.py:630
  33.0 16.2 %all-to-all-start.1 = ((bf16[4,32,1024]{2,1,0:T(8,128)(2,1)}), bf16[4,32,1024]{2,1,0:T(8,128)(2,1)S(1)}, u32[]{:S(2)}, u32[]{:S(2)}) async-start(bf16[4,32,1024]{2,1,0:T(8,128)(2,1)} %all_to_all.53), calls=%async_computation.1 | async-start | bytes 524288 | tf_op jit(solution)/shard_map/all_to_all | solution.py:618
  51.6 12.9 %collective-permute-start.1 = (bf16[128,1024]{1,0:T(8,128)(2,1)S(1)}, bf16[128,1024]{1,0:T(8,128)(2,1)S(1)}, u32[]{:S(2)}, u32[]{:S(2)}) collective-permute-start(bf16[128,1024]{1,0:T(8,128)(2,1)S(1)} %bitcast.31), channel_id=1, source_target_pairs={{0,16},{8,24},{16,0},{24,8},{1,17},{9,25},{17,1},{25,9},{2,18},{10... | collective-permute-start | bytes 786440 | tf_op jit(solution)/shard_map/ppermute | solution.py:578
  52.7 13.4 %all-to-all-start.3 = ((bf16[4,32,1024]{2,1,0:T(8,128)(2,1)}), bf16[4,32,1024]{2,1,0:T(8,128)(2,1)S(1)}, u32[]{:S(2)}, u32[]{:S(2)}) async-start(bf16[4,32,1024]{2,1,0:T(8,128)(2,1)} %bitcast.11), calls=%async_computation.3 | async-start | bytes 524288 | tf_op jit(solution)/shard_map/all_to_all | solution.py:621
  56.1 132.6 %reduce-scatter.3.cloned.1.call-start = ((), (), s32[]{:S(2)}) async-start(), calls=%async_computation.7 | async-start | bytes 5308416 | tf_op jit(solution)/shard_map/reduce_scatter | solution.py:709
  59.5 13.8 %collective-permute-start.6 = (bf16[4,128,256]{2,1,0:T(8,128)(2,1)S(1)}, bf16[4,128,256]{2,1,0:T(8,128)(2,1)S(1)}, u32[]{:S(2)}, u32[]{:S(2)}) collective-permute-start(bf16[4,128,256]{2,1,0:T(8,128)(2,1)S(1)} %dynamic-slice_bitcast_fusion.refs_9_), channel_id=1, source_target_pairs={{0,24},{8,16},{16,8},{24,0},{1,25},{9,17},{17,9},{25,1},{2,26},{10... | collective-permute-start | bytes 786440 | tf_op jit(solution)/shard_map/ppermute | solution.py:578
  75.0 27.5 %collective-permute-start.10 = (bf16[4,4,128,256]{3,2,1,0:T(8,128)(2,1)S(1)}, bf16[4,4,128,256]{3,2,1,0:T(8,128)(2,1)S(1)}, u32[]{:S(2)}, u32[]{:S(2)}) collective-permute-start(bf16[4,4,128,256]{3,2,1,0:T(8,128)(2,1)S(1)} %pad_maximum_fusion.1), channel_id=1, source_target_pairs={{0,1},{1,0},{2,3},{3,2},{4,5},{5,4},{6,7},{7,6},{8,9},{9,8},{10,11... | collective-permute-start | bytes 3145736 | tf_op jit(solution)/shard_map/ppermute | solution.py:586
  75.1 14.7 %collective-permute-start.13 = (bf16[128,1024]{1,0:T(8,128)(2,1)}, bf16[128,1024]{1,0:T(8,128)(2,1)S(1)}, u32[]{:S(2)}, u32[]{:S(2)}) collective-permute-start(bf16[128,1024]{1,0:T(8,128)(2,1)} %bitcast.38), channel_id=1, source_target_pairs={{0,24},{8,16},{16,8},{24,0},{1,25},{9,17},{17,9},{25,1},{2,26},{10... | collective-permute-start | bytes 786440 | tf_op jit(solution)/shard_map/ppermute | solution.py:578
  77.8 14.2 %collective-permute-start.11 = (bf16[128,1024]{1,0:T(8,128)(2,1)}, bf16[128,1024]{1,0:T(8,128)(2,1)S(1)}, u32[]{:S(2)}, u32[]{:S(2)}) collective-permute-start(bf16[128,1024]{1,0:T(8,128)(2,1)} %bitcast.40), channel_id=1, source_target_pairs={{0,8},{8,0},{16,24},{24,16},{1,9},{9,1},{17,25},{25,17},{2,10},{10... | collective-permute-start | bytes 786440 | tf_op jit(solution)/shard_map/ppermute | solution.py:578
  120.3 13.4 %collective-permute-start.15 = (bf16[128,1024]{1,0:T(8,128)(2,1)}, bf16[128,1024]{1,0:T(8,128)(2,1)S(1)}, u32[]{:S(2)}, u32[]{:S(2)}) collective-permute-start(bf16[128,1024]{1,0:T(8,128)(2,1)} %get-tuple-element.83), channel_id=1, source_target_pairs={{0,16},{8,24},{16,0},{24,8},{1,17},{9,25},{17,1},{25,9},{2,18},{10... | collective-permute-start | bytes 786440 | tf_op jit(solution)/shard_map/ppermute | solution.py:578
  134.4 93.9 %reduce-scatter.5.cloned.1.call-start = ((), (), s32[]{:S(2)}) async-start(), calls=%async_computation.8 | async-start | bytes 1392640 | tf_op jit(solution)/shard_map/reduce_scatter | solution.py:752
  141.4 13.2 %collective-permute-start.17 = (bf16[128,1024]{1,0:T(8,128)(2,1)S(1)}, bf16[128,1024]{1,0:T(8,128)(2,1)S(1)}, u32[]{:S(2)}, u32[]{:S(2)}) collective-permute-start(bf16[128,1024]{1,0:T(8,128)(2,1)S(1)} %get-tuple-element.90.refs_1_), channel_id=1, source_target_pairs={{0,8},{8,0},{16,24},{24,16},{1,9},{9,1},{17,25},{25,17},{2,10},{10... | collective-permute-start | bytes 786440 | tf_op jit(solution)/shard_map/ppermute | solution.py:578
  148.7 13.0 %collective-permute-start.20 = (bf16[128,1024]{1,0:T(8,128)(2,1)S(1)}, bf16[128,1024]{1,0:T(8,128)(2,1)S(1)}, u32[]{:S(2)}, u32[]{:S(2)}) collective-permute-start(bf16[128,1024]{1,0:T(8,128)(2,1)S(1)} %copy-done.59), channel_id=1, source_target_pairs={{0,8},{8,0},{16,24},{24,16},{1,9},{9,1},{17,25},{25,17},{2,10},{10... | collective-permute-start | bytes 786440 | tf_op jit(solution)/shard_map/ppermute | solution.py:578
  151.1 12.9 %collective-permute-start.22 = (bf16[128,1024]{1,0:T(8,128)(2,1)S(1)}, bf16[128,1024]{1,0:T(8,128)(2,1)S(1)}, u32[]{:S(2)}, u32[]{:S(2)}) collective-permute-start(bf16[128,1024]{1,0:T(8,128)(2,1)S(1)} %copy-done.56), channel_id=1, source_target_pairs={{0,24},{8,16},{16,8},{24,0},{1,25},{9,17},{17,9},{25,1},{2,26},{10... | collective-permute-start | bytes 786440 | tf_op jit(solution)/shard_map/ppermute | solution.py:578
  172.2 13.7 %collective-permute-start.25 = (bf16[128,1024]{1,0:T(8,128)(2,1)S(1)}, bf16[128,1024]{1,0:T(8,128)(2,1)S(1)}, u32[]{:S(2)}, u32[]{:S(2)}) collective-permute-start(bf16[128,1024]{1,0:T(8,128)(2,1)S(1)} %get-tuple-element.110), channel_id=1, source_target_pairs={{0,16},{8,24},{16,0},{24,8},{1,17},{9,25},{17,1},{25,9},{2,18},{10... | collective-permute-start | bytes 786440 | tf_op jit(solution)/shard_map/ppermute | solution.py:578
  172.6 13.3 %collective-permute-start.26 = (bf16[128,1024]{1,0:T(8,128)(2,1)S(1)}, bf16[128,1024]{1,0:T(8,128)(2,1)S(1)}, u32[]{:S(2)}, u32[]{:S(2)}) collective-permute-start(bf16[128,1024]{1,0:T(8,128)(2,1)S(1)} %get-tuple-element.111), channel_id=1, source_target_pairs={{0,24},{8,16},{16,8},{24,0},{1,25},{9,17},{17,9},{25,1},{2,26},{10... | collective-permute-start | bytes 786440 | tf_op jit(solution)/shard_map/ppermute | solution.py:578
  192.0 47.4 %all-to-all-start.4 = ((bf16[4,192,1536]{2,1,0:T(8,128)(2,1)}), bf16[4,192,1536]{2,1,0:T(8,128)(2,1)S(1)}, u32[]{:S(2)}, u32[]{:S(2)}) async-start(bf16[4,192,1536]{2,1,0:T(8,128)(2,1)} %bitcast.47), calls=%async_computation.6 | async-start | bytes 4718592 | tf_op jit(solution)/shard_map/all_to_all | solution.py:760
  200.8 25.3 %collective-permute-start.28 = (bf16[64,1024]{1,0:T(8,128)(2,1)}, bf16[64,1024]{1,0:T(8,128)(2,1)S(1)}, u32[]{:S(2)}, u32[]{:S(2)}) collective-permute-start(bf16[64,1024]{1,0:T(8,128)(2,1)} %get-tuple-element.116), channel_id=1, source_target_pairs={{0,2},{1,3},{2,10},{3,11},{4,18},{5,19},{6,26},{7,27},{8,0},{9,1},... | collective-permute-start | bytes 393224 | tf_op jit(solution)/shard_map/ppermute | solution.py:605
  204.7 22.3 %collective-permute-start.29 = (bf16[64,1024]{1,0:T(8,128)(2,1)}, bf16[64,1024]{1,0:T(8,128)(2,1)S(1)}, u32[]{:S(2)}, u32[]{:S(2)}) collective-permute-start(bf16[64,1024]{1,0:T(8,128)(2,1)} %get-tuple-element.117), channel_id=1, source_target_pairs={{0,4},{1,5},{2,12},{3,13},{4,20},{5,21},{6,28},{7,29},{8,6},{9,7},... | collective-permute-start | bytes 393224 | tf_op jit(solution)/shard_map/ppermute | solution.py:605
  205.6 22.0 %collective-permute-start.30 = (bf16[64,1024]{1,0:T(8,128)(2,1)}, bf16[64,1024]{1,0:T(8,128)(2,1)S(1)}, u32[]{:S(2)}, u32[]{:S(2)}) collective-permute-start(bf16[64,1024]{1,0:T(8,128)(2,1)} %get-tuple-element.118), channel_id=1, source_target_pairs={{0,6},{1,7},{2,14},{3,15},{4,22},{5,23},{6,30},{7,31},{8,4},{9,5},... | collective-permute-start | bytes 393224 | tf_op jit(solution)/shard_map/ppermute | solution.py:605
  228.3 15.1 %collective-permute-start.34 = (bf16[136,1024]{1,0:T(8,128)(2,1)}, bf16[136,1024]{1,0:T(8,128)(2,1)S(1)}, u32[]{:S(2)}, u32[]{:S(2)}) collective-permute-start(bf16[136,1024]{1,0:T(8,128)(2,1)} %reduce-scatter.5.cloned.1.call-done.refs_5_.refs_1_), channel_id=1, source_target_pairs={{0,24},{8,16},{16,8},{24,0},{1,25},{9,17},{17,9},{25,1},{2,26},{10... | collective-permute-start | bytes 835592 | tf_op jit(solution)/shard_map/ppermute | solution.py:578
  228.8 15.7 %collective-permute-start.33 = (bf16[136,1024]{1,0:T(8,128)(2,1)}, bf16[136,1024]{1,0:T(8,128)(2,1)S(1)}, u32[]{:S(2)}, u32[]{:S(2)}) collective-permute-start(bf16[136,1024]{1,0:T(8,128)(2,1)} %reduce-scatter.5.cloned.1.call-done.refs_5_.refs_1_), channel_id=1, source_target_pairs={{0,16},{8,24},{16,0},{24,8},{1,17},{9,25},{17,1},{25,9},{2,18},{10... | collective-permute-start | bytes 835592 | tf_op jit(solution)/shard_map/ppermute | solution.py:578
  232.0 14.3 %collective-permute-start.32 = (bf16[136,1024]{1,0:T(8,128)(2,1)}, bf16[136,1024]{1,0:T(8,128)(2,1)S(1)}, u32[]{:S(2)}, u32[]{:S(2)}) collective-permute-start(bf16[136,1024]{1,0:T(8,128)(2,1)} %reduce-scatter.5.cloned.1.call-done.refs_5_.refs_1_), channel_id=1, source_target_pairs={{0,8},{8,0},{16,24},{24,16},{1,9},{9,1},{17,25},{25,17},{2,10},{10... | collective-permute-start | bytes 835592 | tf_op jit(solution)/shard_map/ppermute | solution.py:578
  (86 other events, 685.8 us)
Sparse Core Ops, SparseCore 0:
  11.6 37.4 all-gather.4
  51.3 52.7 all-gather.6
  134.6 54.0 reduce-scatter.2
  191.4 34.9 reduce-scatter.4

commit v5 on v4

--- a/solution.py
+++ b/solution.py
@@ -511,10 +511,12 @@
     gains_ref[...] = gains
 
 
-def ff_out_kernel(n_rep, unit, pitch, scr, in_ref, down_ref, down_scr):
-    _, high, lanes = scr.shape
+def ff_out_kernel(n_rep, unit, pitch, cuts, at_ref, pieces, in_ref, down_ref, scr, down_scr):
+    lanes = pieces[0].shape[1]
     rows = in_ref.shape[0]
     shard, dim = down_ref.shape
+    for (m, top), piece in zip(cuts, pieces, strict=True):
+        scr[at_ref[0] ^ m, top : top + piece.shape[0], :] = piece[...]
     _, spots = packed_rows(pitch, dim, lanes)
     strips = []
     for jj in range(n_rep):
@@ -587,6 +589,13 @@
 
     def rep_gather(x):
         return [x] + [rep_swap(x, m) for m in range(1, n_rep)]
+
+    def rep_spread(x):
+        if n_rep != 4:
+            return [[piece] for piece in rep_gather(x)]
+        half = x.shape[0] // 2
+        near = [rep_swap(x, 1), rep_swap(x, 2)]
+        return [[x], [near[0]], [near[1]], [rep_swap(near[0][:half], 2), rep_swap(near[1][half:], 1)]]
 
     def rep_trade(pieces):
         return [pieces[0]] + [rep_swap(pieces[m], m) for m in range(1, n_rep)]
@@ -703,10 +712,10 @@
     dr, dz = call(
         grouped(middle_kernel, (n_rep,), (n_rep,) + (None,) * 5),
         [((rows, dim), F32), ((rows, dim), BF16)],
-        [*das, r_own, c_own, gains, ff_grad],
+        [*das, r_own, c_own, gains, lo[0]],
         n_any=1, micros=2,
     )
-    ff_grad = lax.psum_scatter(after(ff_grad, *das[1:]), "inner", scatter_dimension=0)
+    ff_grad = lax.psum_scatter(after(ff_grad, das[1]), "inner", scatter_dimension=0)
     dzs = rep_gather(dz)
 
     back = call(
@@ -748,7 +757,6 @@
         grouped(part_sum_kernel, (), (None, part - 1, None)), [((n_rep * high, lanes), BF16)], [keep, *gots]
     )
     das = rep_trade(da_one)
-    ff_grad = after(ff_grad, *das[1:])
     d_pack = lax.psum_scatter(
         after(summed, ff_grad), "inner", scatter_dimension=0, axis_index_groups=planes, tiled=True
     )
@@ -756,8 +764,7 @@
         grouped(last_kernel, (n_rep,), (None, n_rep, n_rep, None, None, None, None, n_rep, None)),
         home, [at, *das, *los, xs[0], dr, r_own, gains], [((rows, dim), F32)], n_smem=1, whole=True, micros=2,
     )
-    ff_grads = jnp.concatenate([ff_grad] * n_rep, axis=0)
-    ff_grads = lax.all_to_all(ff_grads, "rep", 0, 0, tiled=True).reshape(n_rep, ff_high, 2 * ff)
+    ff_grads = rep_spread(after(ff_grad, *das[1:]))
     back_home = send_home(parts)
     quarter = after(d_pack, *back_home)
     input_grad, layer_out = call(
@@ -770,12 +777,19 @@
         [at, *rep_gather(quarter)],
         n_smem=1, micros=2,
     )
+    cuts, flat = [], []
+    for m, pieces in enumerate(ff_grads):
+        top = 0
+        for piece in pieces:
+            cuts.append((m, top))
+            flat.append(piece)
+            top += piece.shape[0]
     g_in, g_down = call(
-        grouped(ff_out_kernel, (n_rep, unit, pitch), (None,) * 4),
+        grouped(ff_out_kernel, (n_rep, unit, pitch, cuts), (None, len(flat)) + (None,) * 4),
         [((w_rows, 2 * n_inner * ff_shard), F32), ((ff_shard, dim), F32)],
-        [ff_grads, d_pack],
-        [((pitch, dim), F32)],
-        n_any=1, micros=4,
+        [at, *flat, d_pack],
+        [((n_rep, ff_high, 2 * ff), BF16), ((pitch, dim), F32)],
+        n_smem=1, n_any=1, micros=4,
     )
     gain_grads = g_gains[: 2 * dim // lanes].reshape(2, dim)
     gain_grads = lax.dynamic_slice_in_dim(gain_grads, i * w_rows, w_rows, 1)

time: 256 us -> 254 us (level)
  local copies, waits for them, and re-layouts: 17.9 us -> 7.88 us
  starting transfers between devices: 55.5 us -> 65.2 us
  other arithmetic: 6.64 us -> 3.19 us
    ppermute x4, waiting for transfers between devices: 17.9 us -> 6.74 us  [send_home(): got.append(lax.ppermute(pieces[k], ('rep', 'inner'), pairs))]
    unnamed x136 -> x124, local copies, waits for them, and re-layouts: 16.4 us -> 6.31 us
    ppermute x27 -> x31, waiting for transfers between devices: 43.6 us -> 51.8 us  [rep_swap(): return lax.ppermute(x, 'rep', [(a, a ^ m) for a in range(n_rep)])]
    ppermute x27 -> x31, starting transfers between devices: 34.1 us -> 41.8 us  [rep_swap(): return lax.ppermute(x, 'rep', [(a, a ^ m) for a in range(n_rep)])]
    ppermute x4, starting transfers between devices: 8.52 us -> 14.1 us  [send_home(): got.append(lax.ppermute(pieces[k], ('rep', 'inner'), pairs))]
    all_to_all x1 -> x0, starting transfers between devices: 3.66 us -> none  [on_device(): lax.all_to_all(ff_grads, 'rep', 0, 0, tiled=True)]
    concatenate x1 -> x0, other arithmetic: 3.34 us -> none  [on_device(): ff_grads = jnp.concatenate([ff_grad] * n_rep, axis=0)]
  transfers between devices with their start and end apart: 42 -> 45, of which waited for: 25 -> 23; matrix products, arithmetic and copies ran while one was open for 3% -> 1% of each run, Pallas kernels for 17% -> 18%
where the time goes in v5:
time: 254 us
  waiting for transfers between devices  80.3 us (32%)
  starting transfers between devices  65.2 us (26%)
  Pallas kernels  62.9 us (25%)
  blocking collectives  19.6 us (8%)
  between operations  14.5 us (6%)
  local copies, waits for them, and re-layouts  7.88 us (3%)
  other arithmetic  3.19 us (1%)
    pallas_call x15, Pallas kernels, call(): pl.pallas_call(without_waited, out_shape=[jax.ShapeDtypeStruct(s, d) for...  62.9 us
    ppermute x31, waiting for transfers between devices, rep_swap(): return lax.ppermute(x, 'rep', [(a, a ^ m) for a in range(n_rep)])  51.8 us
    ppermute x31, starting transfers between devices, rep_swap(): return lax.ppermute(x, 'rep', [(a, a ^ m) for a in range(n_rep)])  41.8 us
    ppermute x4, starting transfers between devices, send_home(): got.append(lax.ppermute(pieces[k], ('rep', 'inner'), pairs))  14.1 us
    all_to_all x1, waiting for transfers between devices, on_device(): lax.all_to_all(x_first, 'inner', 0, 0, axis_index_groups=planes, tiled=True)  11.4 us
    all_to_all x1, blocking collectives, on_device(): x_first = lax.all_to_all(after(tokens, w_pack), 'rep', 0, 0, tiled=True)  10.8 us
    all_to_all x1, blocking collectives, on_device(): c_first = lax.all_to_all(after(cotangent, x_first), 'rep', 0, 0, tiled=True)  8.78 us
    ppermute x4, waiting for transfers between devices, send_home(): got.append(lax.ppermute(pieces[k], ('rep', 'inner'), pairs))  6.74 us
  transfers between devices with their start and end apart: 45, of which 23 were waited for; matrix products, arithmetic and copies ran while one was open for 1% of the time, Pallas kernels for 18%

profile of v5, /device:TPU:0, one launch (start us, length us, event | category | flops | bytes accessed | tf_op | source)
XLA Modules:
  0.0 253.6 jit_solution(9487471574532155610)
XLA Ops:
  11.5 10.8 %all_to_all.44 = bf16[4,32,1024]{2,1,0:T(8,128)(2,1)} all-to-all(bf16[4,32,1024]{2,1,0:T(8,128)(2,1)S(1)} %bitcast.50), channel_id=1, replica_groups=mesh['rep'=4,'inner'=8] {'rep'}, dimensions={0} | all-to-all | bytes 524288 | tf_op jit(solution)/shard_map/all_to_all | solution.py:625
  24.0 8.8 %all_to_all.45 = bf16[4,32,1024]{2,1,0:T(8,128)(2,1)} all-to-all(bf16[4,32,1024]{2,1,0:T(8,128)(2,1)S(1)} %bitcast.51), channel_id=1, replica_groups=mesh['rep'=4,'inner'=8] {'rep'}, dimensions={0} | all-to-all | bytes 524288 | tf_op jit(solution)/shard_map/all_to_all | solution.py:628
  32.8 4.9 %all-to-all-start.1 = ((bf16[4,32,1024]{2,1,0:T(8,128)(2,1)}), bf16[4,32,1024]{2,1,0:T(8,128)(2,1)S(1)}, u32[]{:S(2)}, u32[]{:S(2)}) async-start(bf16[4,32,1024]{2,1,0:T(8,128)(2,1)} %all_to_all.44), calls=%async_computation.1 | async-start | bytes 524288 | tf_op jit(solution)/shard_map/all_to_all | solution.py:627
  37.7 11.4 %all-to-all-done.1 = bf16[4,32,1024]{2,1,0:T(8,128)(2,1)S(1)} async-done(((bf16[4,32,1024]{2,1,0:T(8,128)(2,1)}), bf16[4,32,1024]{2,1,0:T(8,128)(2,1)S(1)}, u32[]{:S(2)}, u32[]{:S(2)}) %all-to-all-start.1) | async-done | bytes 262176 | tf_op jit(solution)/shard_map/all_to_all | solution.py:627
  52.6 3.4 %all-to-all-start.3 = ((bf16[4,32,1024]{2,1,0:T(8,128)(2,1)}), bf16[4,32,1024]{2,1,0:T(8,128)(2,1)S(1)}, u32[]{:S(2)}, u32[]{:S(2)}) async-start(bf16[4,32,1024]{2,1,0:T(8,128)(2,1)} %bitcast.11), calls=%async_computation.3 | async-start | bytes 524288 | tf_op jit(solution)/shard_map/all_to_all | solution.py:630
  66.8 6.4 %shard_map.144 = (bf16[512,256]{1,0:T(8,128)(2,1)}, bf16[512,512]{1,0:T(8,128)(2,1)}, bf16[512,1024]{1,0:T(8,128)(2,1)}, bf16[8,128,768]{2,1,0:T(8,128)(2,1)}, f32[2,1024]{1,0:T(2,128)}) custom-call(s32[3]{0:T(128)} %copy-done.10, bf16[128,1024]{1,0:T(8,128)(2,1)} %bitcast.32, bf16[128,1024]{1,0:T(8,128)(2,1)} %copy-done.25, bf16[128,1024]{1,0:T(8,128)(2,1)} %copy-done.23, ...), custom_call_target="tpu_custom_call" | custom-call | flops 2000000000 | bytes 2000000 | tf_op jit(solution)/shard_map/pallas_call | solution.py:44
  78.6 6.2 %shard_map.145 = (bf16[512,256]{1,0:T(8,128)(2,1)S(1)}, f32[8,512]{1,0:T(8,128)S(1)}) custom-call(bf16[512,256]{1,0:T(8,128)(2,1)S(1)} %copy-done.34, bf16[512,512]{1,0:T(8,128)(2,1)S(1)} %copy-done.17, bf16[512,512]{1,0:T(8,128)(2,1)S(1)} %collective-permute-done.3.refs_2_.refs_9_, bf16[4,128,256]{2,1,0:T(8,128)(2,1)S(1)} %collective-permute-done.4.refs_3_.refs_10_, ...), custom_call_target="tpu_custom_call" | custom-call | flops 6000000000 | bytes 6000000 | tf_op jit(solution)/shard_map/pallas_call | solution.py:44
  92.2 4.2 %collective-permute-done.9.refs_8_ = bf16[512,256]{1,0:T(8,128)(2,1)S(1)} collective-permute-done((bf16[512,256]{1,0:T(8,128)(2,1)S(1)}, bf16[512,256]{1,0:T(8,128)(2,1)S(1)}, u32[]{:S(2)}, u32[]{:S(2)}) %collective-permute-start.9) | collective-permute-done | bytes 262176 | tf_op jit(solution)/shard_map/ppermute | solution.py:580
  96.4 5.1 %collective-permute-done.8.refs_7_ = bf16[512,256]{1,0:T(8,128)(2,1)S(1)} collective-permute-done((bf16[512,256]{1,0:T(8,128)(2,1)S(1)}, bf16[512,256]{1,0:T(8,128)(2,1)S(1)}, u32[]{:S(2)}, u32[]{:S(2)}) %collective-permute-start.8) | collective-permute-done | bytes 262176 | tf_op jit(solution)/shard_map/ppermute | solution.py:580
  104.0 14.9 %shard_map.147 = (f32[128,1024]{1,0:T(8,128)}, bf16[128,1024]{1,0:T(8,128)(2,1)}, bf16[128,1024]{1,0:T(8,128)(2,1)}, bf16[128,1024]{1,0:T(8,128)(2,1)}, bf16[128...) custom-call(s32[3]{0:T(128)} %copy-done.10, ...), custom_call_target="tpu_custom_call" | custom-call | flops 11000000512 | bytes 11000000 | tf_op jit(solution)/shard_map/pallas_call | solution.py:44
  120.6 7.2 %shard_map.148 = (bf16[128,1024]{1,0:T(8,128)(2,1)}, bf16[128,1024]{1,0:T(8,128)(2,1)}, bf16[128,1024]{1,0:T(8,128)(2,1)}, bf16[128,1024]{1,0:T(8,128)(2,1)}, bf16[8,192,1536]{2,1,0:T(8,128)(2,1)}) custom-call(s32[3]{0:T(128)} %copy-done.10, bf16[512,768]{1,0:T(8,128)(2,1)} %get-tuple-element.86.refs_1_, bf16[8,192,1536]{2,1,0:T(8,128)(2,1)} %bitcast.55, ...), custom_call_target="tpu_custom_call" | custom-call | flops 5000000000 | bytes 5000000 | tf_op jit(solution)/shard_map/pallas_call | solution.py:44
  131.7 10.9 %collective-permute-done.15.refs_2_ = bf16[128,1024]{1,0:T(8,128)(2,1)S(1)} collective-permute-done((bf16[128,1024]{1,0:T(8,128)(2,1)S(1)}, bf16[128,1024]{1,0:T(8,128)(2,1)S(1)}, u32[]{:S(2)}, u32[]{:S(2)}) %collective-permute-start.15) | collective-permute-done | bytes 262176 | tf_op jit(solution)/shard_map/ppermute | solution.py:580
  147.5 6.7 %collective-permute-done.19.refs_4_ = bf16[128,1024]{1,0:T(8,128)(2,1)S(1)} collective-permute-done((bf16[128,1024]{1,0:T(8,128)(2,1)S(1)}, bf16[128,1024]{1,0:T(8,128)(2,1)S(1)}, u32[]{:S(2)}, u32[]{:S(2)}) %collective-permute-start.19) | collective-permute-done | bytes 262176 | tf_op jit(solution)/shard_map/ppermute | solution.py:580
  159.7 7.1 %shard_map.150 = (bf16[512,256]{1,0:T(8,128)(2,1)S(1)}, f32[512,512]{1,0:T(8,128)S(1)}, bf16[512,512]{1,0:T(8,128)(2,1)S(1)}, bf16[512,1024]{1,0:T(8,128)(2,1)S(1)}) custom-call(s32[3]{0:T(128)S(1)} %copy-done.11, bf16[128,1024]{1,0:T(8,128)(2,1)S(1)} %get-tuple-element.90.refs_1_, bf16[128,1024]{1,0:T(8,128)(2,1)S(1)} %collective-permute-done.17.refs_2_, ...), custom_call_target="tpu_custom_call" | custom-call | flops 10000000000 | bytes 10000000 | tf_op jit(solution)/shard_map/pallas_call | solution.py:44
  171.3 3.6 %shard_map.152 = (bf16[544,1024]{1,0:T(8,128)(2,1)S(1)}, bf16[544,1024]{1,0:T(8,128)(2,1)S(1)}, bf16[128,1024]{1,0:T(8,128)(2,1)S(1)}, bf16[128,1024]{1,0:T(8,12...) custom-call(s32[3]{0:T(128)S(1)} %copy-done.11, ...), custom_call_target="tpu_custom_call" | custom-call | flops 4000000000 | bytes 4000000 | tf_op jit(solution)/shard_map/pallas_call | solution.py:44
  179.8 3.5 %reduce-scatter.3.cloned.1.call-done = bf16[1,192,1536]{2,1,0:T(8,128)(2,1)} async-done(((bf16[8,192,1536]{2,1,0:T(8,128)(2,1)}), bf16[1,192,1536]{2,1,0:T(8,128)(2,1)}) %reduce-scatter.3.cloned.1.call-update) | async-done | bytes 589840 | tf_op jit(solution)/shard_map/reduce_scatter | solution.py:718
  186.9 5.2 %collective-permute-done.24.refs_2_ = bf16[128,1024]{1,0:T(8,128)(2,1)S(1)} collective-permute-done((bf16[128,1024]{1,0:T(8,128)(2,1)S(1)}, bf16[128,1024]{1,0:T(8,128)(2,1)S(1)}, u32[]{:S(2)}, u32[]{:S(2)}) %collective-permute-start.24) | collective-permute-done | bytes 262176 | tf_op jit(solution)/shard_map/ppermute | solution.py:580
  192.1 4.1 %collective-permute-done.25.refs_3_ = bf16[128,1024]{1,0:T(8,128)(2,1)S(1)} collective-permute-done((bf16[128,1024]{1,0:T(8,128)(2,1)S(1)}, bf16[128,1024]{1,0:T(8,128)(2,1)S(1)}, u32[]{:S(2)}, u32[]{:S(2)}) %collective-permute-start.25) | collective-permute-done | bytes 262176 | tf_op jit(solution)/shard_map/ppermute | solution.py:580
  198.7 3.5 %shard_map.153 = (bf16[64,1024]{1,0:T(8,128)(2,1)}, bf16[64,1024]{1,0:T(8,128)(2,1)}, bf16[64,1024]{1,0:T(8,128)(2,1)}, bf16[64,1024]{1,0:T(8,128)(2,1)}) custom-call(s32[3]{0:T(128)} %copy-done.10, bf16[128,1024]{1,0:T(8,128)(2,1)} %copy-done.36, bf16[128,1024]{1,0:T(8,128)(2,1)} %copy-done.58, bf16[128,1024]{1,0:T(8,128)(2,1)} %copy-done.59, ...), custom_call_target="tpu_custom_call" | custom-call | flops 2000000000 | bytes 2000000 | tf_op jit(solution)/shard_map/pallas_call | solution.py:44
  203.8 4.9 %collective-permute-done.36.refs_3_ = bf16[192,1536]{1,0:T(8,128)(2,1)S(1)} collective-permute-done((bf16[192,1536]{1,0:T(8,128)(2,1)}, bf16[192,1536]{1,0:T(8,128)(2,1)S(1)}, u32[]{:S(2)}, u32[]{:S(2)}) %collective-permute-start.36) | collective-permute-done | bytes 589856 | tf_op jit(solution)/shard_map/ppermute | solution.py:580
  212.3 9.7 %collective-permute-start.28 = (bf16[64,1024]{1,0:T(8,128)(2,1)}, bf16[64,1024]{1,0:T(8,128)(2,1)S(1)}, u32[]{:S(2)}, u32[]{:S(2)}) collective-permute-start(bf16[64,1024]{1,0:T(8,128)(2,1)} %get-tuple-element.115), channel_id=1, source_target_pairs={{0,2},{1,3},{2,10},{3,11},{4,18},{5,19},{6,26},{7,27},{8,0},{9,1},... | collective-permute-start | bytes 393224 | tf_op jit(solution)/shard_map/ppermute | solution.py:614
  227.8 3.9 %collective-permute-done.30.refs_4_ = bf16[64,1024]{1,0:T(8,128)(2,1)S(1)} collective-permute-done((bf16[64,1024]{1,0:T(8,128)(2,1)}, bf16[64,1024]{1,0:T(8,128)(2,1)S(1)}, u32[]{:S(2)}, u32[]{:S(2)}) %collective-permute-start.30) | collective-permute-done | bytes 131104 | tf_op jit(solution)/shard_map/ppermute | solution.py:614
  233.0 4.4 %collective-permute-start.33 = (bf16[136,1024]{1,0:T(8,128)(2,1)}, bf16[136,1024]{1,0:T(8,128)(2,1)S(1)}, u32[]{:S(2)}, u32[]{:S(2)}) collective-permute-start(bf16[136,1024]{1,0:T(8,128)(2,1)} %reduce-scatter.5.cloned.1.call-done.refs_5_.refs_1_.refs_6_), channel_id=1, source_target_pairs={{0,16},{8,24},{16,0},{24,8},{1,17},{9,25},{17,1},{25,9},{2,18},{10... | collective-permute-start | bytes 835592 | tf_op jit(solution)/shard_map/ppermute | solution.py:580
  239.8 4.7 %shard_map.157 = (f32[128,5248]{1,0:T(8,128)}, f32[328,1024]{1,0:T(8,128)}) custom-call(s32[3]{0:T(128)S(1)} %copy-done.12, bf16[192,1536]{1,0:T(8,128)(2,1)S(1)} %bitcast.48, bf16[192,1536]{1,0:T(8,128)(2,1)S(1)} %collective-permute-done.35.refs_2_, bf16[192,1536]{1,0:T(8,128)(2,1)S(1)} %collective-permute-done.36.refs_3_, ...), custom_call_target="tpu_custom_call" | custom-call | flops 4000000000 | bytes 4000000 | tf_op jit(solution)/shard_map/pallas_call | solution.py:44
  (224 shorter events, 83.6 us)
Async XLA Ops:
  7.2 51.2 %all-gather.5.cloned.1.call-start = ((), (), s32[]{:S(2)}) async-start(), calls=%async_computation.8 | async-start | bytes 2506752 | tf_op jit(solution)/shard_map/all_gather | solution.py:624
  11.4 92.6 %all-gather.7.cloned.1.call-start = ((), (), s32[]{:S(2)}) async-start(), calls=%async_computation.9 | async-start | bytes 5308416 | tf_op jit(solution)/shard_map/all_gather | solution.py:639
  32.8 16.3 %all-to-all-start.1 = ((bf16[4,32,1024]{2,1,0:T(8,128)(2,1)}), bf16[4,32,1024]{2,1,0:T(8,128)(2,1)S(1)}, u32[]{:S(2)}, u32[]{:S(2)}) async-start(bf16[4,32,1024]{2,1,0:T(8,128)(2,1)} %all_to_all.44), calls=%async_computation.1 | async-start | bytes 524288 | tf_op jit(solution)/shard_map/all_to_all | solution.py:627
  51.5 13.0 %collective-permute-start.1 = (bf16[128,1024]{1,0:T(8,128)(2,1)S(1)}, bf16[128,1024]{1,0:T(8,128)(2,1)S(1)}, u32[]{:S(2)}, u32[]{:S(2)}) collective-permute-start(bf16[128,1024]{1,0:T(8,128)(2,1)S(1)} %bitcast.30), channel_id=1, source_target_pairs={{0,16},{8,24},{16,0},{24,8},{1,17},{9,25},{17,1},{25,9},{2,18},{10... | collective-permute-start | bytes 786440 | tf_op jit(solution)/shard_map/ppermute | solution.py:580
  52.0 12.9 %collective-permute-start = (bf16[128,1024]{1,0:T(8,128)(2,1)S(1)}, bf16[128,1024]{1,0:T(8,128)(2,1)S(1)}, u32[]{:S(2)}, u32[]{:S(2)}) collective-permute-start(bf16[128,1024]{1,0:T(8,128)(2,1)S(1)} %bitcast.31), channel_id=1, source_target_pairs={{0,8},{8,0},{16,24},{24,16},{1,9},{9,1},{17,25},{25,17},{2,10},{10... | collective-permute-start | bytes 786440 | tf_op jit(solution)/shard_map/ppermute | solution.py:580
  52.6 13.5 %all-to-all-start.3 = ((bf16[4,32,1024]{2,1,0:T(8,128)(2,1)}), bf16[4,32,1024]{2,1,0:T(8,128)(2,1)S(1)}, u32[]{:S(2)}, u32[]{:S(2)}) async-start(bf16[4,32,1024]{2,1,0:T(8,128)(2,1)} %bitcast.11), calls=%async_computation.3 | async-start | bytes 524288 | tf_op jit(solution)/shard_map/all_to_all | solution.py:630
  56.0 127.3 %reduce-scatter.3.cloned.1.call-start = ((), (), s32[]{:S(2)}) async-start(), calls=%async_computation.6 | async-start | bytes 5308416 | tf_op jit(solution)/shard_map/reduce_scatter | solution.py:718
  59.4 13.9 %collective-permute-start.6 = (bf16[4,128,256]{2,1,0:T(8,128)(2,1)S(1)}, bf16[4,128,256]{2,1,0:T(8,128)(2,1)S(1)}, u32[]{:S(2)}, u32[]{:S(2)}) collective-permute-start(bf16[4,128,256]{2,1,0:T(8,128)(2,1)S(1)} %dynamic-slice_bitcast_fusion.refs_9_), channel_id=1, source_target_pairs={{0,24},{8,16},{16,8},{24,0},{1,25},{9,17},{17,9},{25,1},{2,26},{10... | collective-permute-start | bytes 786440 | tf_op jit(solution)/shard_map/ppermute | solution.py:580
  74.9 26.6 %collective-permute-start.10 = (bf16[4,4,128,256]{3,2,1,0:T(8,128)(2,1)S(1)}, bf16[4,4,128,256]{3,2,1,0:T(8,128)(2,1)S(1)}, u32[]{:S(2)}, u32[]{:S(2)}) collective-permute-start(bf16[4,4,128,256]{3,2,1,0:T(8,128)(2,1)S(1)} %pad_maximum_fusion), channel_id=1, source_target_pairs={{0,1},{1,0},{2,3},{3,2},{4,5},{5,4},{6,7},{7,6},{8,9},{9,8},{10,11... | collective-permute-start | bytes 3145736 | tf_op jit(solution)/shard_map/ppermute | solution.py:588
  75.0 12.8 %collective-permute-start.13 = (bf16[128,1024]{1,0:T(8,128)(2,1)S(1)}, bf16[128,1024]{1,0:T(8,128)(2,1)S(1)}, u32[]{:S(2)}, u32[]{:S(2)}) collective-permute-start(bf16[128,1024]{1,0:T(8,128)(2,1)S(1)} %bitcast.39), channel_id=1, source_target_pairs={{0,24},{8,16},{16,8},{24,0},{1,25},{9,17},{17,9},{25,1},{2,26},{10... | collective-permute-start | bytes 786440 | tf_op jit(solution)/shard_map/ppermute | solution.py:580
  78.0 12.8 %collective-permute-start.12 = (bf16[128,1024]{1,0:T(8,128)(2,1)S(1)}, bf16[128,1024]{1,0:T(8,128)(2,1)S(1)}, u32[]{:S(2)}, u32[]{:S(2)}) collective-permute-start(bf16[128,1024]{1,0:T(8,128)(2,1)S(1)} %bitcast.40), channel_id=1, source_target_pairs={{0,16},{8,24},{16,0},{24,8},{1,17},{9,25},{17,1},{25,9},{2,18},{10... | collective-permute-start | bytes 786440 | tf_op jit(solution)/shard_map/ppermute | solution.py:580
  78.0 14.2 %collective-permute-start.11 = (bf16[128,1024]{1,0:T(8,128)(2,1)S(1)}, bf16[128,1024]{1,0:T(8,128)(2,1)S(1)}, u32[]{:S(2)}, u32[]{:S(2)}) collective-permute-start(bf16[128,1024]{1,0:T(8,128)(2,1)S(1)} %bitcast.41), channel_id=1, source_target_pairs={{0,8},{8,0},{16,24},{24,16},{1,9},{9,1},{17,25},{25,17},{2,10},{10... | collective-permute-start | bytes 786440 | tf_op jit(solution)/shard_map/ppermute | solution.py:580
  87.8 13.6 %collective-permute-start.8 = (bf16[512,256]{1,0:T(8,128)(2,1)S(1)}, bf16[512,256]{1,0:T(8,128)(2,1)S(1)}, u32[]{:S(2)}, u32[]{:S(2)}) collective-permute-start(bf16[512,256]{1,0:T(8,128)(2,1)S(1)} %get-tuple-element.77.refs_5_.refs_6_), channel_id=1, source_target_pairs={{0,16},{8,24},{16,0},{24,8},{1,17},{9,25},{17,1},{25,9},{2,18},{10... | collective-permute-start | bytes 786440 | tf_op jit(solution)/shard_map/ppermute | solution.py:580
  127.9 103.7 %reduce-scatter.5.cloned.1.call-start = ((), (), s32[]{:S(2)}) async-start(), calls=%async_computation.7 | async-start | bytes 1392640 | tf_op jit(solution)/shard_map/reduce_scatter | solution.py:760
  128.7 13.8 %collective-permute-start.15 = (bf16[128,1024]{1,0:T(8,128)(2,1)S(1)}, bf16[128,1024]{1,0:T(8,128)(2,1)S(1)}, u32[]{:S(2)}, u32[]{:S(2)}) collective-permute-start(bf16[128,1024]{1,0:T(8,128)(2,1)S(1)} %copy-done.55), channel_id=1, source_target_pairs={{0,16},{8,24},{16,0},{24,8},{1,17},{9,25},{17,1},{25,9},{2,18},{10... | collective-permute-start | bytes 786440 | tf_op jit(solution)/shard_map/ppermute | solution.py:580
  146.3 13.3 %collective-permute-start.17 = (bf16[128,1024]{1,0:T(8,128)(2,1)S(1)}, bf16[128,1024]{1,0:T(8,128)(2,1)S(1)}, u32[]{:S(2)}, u32[]{:S(2)}) collective-permute-start(bf16[128,1024]{1,0:T(8,128)(2,1)S(1)} %get-tuple-element.90.refs_1_), channel_id=1, source_target_pairs={{0,8},{8,0},{16,24},{24,16},{1,9},{9,1},{17,25},{25,17},{2,10},{10... | collective-permute-start | bytes 786440 | tf_op jit(solution)/shard_map/ppermute | solution.py:580
  154.1 12.7 %collective-permute-start.20 = (bf16[128,1024]{1,0:T(8,128)(2,1)S(1)}, bf16[128,1024]{1,0:T(8,128)(2,1)S(1)}, u32[]{:S(2)}, u32[]{:S(2)}) collective-permute-start(bf16[128,1024]{1,0:T(8,128)(2,1)S(1)} %copy-done.50), channel_id=1, source_target_pairs={{0,8},{8,0},{16,24},{24,16},{1,9},{9,1},{17,25},{25,17},{2,10},{10... | collective-permute-start | bytes 786440 | tf_op jit(solution)/shard_map/ppermute | solution.py:580
  156.4 12.8 %collective-permute-start.22 = (bf16[128,1024]{1,0:T(8,128)(2,1)S(1)}, bf16[128,1024]{1,0:T(8,128)(2,1)S(1)}, u32[]{:S(2)}, u32[]{:S(2)}) collective-permute-start(bf16[128,1024]{1,0:T(8,128)(2,1)S(1)} %copy-done.48), channel_id=1, source_target_pairs={{0,24},{8,16},{16,8},{24,0},{1,25},{9,17},{17,9},{25,1},{2,26},{10... | collective-permute-start | bytes 786440 | tf_op jit(solution)/shard_map/ppermute | solution.py:580
  196.2 12.5 %collective-permute-start.36 = (bf16[192,1536]{1,0:T(8,128)(2,1)}, bf16[192,1536]{1,0:T(8,128)(2,1)S(1)}, u32[]{:S(2)}, u32[]{:S(2)}) collective-permute-start(bf16[192,1536]{1,0:T(8,128)(2,1)} %bitcast.46), channel_id=1, source_target_pairs={{0,16},{8,24},{16,0},{24,8},{1,17},{9,25},{17,1},{25,9},{2,18},{10... | collective-permute-start | bytes 1769480 | tf_op jit(solution)/shard_map/ppermute | solution.py:580
  202.3 22.5 %collective-permute-start.27 = (bf16[64,1024]{1,0:T(8,128)(2,1)}, bf16[64,1024]{1,0:T(8,128)(2,1)S(1)}, u32[]{:S(2)}, u32[]{:S(2)}) collective-permute-start(bf16[64,1024]{1,0:T(8,128)(2,1)} %get-tuple-element.114), channel_id=1, source_target_pairs={{0,0},{1,1},{2,8},{3,9},{4,16},{5,17},{6,24},{7,25},{8,2},{9,3},{1... | collective-permute-start | bytes 393224 | tf_op jit(solution)/shard_map/ppermute | solution.py:614
  208.8 31.0 %collective-permute-start.38 = (bf16[96,1536]{1,0:T(8,128)(2,1)S(1)}, bf16[96,1536]{1,0:T(8,128)(2,1)S(1)}, u32[]{:S(2)}, u32[]{:S(2)}) collective-permute-start(bf16[96,1536]{1,0:T(8,128)(2,1)S(1)} %slice.25), channel_id=1, source_target_pairs={{0,8},{8,0},{16,24},{24,16},{1,9},{9,1},{17,25},{25,17},{2,10},{10... | collective-permute-start | bytes 884744 | tf_op jit(solution)/shard_map/ppermute | solution.py:580
  210.3 29.5 %collective-permute-start.37 = (bf16[96,1536]{1,0:T(8,128)(2,1)S(1)}, bf16[96,1536]{1,0:T(8,128)(2,1)S(1)}, u32[]{:S(2)}, u32[]{:S(2)}) collective-permute-start(bf16[96,1536]{1,0:T(8,128)(2,1)S(1)} %slice.24), channel_id=1, source_target_pairs={{0,16},{8,24},{16,0},{24,8},{1,17},{9,25},{17,1},{25,9},{2,18},{10... | collective-permute-start | bytes 884744 | tf_op jit(solution)/shard_map/ppermute | solution.py:580
  212.3 12.6 %collective-permute-start.28 = (bf16[64,1024]{1,0:T(8,128)(2,1)}, bf16[64,1024]{1,0:T(8,128)(2,1)S(1)}, u32[]{:S(2)}, u32[]{:S(2)}) collective-permute-start(bf16[64,1024]{1,0:T(8,128)(2,1)} %get-tuple-element.115), channel_id=1, source_target_pairs={{0,2},{1,3},{2,10},{3,11},{4,18},{5,19},{6,26},{7,27},{8,0},{9,1},... | collective-permute-start | bytes 393224 | tf_op jit(solution)/shard_map/ppermute | solution.py:614
  231.6 12.9 %collective-permute-start.34 = (bf16[136,1024]{1,0:T(8,128)(2,1)}, bf16[136,1024]{1,0:T(8,128)(2,1)S(1)}, u32[]{:S(2)}, u32[]{:S(2)}) collective-permute-start(bf16[136,1024]{1,0:T(8,128)(2,1)} %reduce-scatter.5.cloned.1.call-done.refs_5_.refs_1_.refs_6_), channel_id=1, source_target_pairs={{0,24},{8,16},{16,8},{24,0},{1,25},{9,17},{17,9},{25,1},{2,26},{10... | collective-permute-start | bytes 835592 | tf_op jit(solution)/shard_map/ppermute | solution.py:580
  (83 other events, 686.4 us)
Sparse Core Ops, SparseCore 0:
  11.5 37.4 all-gather.4
  51.2 52.7 all-gather.6
  128.0 55.2 reduce-scatter.2
  186.1 32.0 reduce-scatter.4

commit v6 on v5

--- a/solution.py
+++ b/solution.py
@@ -766,7 +766,7 @@
     )
     ff_grads = rep_spread(after(ff_grad, *das[1:]))
     back_home = send_home(parts)
-    quarter = after(d_pack, *back_home)
+    quarter = after(d_pack, back_home[1])
     input_grad, layer_out = call(
         grouped(place_kernel, (n_rep,), (None, n_rep, None, None)),
         [((rows, dim), BF16)] * 2, [at, *back_home, d_pack], n_smem=1, n_any=1,

time: 254 us -> 252 us (level)
  starting transfers between devices: 65.2 us -> 62.1 us
    ppermute x4, starting transfers between devices: 14.1 us -> 9.36 us  [send_home(): got.append(lax.ppermute(pieces[k], ('rep', 'inner'), pairs))]
  transfers between devices with their start and end apart: 45 -> 45, of which waited for: 23 -> 22; matrix products, arithmetic and copies ran while one was open for 1% -> 1% of each run, Pallas kernels for 18% -> 18%
where the time goes in v6:
time: 252 us; the launch traced here: 250 us
  waiting for transfers between devices  79.8 us (32%)
  Pallas kernels  62.9 us (25%)
  starting transfers between devices  62.1 us (25%)
  blocking collectives  19.6 us (8%)
  between operations  14.6 us (6%)
  local copies, waits for them, and re-layouts  7.86 us (3%)
  other arithmetic  3.19 us (1%)
    pallas_call x15, Pallas kernels, call(): pl.pallas_call(without_waited, out_shape=[jax.ShapeDtypeStruct(s, d) for...  62.9 us
    ppermute x31, waiting for transfers between devices, rep_swap(): return lax.ppermute(x, 'rep', [(a, a ^ m) for a in range(n_rep)])  51.8 us
    ppermute x31, starting transfers between devices, rep_swap(): return lax.ppermute(x, 'rep', [(a, a ^ m) for a in range(n_rep)])  43.5 us
    all_to_all x1, waiting for transfers between devices, on_device(): lax.all_to_all(x_first, 'inner', 0, 0, axis_index_groups=planes, tiled=True)  11.4 us
    all_to_all x1, blocking collectives, on_device(): x_first = lax.all_to_all(after(tokens, w_pack), 'rep', 0, 0, tiled=True)  10.8 us
    ppermute x4, starting transfers between devices, send_home(): got.append(lax.ppermute(pieces[k], ('rep', 'inner'), pairs))  9.36 us
    all_to_all x1, blocking collectives, on_device(): c_first = lax.all_to_all(after(cotangent, x_first), 'rep', 0, 0, tiled=True)  8.78 us
    unnamed x124, local copies, waits for them, and re-layouts  6.3 us
  transfers between devices with their start and end apart: 45, of which 22 were waited for; matrix products, arithmetic and copies ran while one was open for 1% of the time, Pallas kernels for 18%

profile of v6, /device:TPU:0, one launch (start us, length us, event | category | flops | bytes accessed | tf_op | source)
XLA Modules:
  0.0 250.0 jit_solution(8729980307863442400)
XLA Ops:
  11.5 10.8 %all_to_all.44 = bf16[4,32,1024]{2,1,0:T(8,128)(2,1)} all-to-all(bf16[4,32,1024]{2,1,0:T(8,128)(2,1)S(1)} %bitcast.50), channel_id=1, replica_groups=mesh['rep'=4,'inner'=8] {'rep'}, dimensions={0} | all-to-all | bytes 524288 | tf_op jit(solution)/shard_map/all_to_all | solution.py:625
  24.0 8.8 %all_to_all.45 = bf16[4,32,1024]{2,1,0:T(8,128)(2,1)} all-to-all(bf16[4,32,1024]{2,1,0:T(8,128)(2,1)S(1)} %bitcast.51), channel_id=1, replica_groups=mesh['rep'=4,'inner'=8] {'rep'}, dimensions={0} | all-to-all | bytes 524288 | tf_op jit(solution)/shard_map/all_to_all | solution.py:628
  32.8 4.9 %all-to-all-start.1 = ((bf16[4,32,1024]{2,1,0:T(8,128)(2,1)}), bf16[4,32,1024]{2,1,0:T(8,128)(2,1)S(1)}, u32[]{:S(2)}, u32[]{:S(2)}) async-start(bf16[4,32,1024]{2,1,0:T(8,128)(2,1)} %all_to_all.44), calls=%async_computation.1 | async-start | bytes 524288 | tf_op jit(solution)/shard_map/all_to_all | solution.py:627
  37.7 11.4 %all-to-all-done.1 = bf16[4,32,1024]{2,1,0:T(8,128)(2,1)S(1)} async-done(((bf16[4,32,1024]{2,1,0:T(8,128)(2,1)}), bf16[4,32,1024]{2,1,0:T(8,128)(2,1)S(1)}, u32[]{:S(2)}, u32[]{:S(2)}) %all-to-all-start.1) | async-done | bytes 262176 | tf_op jit(solution)/shard_map/all_to_all | solution.py:627
  66.8 6.4 %shard_map.144 = (bf16[512,256]{1,0:T(8,128)(2,1)}, bf16[512,512]{1,0:T(8,128)(2,1)}, bf16[512,1024]{1,0:T(8,128)(2,1)}, bf16[8,128,768]{2,1,0:T(8,128)(2,1)}, f32[2,1024]{1,0:T(2,128)}) custom-call(s32[3]{0:T(128)} %copy-done.10, bf16[128,1024]{1,0:T(8,128)(2,1)} %bitcast.32, bf16[128,1024]{1,0:T(8,128)(2,1)} %copy-done.25, bf16[128,1024]{1,0:T(8,128)(2,1)} %copy-done.23, ...), custom_call_target="tpu_custom_call" | custom-call | flops 2000000000 | bytes 2000000 | tf_op jit(solution)/shard_map/pallas_call | solution.py:44
  78.6 6.2 %shard_map.145 = (bf16[512,256]{1,0:T(8,128)(2,1)S(1)}, f32[8,512]{1,0:T(8,128)S(1)}) custom-call(bf16[512,256]{1,0:T(8,128)(2,1)S(1)} %copy-done.34, bf16[512,512]{1,0:T(8,128)(2,1)S(1)} %copy-done.17, bf16[512,512]{1,0:T(8,128)(2,1)S(1)} %collective-permute-done.3.refs_2_.refs_9_, bf16[4,128,256]{2,1,0:T(8,128)(2,1)S(1)} %collective-permute-done.4.refs_3_.refs_10_, ...), custom_call_target="tpu_custom_call" | custom-call | flops 6000000000 | bytes 6000000 | tf_op jit(solution)/shard_map/pallas_call | solution.py:44
  92.2 4.2 %collective-permute-done.9.refs_8_ = bf16[512,256]{1,0:T(8,128)(2,1)S(1)} collective-permute-done((bf16[512,256]{1,0:T(8,128)(2,1)S(1)}, bf16[512,256]{1,0:T(8,128)(2,1)S(1)}, u32[]{:S(2)}, u32[]{:S(2)}) %collective-permute-start.9) | collective-permute-done | bytes 262176 | tf_op jit(solution)/shard_map/ppermute | solution.py:580
  96.4 5.1 %collective-permute-done.8.refs_7_ = bf16[512,256]{1,0:T(8,128)(2,1)S(1)} collective-permute-done((bf16[512,256]{1,0:T(8,128)(2,1)S(1)}, bf16[512,256]{1,0:T(8,128)(2,1)S(1)}, u32[]{:S(2)}, u32[]{:S(2)}) %collective-permute-start.8) | collective-permute-done | bytes 262176 | tf_op jit(solution)/shard_map/ppermute | solution.py:580
  104.0 14.9 %shard_map.147 = (f32[128,1024]{1,0:T(8,128)}, bf16[128,1024]{1,0:T(8,128)(2,1)}, bf16[128,1024]{1,0:T(8,128)(2,1)}, bf16[128,1024]{1,0:T(8,128)(2,1)}, bf16[128...) custom-call(s32[3]{0:T(128)} %copy-done.10, ...), custom_call_target="tpu_custom_call" | custom-call | flops 11000000512 | bytes 11000000 | tf_op jit(solution)/shard_map/pallas_call | solution.py:44
  120.6 7.2 %shard_map.148 = (bf16[128,1024]{1,0:T(8,128)(2,1)}, bf16[128,1024]{1,0:T(8,128)(2,1)}, bf16[128,1024]{1,0:T(8,128)(2,1)}, bf16[128,1024]{1,0:T(8,128)(2,1)}, bf16[8,192,1536]{2,1,0:T(8,128)(2,1)}) custom-call(s32[3]{0:T(128)} %copy-done.10, bf16[512,768]{1,0:T(8,128)(2,1)} %get-tuple-element.86.refs_1_, bf16[8,192,1536]{2,1,0:T(8,128)(2,1)} %bitcast.55, ...), custom_call_target="tpu_custom_call" | custom-call | flops 5000000000 | bytes 5000000 | tf_op jit(solution)/shard_map/pallas_call | solution.py:44
  131.7 10.9 %collective-permute-done.15.refs_2_ = bf16[128,1024]{1,0:T(8,128)(2,1)S(1)} collective-permute-done((bf16[128,1024]{1,0:T(8,128)(2,1)S(1)}, bf16[128,1024]{1,0:T(8,128)(2,1)S(1)}, u32[]{:S(2)}, u32[]{:S(2)}) %collective-permute-start.15) | collective-permute-done | bytes 262176 | tf_op jit(solution)/shard_map/ppermute | solution.py:580
  147.5 6.7 %collective-permute-done.19.refs_4_ = bf16[128,1024]{1,0:T(8,128)(2,1)S(1)} collective-permute-done((bf16[128,1024]{1,0:T(8,128)(2,1)S(1)}, bf16[128,1024]{1,0:T(8,128)(2,1)S(1)}, u32[]{:S(2)}, u32[]{:S(2)}) %collective-permute-start.19) | collective-permute-done | bytes 262176 | tf_op jit(solution)/shard_map/ppermute | solution.py:580
  159.7 7.1 %shard_map.150 = (bf16[512,256]{1,0:T(8,128)(2,1)S(1)}, f32[512,512]{1,0:T(8,128)S(1)}, bf16[512,512]{1,0:T(8,128)(2,1)S(1)}, bf16[512,1024]{1,0:T(8,128)(2,1)S(1)}) custom-call(s32[3]{0:T(128)S(1)} %copy-done.11, bf16[128,1024]{1,0:T(8,128)(2,1)S(1)} %get-tuple-element.90.refs_1_, bf16[128,1024]{1,0:T(8,128)(2,1)S(1)} %collective-permute-done.17.refs_2_, ...), custom_call_target="tpu_custom_call" | custom-call | flops 10000000000 | bytes 10000000 | tf_op jit(solution)/shard_map/pallas_call | solution.py:44
  171.3 3.6 %shard_map.152 = (bf16[544,1024]{1,0:T(8,128)(2,1)S(1)}, bf16[544,1024]{1,0:T(8,128)(2,1)S(1)}, bf16[128,1024]{1,0:T(8,128)(2,1)S(1)}, bf16[128,1024]{1,0:T(8,12...) custom-call(s32[3]{0:T(128)S(1)} %copy-done.11, ...), custom_call_target="tpu_custom_call" | custom-call | flops 4000000000 | bytes 4000000 | tf_op jit(solution)/shard_map/pallas_call | solution.py:44
  179.8 3.5 %reduce-scatter.3.cloned.1.call-done = bf16[1,192,1536]{2,1,0:T(8,128)(2,1)} async-done(((bf16[8,192,1536]{2,1,0:T(8,128)(2,1)}), bf16[1,192,1536]{2,1,0:T(8,128)(2,1)}) %reduce-scatter.3.cloned.1.call-update) | async-done | bytes 589840 | tf_op jit(solution)/shard_map/reduce_scatter | solution.py:718
  186.9 5.2 %collective-permute-done.24.refs_2_ = bf16[128,1024]{1,0:T(8,128)(2,1)S(1)} collective-permute-done((bf16[128,1024]{1,0:T(8,128)(2,1)S(1)}, bf16[128,1024]{1,0:T(8,128)(2,1)S(1)}, u32[]{:S(2)}, u32[]{:S(2)}) %collective-permute-start.24) | collective-permute-done | bytes 262176 | tf_op jit(solution)/shard_map/ppermute | solution.py:580
  192.1 4.1 %collective-permute-done.25.refs_3_ = bf16[128,1024]{1,0:T(8,128)(2,1)S(1)} collective-permute-done((bf16[128,1024]{1,0:T(8,128)(2,1)S(1)}, bf16[128,1024]{1,0:T(8,128)(2,1)S(1)}, u32[]{:S(2)}, u32[]{:S(2)}) %collective-permute-start.25) | collective-permute-done | bytes 262176 | tf_op jit(solution)/shard_map/ppermute | solution.py:580
  198.7 3.5 %shard_map.153 = (bf16[64,1024]{1,0:T(8,128)(2,1)}, bf16[64,1024]{1,0:T(8,128)(2,1)}, bf16[64,1024]{1,0:T(8,128)(2,1)}, bf16[64,1024]{1,0:T(8,128)(2,1)}) custom-call(s32[3]{0:T(128)} %copy-done.10, bf16[128,1024]{1,0:T(8,128)(2,1)} %copy-done.36, bf16[128,1024]{1,0:T(8,128)(2,1)} %copy-done.58, bf16[128,1024]{1,0:T(8,128)(2,1)} %copy-done.59, ...), custom_call_target="tpu_custom_call" | custom-call | flops 2000000000 | bytes 2000000 | tf_op jit(solution)/shard_map/pallas_call | solution.py:44
  203.9 4.9 %collective-permute-done.36.refs_3_ = bf16[192,1536]{1,0:T(8,128)(2,1)S(1)} collective-permute-done((bf16[192,1536]{1,0:T(8,128)(2,1)}, bf16[192,1536]{1,0:T(8,128)(2,1)S(1)}, u32[]{:S(2)}, u32[]{:S(2)}) %collective-permute-start.36) | collective-permute-done | bytes 589856 | tf_op jit(solution)/shard_map/ppermute | solution.py:580
  208.8 4.3 %collective-permute-start.38 = (bf16[96,1536]{1,0:T(8,128)(2,1)S(1)}, bf16[96,1536]{1,0:T(8,128)(2,1)S(1)}, u32[]{:S(2)}, u32[]{:S(2)}) collective-permute-start(bf16[96,1536]{1,0:T(8,128)(2,1)S(1)} %slice.25), channel_id=1, source_target_pairs={{0,8},{8,0},{16,24},{24,16},{1,9},{9,1},{17,25},{25,17},{2,10},{10... | collective-permute-start | bytes 884744 | tf_op jit(solution)/shard_map/ppermute | solution.py:580
  217.3 5.2 %collective-permute-start.29 = (bf16[64,1024]{1,0:T(8,128)(2,1)}, bf16[64,1024]{1,0:T(8,128)(2,1)S(1)}, u32[]{:S(2)}, u32[]{:S(2)}) collective-permute-start(bf16[64,1024]{1,0:T(8,128)(2,1)} %get-tuple-element.116), channel_id=1, source_target_pairs={{0,4},{1,5},{2,12},{3,13},{4,20},{5,21},{6,28},{7,29},{8,6},{9,7},... | collective-permute-start | bytes 393224 | tf_op jit(solution)/shard_map/ppermute | solution.py:614
  223.5 4.0 %collective-permute-start.34 = (bf16[136,1024]{1,0:T(8,128)(2,1)}, bf16[136,1024]{1,0:T(8,128)(2,1)S(1)}, u32[]{:S(2)}, u32[]{:S(2)}) collective-permute-start(bf16[136,1024]{1,0:T(8,128)(2,1)} %reduce-scatter.5.cloned.1.call-done.refs_5_.refs_1_.refs_6_), channel_id=1, source_target_pairs={{0,24},{8,16},{16,8},{24,0},{1,25},{9,17},{17,9},{25,1},{2,26},{10... | collective-permute-start | bytes 835592 | tf_op jit(solution)/shard_map/ppermute | solution.py:580
  227.6 6.2 %collective-permute-done.29.refs_3_ = bf16[64,1024]{1,0:T(8,128)(2,1)S(1)} collective-permute-done((bf16[64,1024]{1,0:T(8,128)(2,1)}, bf16[64,1024]{1,0:T(8,128)(2,1)S(1)}, u32[]{:S(2)}, u32[]{:S(2)}) %collective-permute-start.29) | collective-permute-done | bytes 131104 | tf_op jit(solution)/shard_map/ppermute | solution.py:614
  236.2 4.7 %shard_map.157 = (f32[128,5248]{1,0:T(8,128)}, f32[328,1024]{1,0:T(8,128)}) custom-call(s32[3]{0:T(128)S(1)} %copy-done.12, bf16[192,1536]{1,0:T(8,128)(2,1)S(1)} %bitcast.48, bf16[192,1536]{1,0:T(8,128)(2,1)S(1)} %collective-permute-done.35.refs_2_, bf16[192,1536]{1,0:T(8,128)(2,1)S(1)} %collective-permute-done.36.refs_3_, ...), custom_call_target="tpu_custom_call" | custom-call | flops 4000000000 | bytes 4000000 | tf_op jit(solution)/shard_map/pallas_call | solution.py:44
  (224 shorter events, 81.6 us)
Async XLA Ops:
  7.2 51.2 %all-gather.5.cloned.1.call-start = ((), (), s32[]{:S(2)}) async-start(), calls=%async_computation.8 | async-start | bytes 2506752 | tf_op jit(solution)/shard_map/all_gather | solution.py:624
  11.4 92.6 %all-gather.7.cloned.1.call-start = ((), (), s32[]{:S(2)}) async-start(), calls=%async_computation.9 | async-start | bytes 5308416 | tf_op jit(solution)/shard_map/all_gather | solution.py:639
  32.8 16.3 %all-to-all-start.1 = ((bf16[4,32,1024]{2,1,0:T(8,128)(2,1)}), bf16[4,32,1024]{2,1,0:T(8,128)(2,1)S(1)}, u32[]{:S(2)}, u32[]{:S(2)}) async-start(bf16[4,32,1024]{2,1,0:T(8,128)(2,1)} %all_to_all.44), calls=%async_computation.1 | async-start | bytes 524288 | tf_op jit(solution)/shard_map/all_to_all | solution.py:627
  51.5 13.0 %collective-permute-start.1 = (bf16[128,1024]{1,0:T(8,128)(2,1)S(1)}, bf16[128,1024]{1,0:T(8,128)(2,1)S(1)}, u32[]{:S(2)}, u32[]{:S(2)}) collective-permute-start(bf16[128,1024]{1,0:T(8,128)(2,1)S(1)} %bitcast.30), channel_id=1, source_target_pairs={{0,16},{8,24},{16,0},{24,8},{1,17},{9,25},{17,1},{25,9},{2,18},{10... | collective-permute-start | bytes 786440 | tf_op jit(solution)/shard_map/ppermute | solution.py:580
  52.0 12.9 %collective-permute-start = (bf16[128,1024]{1,0:T(8,128)(2,1)S(1)}, bf16[128,1024]{1,0:T(8,128)(2,1)S(1)}, u32[]{:S(2)}, u32[]{:S(2)}) collective-permute-start(bf16[128,1024]{1,0:T(8,128)(2,1)S(1)} %bitcast.31), channel_id=1, source_target_pairs={{0,8},{8,0},{16,24},{24,16},{1,9},{9,1},{17,25},{25,17},{2,10},{10... | collective-permute-start | bytes 786440 | tf_op jit(solution)/shard_map/ppermute | solution.py:580
  52.6 13.5 %all-to-all-start.3 = ((bf16[4,32,1024]{2,1,0:T(8,128)(2,1)}), bf16[4,32,1024]{2,1,0:T(8,128)(2,1)S(1)}, u32[]{:S(2)}, u32[]{:S(2)}) async-start(bf16[4,32,1024]{2,1,0:T(8,128)(2,1)} %bitcast.11), calls=%async_computation.3 | async-start | bytes 524288 | tf_op jit(solution)/shard_map/all_to_all | solution.py:630
  56.0 127.3 %reduce-scatter.3.cloned.1.call-start = ((), (), s32[]{:S(2)}) async-start(), calls=%async_computation.6 | async-start | bytes 5308416 | tf_op jit(solution)/shard_map/reduce_scatter | solution.py:718
  59.4 13.9 %collective-permute-start.6 = (bf16[4,128,256]{2,1,0:T(8,128)(2,1)S(1)}, bf16[4,128,256]{2,1,0:T(8,128)(2,1)S(1)}, u32[]{:S(2)}, u32[]{:S(2)}) collective-permute-start(bf16[4,128,256]{2,1,0:T(8,128)(2,1)S(1)} %dynamic-slice_bitcast_fusion.refs_9_), channel_id=1, source_target_pairs={{0,24},{8,16},{16,8},{24,0},{1,25},{9,17},{17,9},{25,1},{2,26},{10... | collective-permute-start | bytes 786440 | tf_op jit(solution)/shard_map/ppermute | solution.py:580
  74.9 26.6 %collective-permute-start.10 = (bf16[4,4,128,256]{3,2,1,0:T(8,128)(2,1)S(1)}, bf16[4,4,128,256]{3,2,1,0:T(8,128)(2,1)S(1)}, u32[]{:S(2)}, u32[]{:S(2)}) collective-permute-start(bf16[4,4,128,256]{3,2,1,0:T(8,128)(2,1)S(1)} %pad_maximum_fusion), channel_id=1, source_target_pairs={{0,1},{1,0},{2,3},{3,2},{4,5},{5,4},{6,7},{7,6},{8,9},{9,8},{10,11... | collective-permute-start | bytes 3145736 | tf_op jit(solution)/shard_map/ppermute | solution.py:588
  75.0 12.8 %collective-permute-start.13 = (bf16[128,1024]{1,0:T(8,128)(2,1)S(1)}, bf16[128,1024]{1,0:T(8,128)(2,1)S(1)}, u32[]{:S(2)}, u32[]{:S(2)}) collective-permute-start(bf16[128,1024]{1,0:T(8,128)(2,1)S(1)} %bitcast.39), channel_id=1, source_target_pairs={{0,24},{8,16},{16,8},{24,0},{1,25},{9,17},{17,9},{25,1},{2,26},{10... | collective-permute-start | bytes 786440 | tf_op jit(solution)/shard_map/ppermute | solution.py:580
  78.0 12.8 %collective-permute-start.12 = (bf16[128,1024]{1,0:T(8,128)(2,1)S(1)}, bf16[128,1024]{1,0:T(8,128)(2,1)S(1)}, u32[]{:S(2)}, u32[]{:S(2)}) collective-permute-start(bf16[128,1024]{1,0:T(8,128)(2,1)S(1)} %bitcast.40), channel_id=1, source_target_pairs={{0,16},{8,24},{16,0},{24,8},{1,17},{9,25},{17,1},{25,9},{2,18},{10... | collective-permute-start | bytes 786440 | tf_op jit(solution)/shard_map/ppermute | solution.py:580
  78.0 14.2 %collective-permute-start.11 = (bf16[128,1024]{1,0:T(8,128)(2,1)S(1)}, bf16[128,1024]{1,0:T(8,128)(2,1)S(1)}, u32[]{:S(2)}, u32[]{:S(2)}) collective-permute-start(bf16[128,1024]{1,0:T(8,128)(2,1)S(1)} %bitcast.41), channel_id=1, source_target_pairs={{0,8},{8,0},{16,24},{24,16},{1,9},{9,1},{17,25},{25,17},{2,10},{10... | collective-permute-start | bytes 786440 | tf_op jit(solution)/shard_map/ppermute | solution.py:580
  87.8 13.6 %collective-permute-start.8 = (bf16[512,256]{1,0:T(8,128)(2,1)S(1)}, bf16[512,256]{1,0:T(8,128)(2,1)S(1)}, u32[]{:S(2)}, u32[]{:S(2)}) collective-permute-start(bf16[512,256]{1,0:T(8,128)(2,1)S(1)} %get-tuple-element.77.refs_5_.refs_6_), channel_id=1, source_target_pairs={{0,16},{8,24},{16,0},{24,8},{1,17},{9,25},{17,1},{25,9},{2,18},{10... | collective-permute-start | bytes 786440 | tf_op jit(solution)/shard_map/ppermute | solution.py:580
  127.9 95.6 %reduce-scatter.5.cloned.1.call-start = ((), (), s32[]{:S(2)}) async-start(), calls=%async_computation.7 | async-start | bytes 1392640 | tf_op jit(solution)/shard_map/reduce_scatter | solution.py:760
  128.7 13.8 %collective-permute-start.15 = (bf16[128,1024]{1,0:T(8,128)(2,1)S(1)}, bf16[128,1024]{1,0:T(8,128)(2,1)S(1)}, u32[]{:S(2)}, u32[]{:S(2)}) collective-permute-start(bf16[128,1024]{1,0:T(8,128)(2,1)S(1)} %copy-done.55), channel_id=1, source_target_pairs={{0,16},{8,24},{16,0},{24,8},{1,17},{9,25},{17,1},{25,9},{2,18},{10... | collective-permute-start | bytes 786440 | tf_op jit(solution)/shard_map/ppermute | solution.py:580
  146.3 13.3 %collective-permute-start.17 = (bf16[128,1024]{1,0:T(8,128)(2,1)S(1)}, bf16[128,1024]{1,0:T(8,128)(2,1)S(1)}, u32[]{:S(2)}, u32[]{:S(2)}) collective-permute-start(bf16[128,1024]{1,0:T(8,128)(2,1)S(1)} %get-tuple-element.90.refs_1_), channel_id=1, source_target_pairs={{0,8},{8,0},{16,24},{24,16},{1,9},{9,1},{17,25},{25,17},{2,10},{10... | collective-permute-start | bytes 786440 | tf_op jit(solution)/shard_map/ppermute | solution.py:580
  154.1 12.7 %collective-permute-start.20 = (bf16[128,1024]{1,0:T(8,128)(2,1)S(1)}, bf16[128,1024]{1,0:T(8,128)(2,1)S(1)}, u32[]{:S(2)}, u32[]{:S(2)}) collective-permute-start(bf16[128,1024]{1,0:T(8,128)(2,1)S(1)} %copy-done.50), channel_id=1, source_target_pairs={{0,8},{8,0},{16,24},{24,16},{1,9},{9,1},{17,25},{25,17},{2,10},{10... | collective-permute-start | bytes 786440 | tf_op jit(solution)/shard_map/ppermute | solution.py:580
  156.4 12.8 %collective-permute-start.22 = (bf16[128,1024]{1,0:T(8,128)(2,1)S(1)}, bf16[128,1024]{1,0:T(8,128)(2,1)S(1)}, u32[]{:S(2)}, u32[]{:S(2)}) collective-permute-start(bf16[128,1024]{1,0:T(8,128)(2,1)S(1)} %copy-done.48), channel_id=1, source_target_pairs={{0,24},{8,16},{16,8},{24,0},{1,25},{9,17},{17,9},{25,1},{2,26},{10... | collective-permute-start | bytes 786440 | tf_op jit(solution)/shard_map/ppermute | solution.py:580
  198.7 14.5 %collective-permute-start.35 = (bf16[192,1536]{1,0:T(8,128)(2,1)}, bf16[192,1536]{1,0:T(8,128)(2,1)S(1)}, u32[]{:S(2)}, u32[]{:S(2)}) collective-permute-start(bf16[192,1536]{1,0:T(8,128)(2,1)} %bitcast.47), channel_id=1, source_target_pairs={{0,8},{8,0},{16,24},{24,16},{1,9},{9,1},{17,25},{25,17},{2,10},{10... | collective-permute-start | bytes 1769480 | tf_op jit(solution)/shard_map/ppermute | solution.py:580
  202.3 20.2 %collective-permute-start.28 = (bf16[64,1024]{1,0:T(8,128)(2,1)}, bf16[64,1024]{1,0:T(8,128)(2,1)S(1)}, u32[]{:S(2)}, u32[]{:S(2)}) collective-permute-start(bf16[64,1024]{1,0:T(8,128)(2,1)} %get-tuple-element.115), channel_id=1, source_target_pairs={{0,2},{1,3},{2,10},{3,11},{4,18},{5,19},{6,26},{7,27},{8,0},{9,1},... | collective-permute-start | bytes 393224 | tf_op jit(solution)/shard_map/ppermute | solution.py:614
  208.8 27.3 %collective-permute-start.38 = (bf16[96,1536]{1,0:T(8,128)(2,1)S(1)}, bf16[96,1536]{1,0:T(8,128)(2,1)S(1)}, u32[]{:S(2)}, u32[]{:S(2)}) collective-permute-start(bf16[96,1536]{1,0:T(8,128)(2,1)S(1)} %slice.25), channel_id=1, source_target_pairs={{0,8},{8,0},{16,24},{24,16},{1,9},{9,1},{17,25},{25,17},{2,10},{10... | collective-permute-start | bytes 884744 | tf_op jit(solution)/shard_map/ppermute | solution.py:580
  213.2 23.0 %collective-permute-start.37 = (bf16[96,1536]{1,0:T(8,128)(2,1)S(1)}, bf16[96,1536]{1,0:T(8,128)(2,1)S(1)}, u32[]{:S(2)}, u32[]{:S(2)}) collective-permute-start(bf16[96,1536]{1,0:T(8,128)(2,1)S(1)} %slice.24), channel_id=1, source_target_pairs={{0,16},{8,24},{16,0},{24,8},{1,17},{9,25},{17,1},{25,9},{2,18},{10... | collective-permute-start | bytes 884744 | tf_op jit(solution)/shard_map/ppermute | solution.py:580
  217.3 16.4 %collective-permute-start.29 = (bf16[64,1024]{1,0:T(8,128)(2,1)}, bf16[64,1024]{1,0:T(8,128)(2,1)S(1)}, u32[]{:S(2)}, u32[]{:S(2)}) collective-permute-start(bf16[64,1024]{1,0:T(8,128)(2,1)} %get-tuple-element.116), channel_id=1, source_target_pairs={{0,4},{1,5},{2,12},{3,13},{4,20},{5,21},{6,28},{7,29},{8,6},{9,7},... | collective-permute-start | bytes 393224 | tf_op jit(solution)/shard_map/ppermute | solution.py:614
  223.5 17.4 %collective-permute-start.34 = (bf16[136,1024]{1,0:T(8,128)(2,1)}, bf16[136,1024]{1,0:T(8,128)(2,1)S(1)}, u32[]{:S(2)}, u32[]{:S(2)}) collective-permute-start(bf16[136,1024]{1,0:T(8,128)(2,1)} %reduce-scatter.5.cloned.1.call-done.refs_5_.refs_1_.refs_6_), channel_id=1, source_target_pairs={{0,24},{8,16},{16,8},{24,0},{1,25},{9,17},{17,9},{25,1},{2,26},{10... | collective-permute-start | bytes 835592 | tf_op jit(solution)/shard_map/ppermute | solution.py:580
  (83 other events, 683.6 us)
Sparse Core Ops, SparseCore 0:
  11.5 37.4 all-gather.4
  51.2 52.7 all-gather.6
  128.0 55.2 reduce-scatter.2
  186.1 29.3 reduce-scatter.4

commit v7 on v6

--- a/solution.py
+++ b/solution.py
@@ -619,7 +619,7 @@
 
     (w_pack,) = call(
         functools.partial(weight_kernel, n_inner, part), [((high, lanes), BF16)],
-        [at, qkv_weight, out_weight, jnp.stack([gain_one, gain_two])], n_smem=1,
+        [at, qkv_weight, out_weight, jnp.stack([gain_one, gain_two])], n_smem=1, whole=True,
     )
     w_all = lax.all_gather(w_pack, "inner")
     x_first = lax.all_to_all(after(tokens, w_pack), "rep", 0, 0, tiled=True)
@@ -667,9 +667,9 @@
     o, lse = call(
         grouped(attend_kernel, (part,), (None, part) + (None,) * 4),
         [((total, width), BF16), ((stat_rows, total), F32)],
-        [q, *kvs, *wo_own[1:]],
+        [after(q, *wo_own[1:]), *kvs],
         [((total * part, width), BF16), ((width, total * part), BF16)],
-        n_any=n_rep - 1, micros=6,
+        micros=6,
     )
     os_ = rep_gather(o)
     cs = rep_gather(after(c_own, xs[-1]))

time: 252 us -> 252 us (level)
    unnamed x124 -> x122, local copies, waits for them, and re-layouts: 6.3 us -> 5.24 us
  transfers between devices with their start and end apart: 45 -> 45, of which waited for: 22 -> 21; matrix products, arithmetic and copies ran while one was open for 1% -> 1% of each run, Pallas kernels for 18% -> 18%
where the time goes in v7:
time: 252 us; the launch traced here: 250 us
  waiting for transfers between devices  78.9 us (31%)
  Pallas kernels  63.7 us (25%)
  starting transfers between devices  62.1 us (25%)
  blocking collectives  19.6 us (8%)
  between operations  14.5 us (6%)
  local copies, waits for them, and re-layouts  6.8 us (3%)
  other arithmetic  4.22 us (2%)
    pallas_call x15, Pallas kernels, call(): pl.pallas_call(without_waited, out_shape=[jax.ShapeDtypeStruct(s, d) for...  63.7 us
    ppermute x31, waiting for transfers between devices, rep_swap(): return lax.ppermute(x, 'rep', [(a, a ^ m) for a in range(n_rep)])  51.4 us
    ppermute x31, starting transfers between devices, rep_swap(): return lax.ppermute(x, 'rep', [(a, a ^ m) for a in range(n_rep)])  43.5 us
    all_to_all x1, blocking collectives, on_device(): x_first = lax.all_to_all(after(tokens, w_pack), 'rep', 0, 0, tiled=True)  10.8 us
    all_to_all x1, waiting for transfers between devices, on_device(): lax.all_to_all(x_first, 'inner', 0, 0, axis_index_groups=planes, tiled=True)  10.5 us
    ppermute x4, starting transfers between devices, send_home(): got.append(lax.ppermute(pieces[k], ('rep', 'inner'), pairs))  9.38 us
    all_to_all x1, blocking collectives, on_device(): c_first = lax.all_to_all(after(cotangent, x_first), 'rep', 0, 0, tiled=True)  8.78 us
    ppermute x4, waiting for transfers between devices, send_home(): got.append(lax.ppermute(pieces[k], ('rep', 'inner'), pairs))  6.09 us
  transfers between devices with their start and end apart: 45, of which 21 were waited for; matrix products, arithmetic and copies ran while one was open for 1% of the time, Pallas kernels for 18%

profile of v7, /device:TPU:0, one launch (start us, length us, event | category | flops | bytes accessed | tf_op | source)
XLA Modules:
  0.0 249.9 jit_solution(6673805807055309239)
XLA Ops:
  11.2 10.8 %all_to_all.44 = bf16[4,32,1024]{2,1,0:T(8,128)(2,1)} all-to-all(bf16[4,32,1024]{2,1,0:T(8,128)(2,1)S(1)} %bitcast.47), channel_id=1, replica_groups=mesh['rep'=4,'inner'=8] {'rep'}, dimensions={0} | all-to-all | bytes 524288 | tf_op jit(solution)/shard_map/all_to_all | solution.py:625
  24.7 8.8 %all_to_all.45 = bf16[4,32,1024]{2,1,0:T(8,128)(2,1)} all-to-all(bf16[4,32,1024]{2,1,0:T(8,128)(2,1)S(1)} %bitcast.48), channel_id=1, replica_groups=mesh['rep'=4,'inner'=8] {'rep'}, dimensions={0} | all-to-all | bytes 524288 | tf_op jit(solution)/shard_map/all_to_all | solution.py:628
  33.5 4.9 %all-to-all-start.1 = ((bf16[4,32,1024]{2,1,0:T(8,128)(2,1)}), bf16[4,32,1024]{2,1,0:T(8,128)(2,1)S(1)}, u32[]{:S(2)}, u32[]{:S(2)}) async-start(bf16[4,32,1024]{2,1,0:T(8,128)(2,1)} %all_to_all.44), calls=%async_computation.1 | async-start | bytes 524288 | tf_op jit(solution)/shard_map/all_to_all | solution.py:627
  38.4 10.5 %all-to-all-done.1 = bf16[4,32,1024]{2,1,0:T(8,128)(2,1)S(1)} async-done(((bf16[4,32,1024]{2,1,0:T(8,128)(2,1)}), bf16[4,32,1024]{2,1,0:T(8,128)(2,1)S(1)}, u32[]{:S(2)}, u32[]{:S(2)}) %all-to-all-start.1) | async-done | bytes 262176 | tf_op jit(solution)/shard_map/all_to_all | solution.py:627
  67.5 6.4 %shard_map.144 = (bf16[512,256]{1,0:T(8,128)(2,1)}, bf16[512,512]{1,0:T(8,128)(2,1)}, bf16[512,1024]{1,0:T(8,128)(2,1)}, bf16[8,128,768]{2,1,0:T(8,128)(2,1)}, f32[2,1024]{1,0:T(2,128)}) custom-call(s32[3]{0:T(128)} %pad_add_fusion.refs_0_, bf16[128,1024]{1,0:T(8,128)(2,1)} %bitcast.32, bf16[128,1024]{1,0:T(8,128)(2,1)} %copy-done.21, ...), custom_call_target="tpu_custom_call" | custom-call | flops 2000000000 | bytes 2000000 | tf_op jit(solution)/shard_map/pallas_call | solution.py:44
  74.8 3.6 %collective-permute-start.13 = (bf16[128,1024]{1,0:T(8,128)(2,1)S(1)}, bf16[128,1024]{1,0:T(8,128)(2,1)S(1)}, u32[]{:S(2)}, u32[]{:S(2)}) collective-permute-start(bf16[128,1024]{1,0:T(8,128)(2,1)S(1)} %bitcast.39), channel_id=1, source_target_pairs={{0,24},{8,16},{16,8},{24,0},{1,25},{9,17},{17,9},{25,1},{2,26},{10... | collective-permute-start | bytes 786440 | tf_op jit(solution)/shard_map/ppermute | solution.py:580
  79.1 6.2 %shard_map.145 = (bf16[512,256]{1,0:T(8,128)(2,1)S(1)}, f32[8,512]{1,0:T(8,128)S(1)}) custom-call(bf16[512,256]{1,0:T(8,128)(2,1)S(1)} %copy-done.30, bf16[512,512]{1,0:T(8,128)(2,1)S(1)} %copy-done.14, bf16[512,512]{1,0:T(8,128)(2,1)S(1)} %collective-permute-done.6.refs_2_.refs_9_), custom_call_target="tpu_custom_call" | custom-call | flops 6000000000 | bytes 6000000 | tf_op jit(solution)/shard_map/pallas_call | solution.py:44
  92.1 4.8 %collective-permute-done.9.refs_8_ = bf16[512,256]{1,0:T(8,128)(2,1)S(1)} collective-permute-done((bf16[512,256]{1,0:T(8,128)(2,1)S(1)}, bf16[512,256]{1,0:T(8,128)(2,1)S(1)}, u32[]{:S(2)}, u32[]{:S(2)}) %collective-permute-start.9) | collective-permute-done | bytes 262176 | tf_op jit(solution)/shard_map/ppermute | solution.py:580
  96.9 4.9 %collective-permute-done.8.refs_7_ = bf16[512,256]{1,0:T(8,128)(2,1)S(1)} collective-permute-done((bf16[512,256]{1,0:T(8,128)(2,1)S(1)}, bf16[512,256]{1,0:T(8,128)(2,1)S(1)}, u32[]{:S(2)}, u32[]{:S(2)}) %collective-permute-start.8) | collective-permute-done | bytes 262176 | tf_op jit(solution)/shard_map/ppermute | solution.py:580
  103.9 14.9 %shard_map.147 = (f32[128,1024]{1,0:T(8,128)}, bf16[128,1024]{1,0:T(8,128)(2,1)}, bf16[128,1024]{1,0:T(8,128)(2,1)}, bf16[128,1024]{1,0:T(8,128)(2,1)}, bf16[128...) custom-call(s32[3]{0:T(128)} %pad_add_fusion.refs_0_, ...), custom_call_target="tpu_custom_call" | custom-call | flops 11000000512 | bytes 11000000 | tf_op jit(solution)/shard_map/pallas_call | solution.py:44
  120.4 7.2 %shard_map.148 = (bf16[128,1024]{1,0:T(8,128)(2,1)}, bf16[128,1024]{1,0:T(8,128)(2,1)}, bf16[128,1024]{1,0:T(8,128)(2,1)}, bf16[128,1024]{1,0:T(8,128)(2,1)}, bf16[8,192,1536]{2,1,0:T(8,128)(2,1)}) custom-call(s32[3]{0:T(128)} %pad_add_fusion.refs_0_, bf16[512,768]{1,0:T(8,128)(2,1)} %get-tuple-element.88.refs_1_, bf16[8,192,1536]{2,1,0:T(8,128)(2,1)} %bitcast.55, ...), custom_call_target="tpu_custom_call" | custom-call | flops 5000000000 | bytes 5000000 | tf_op jit(solution)/shard_map/pallas_call | solution.py:44
  131.4 10.9 %collective-permute-done.15.refs_2_ = bf16[128,1024]{1,0:T(8,128)(2,1)S(1)} collective-permute-done((bf16[128,1024]{1,0:T(8,128)(2,1)S(1)}, bf16[128,1024]{1,0:T(8,128)(2,1)S(1)}, u32[]{:S(2)}, u32[]{:S(2)}) %collective-permute-start.15) | collective-permute-done | bytes 262176 | tf_op jit(solution)/shard_map/ppermute | solution.py:580
  147.2 6.7 %collective-permute-done.19.refs_4_ = bf16[128,1024]{1,0:T(8,128)(2,1)S(1)} collective-permute-done((bf16[128,1024]{1,0:T(8,128)(2,1)S(1)}, bf16[128,1024]{1,0:T(8,128)(2,1)S(1)}, u32[]{:S(2)}, u32[]{:S(2)}) %collective-permute-start.19) | collective-permute-done | bytes 262176 | tf_op jit(solution)/shard_map/ppermute | solution.py:580
  159.5 7.1 %shard_map.150 = (bf16[512,256]{1,0:T(8,128)(2,1)S(1)}, f32[512,512]{1,0:T(8,128)S(1)}, bf16[512,512]{1,0:T(8,128)(2,1)S(1)}, bf16[512,1024]{1,0:T(8,128)(2,1)S(1)}) custom-call(s32[3]{0:T(128)S(1)} %copy-done.9, bf16[128,1024]{1,0:T(8,128)(2,1)S(1)} %get-tuple-element.92.refs_1_, bf16[128,1024]{1,0:T(8,128)(2,1)S(1)} %collective-permute-done.17.refs_2_, ...), custom_call_target="tpu_custom_call" | custom-call | flops 10000000000 | bytes 10000000 | tf_op jit(solution)/shard_map/pallas_call | solution.py:44
  171.1 3.6 %shard_map.152 = (bf16[544,1024]{1,0:T(8,128)(2,1)S(1)}, bf16[544,1024]{1,0:T(8,128)(2,1)S(1)}, bf16[128,1024]{1,0:T(8,128)(2,1)S(1)}, bf16[128,1024]{1,0:T(8,12...) custom-call(s32[3]{0:T(128)S(1)} %copy-done.9, ...), custom_call_target="tpu_custom_call" | custom-call | flops 4000000000 | bytes 4000000 | tf_op jit(solution)/shard_map/pallas_call | solution.py:44
  179.4 3.8 %reduce-scatter.3.cloned.1.call-done = bf16[1,192,1536]{2,1,0:T(8,128)(2,1)} async-done(((bf16[8,192,1536]{2,1,0:T(8,128)(2,1)}), bf16[1,192,1536]{2,1,0:T(8,128)(2,1)}) %reduce-scatter.3.cloned.1.call-update) | async-done | bytes 589840 | tf_op jit(solution)/shard_map/reduce_scatter | solution.py:718
  186.8 5.2 %collective-permute-done.24.refs_2_ = bf16[128,1024]{1,0:T(8,128)(2,1)S(1)} collective-permute-done((bf16[128,1024]{1,0:T(8,128)(2,1)S(1)}, bf16[128,1024]{1,0:T(8,128)(2,1)S(1)}, u32[]{:S(2)}, u32[]{:S(2)}) %collective-permute-start.24) | collective-permute-done | bytes 262176 | tf_op jit(solution)/shard_map/ppermute | solution.py:580
  192.0 4.1 %collective-permute-done.25.refs_3_ = bf16[128,1024]{1,0:T(8,128)(2,1)S(1)} collective-permute-done((bf16[128,1024]{1,0:T(8,128)(2,1)S(1)}, bf16[128,1024]{1,0:T(8,128)(2,1)S(1)}, u32[]{:S(2)}, u32[]{:S(2)}) %collective-permute-start.25) | collective-permute-done | bytes 262176 | tf_op jit(solution)/shard_map/ppermute | solution.py:580
  203.8 5.0 %collective-permute-done.36.refs_3_ = bf16[192,1536]{1,0:T(8,128)(2,1)S(1)} collective-permute-done((bf16[192,1536]{1,0:T(8,128)(2,1)}, bf16[192,1536]{1,0:T(8,128)(2,1)S(1)}, u32[]{:S(2)}, u32[]{:S(2)}) %collective-permute-start.36) | collective-permute-done | bytes 589856 | tf_op jit(solution)/shard_map/ppermute | solution.py:580
  208.7 4.3 %collective-permute-start.38 = (bf16[96,1536]{1,0:T(8,128)(2,1)S(1)}, bf16[96,1536]{1,0:T(8,128)(2,1)S(1)}, u32[]{:S(2)}, u32[]{:S(2)}) collective-permute-start(bf16[96,1536]{1,0:T(8,128)(2,1)S(1)} %slice.25), channel_id=1, source_target_pairs={{0,8},{8,0},{16,24},{24,16},{1,9},{9,1},{17,25},{25,17},{2,10},{10... | collective-permute-start | bytes 884744 | tf_op jit(solution)/shard_map/ppermute | solution.py:580
  217.2 5.2 %collective-permute-start.29 = (bf16[64,1024]{1,0:T(8,128)(2,1)}, bf16[64,1024]{1,0:T(8,128)(2,1)S(1)}, u32[]{:S(2)}, u32[]{:S(2)}) collective-permute-start(bf16[64,1024]{1,0:T(8,128)(2,1)} %get-tuple-element.118), channel_id=1, source_target_pairs={{0,4},{1,5},{2,12},{3,13},{4,20},{5,21},{6,28},{7,29},{8,6},{9,7},... | collective-permute-start | bytes 393224 | tf_op jit(solution)/shard_map/ppermute | solution.py:614
  223.4 4.0 %collective-permute-start.34 = (bf16[136,1024]{1,0:T(8,128)(2,1)}, bf16[136,1024]{1,0:T(8,128)(2,1)S(1)}, u32[]{:S(2)}, u32[]{:S(2)}) collective-permute-start(bf16[136,1024]{1,0:T(8,128)(2,1)} %reduce-scatter.5.cloned.1.call-done.refs_5_.refs_1_.refs_6_), channel_id=1, source_target_pairs={{0,24},{8,16},{16,8},{24,0},{1,25},{9,17},{17,9},{25,1},{2,26},{10... | collective-permute-start | bytes 835592 | tf_op jit(solution)/shard_map/ppermute | solution.py:580
  227.4 6.1 %collective-permute-done.29.refs_3_ = bf16[64,1024]{1,0:T(8,128)(2,1)S(1)} collective-permute-done((bf16[64,1024]{1,0:T(8,128)(2,1)}, bf16[64,1024]{1,0:T(8,128)(2,1)S(1)}, u32[]{:S(2)}, u32[]{:S(2)}) %collective-permute-start.29) | collective-permute-done | bytes 131104 | tf_op jit(solution)/shard_map/ppermute | solution.py:614
  236.1 4.7 %shard_map.157 = (f32[128,5248]{1,0:T(8,128)}, f32[328,1024]{1,0:T(8,128)}) custom-call(s32[3]{0:T(128)S(1)} %copy-done.10, bf16[192,1536]{1,0:T(8,128)(2,1)S(1)} %bitcast.45, bf16[192,1536]{1,0:T(8,128)(2,1)S(1)} %collective-permute-done.35.refs_2_, bf16[192,1536]{1,0:T(8,128)(2,1)S(1)} %collective-permute-done.36.refs_3_, ...), custom_call_target="tpu_custom_call" | custom-call | flops 4000000000 | bytes 4000000 | tf_op jit(solution)/shard_map/pallas_call | solution.py:44
  (222 shorter events, 81.7 us)
Async XLA Ops:
  7.2 50.9 %all-gather.5.cloned.1.call-start = ((), (), s32[]{:S(2)}) async-start(), calls=%async_computation.8 | async-start | bytes 2506752 | tf_op jit(solution)/shard_map/all_gather | solution.py:624
  11.2 92.7 %all-gather.7.cloned.1.call-start = ((), (), s32[]{:S(2)}) async-start(), calls=%async_computation.9 | async-start | bytes 5308416 | tf_op jit(solution)/shard_map/all_gather | solution.py:639
  33.5 15.4 %all-to-all-start.1 = ((bf16[4,32,1024]{2,1,0:T(8,128)(2,1)}), bf16[4,32,1024]{2,1,0:T(8,128)(2,1)S(1)}, u32[]{:S(2)}, u32[]{:S(2)}) async-start(bf16[4,32,1024]{2,1,0:T(8,128)(2,1)} %all_to_all.44), calls=%async_computation.1 | async-start | bytes 524288 | tf_op jit(solution)/shard_map/all_to_all | solution.py:627
  51.2 13.5 %collective-permute-start.1 = (bf16[128,1024]{1,0:T(8,128)(2,1)S(1)}, bf16[128,1024]{1,0:T(8,128)(2,1)S(1)}, u32[]{:S(2)}, u32[]{:S(2)}) collective-permute-start(bf16[128,1024]{1,0:T(8,128)(2,1)S(1)} %bitcast.30), channel_id=1, source_target_pairs={{0,16},{8,24},{16,0},{24,8},{1,17},{9,25},{17,1},{25,9},{2,18},{10... | collective-permute-start | bytes 786440 | tf_op jit(solution)/shard_map/ppermute | solution.py:580
  51.8 12.9 %collective-permute-start = (bf16[128,1024]{1,0:T(8,128)(2,1)S(1)}, bf16[128,1024]{1,0:T(8,128)(2,1)S(1)}, u32[]{:S(2)}, u32[]{:S(2)}) collective-permute-start(bf16[128,1024]{1,0:T(8,128)(2,1)S(1)} %bitcast.31), channel_id=1, source_target_pairs={{0,8},{8,0},{16,24},{24,16},{1,9},{9,1},{17,25},{25,17},{2,10},{10... | collective-permute-start | bytes 786440 | tf_op jit(solution)/shard_map/ppermute | solution.py:580
  52.3 14.4 %all-to-all-start.3 = ((bf16[4,32,1024]{2,1,0:T(8,128)(2,1)}), bf16[4,32,1024]{2,1,0:T(8,128)(2,1)S(1)}, u32[]{:S(2)}, u32[]{:S(2)}) async-start(bf16[4,32,1024]{2,1,0:T(8,128)(2,1)} %bitcast.11), calls=%async_computation.3 | async-start | bytes 524288 | tf_op jit(solution)/shard_map/all_to_all | solution.py:630
  55.7 127.5 %reduce-scatter.3.cloned.1.call-start = ((), (), s32[]{:S(2)}) async-start(), calls=%async_computation.6 | async-start | bytes 5308416 | tf_op jit(solution)/shard_map/reduce_scatter | solution.py:718
  59.1 14.9 %collective-permute-start.5 = (bf16[4,128,256]{2,1,0:T(8,128)(2,1)S(1)}, bf16[4,128,256]{2,1,0:T(8,128)(2,1)S(1)}, u32[]{:S(2)}, u32[]{:S(2)}) collective-permute-start(bf16[4,128,256]{2,1,0:T(8,128)(2,1)S(1)} %dynamic-slice_bitcast_fusion.refs_9_), channel_id=1, source_target_pairs={{0,24},{8,16},{16,8},{24,0},{1,25},{9,17},{17,9},{25,1},{2,26},{10... | collective-permute-start | bytes 786440 | tf_op jit(solution)/shard_map/ppermute | solution.py:580
  61.6 12.8 %collective-permute-start.4 = (bf16[4,128,256]{2,1,0:T(8,128)(2,1)S(1)}, bf16[4,128,256]{2,1,0:T(8,128)(2,1)S(1)}, u32[]{:S(2)}, u32[]{:S(2)}) collective-permute-start(bf16[4,128,256]{2,1,0:T(8,128)(2,1)S(1)} %dynamic-slice_bitcast_fusion.refs_9_), channel_id=1, source_target_pairs={{0,16},{8,24},{16,0},{24,8},{1,17},{9,25},{17,1},{25,9},{2,18},{10... | collective-permute-start | bytes 786440 | tf_op jit(solution)/shard_map/ppermute | solution.py:580
  74.7 27.2 %collective-permute-start.10 = (bf16[4,4,128,256]{3,2,1,0:T(8,128)(2,1)S(1)}, bf16[4,4,128,256]{3,2,1,0:T(8,128)(2,1)S(1)}, u32[]{:S(2)}, u32[]{:S(2)}) collective-permute-start(bf16[4,4,128,256]{3,2,1,0:T(8,128)(2,1)S(1)} %pad_maximum_fusion), channel_id=1, source_target_pairs={{0,1},{1,0},{2,3},{3,2},{4,5},{5,4},{6,7},{7,6},{8,9},{9,8},{10,11... | collective-permute-start | bytes 3145736 | tf_op jit(solution)/shard_map/ppermute | solution.py:588
  74.8 13.5 %collective-permute-start.13 = (bf16[128,1024]{1,0:T(8,128)(2,1)S(1)}, bf16[128,1024]{1,0:T(8,128)(2,1)S(1)}, u32[]{:S(2)}, u32[]{:S(2)}) collective-permute-start(bf16[128,1024]{1,0:T(8,128)(2,1)S(1)} %bitcast.39), channel_id=1, source_target_pairs={{0,24},{8,16},{16,8},{24,0},{1,25},{9,17},{17,9},{25,1},{2,26},{10... | collective-permute-start | bytes 786440 | tf_op jit(solution)/shard_map/ppermute | solution.py:580
  78.5 12.8 %collective-permute-start.12 = (bf16[128,1024]{1,0:T(8,128)(2,1)S(1)}, bf16[128,1024]{1,0:T(8,128)(2,1)S(1)}, u32[]{:S(2)}, u32[]{:S(2)}) collective-permute-start(bf16[128,1024]{1,0:T(8,128)(2,1)S(1)} %bitcast.40), channel_id=1, source_target_pairs={{0,16},{8,24},{16,0},{24,8},{1,17},{9,25},{17,1},{25,9},{2,18},{10... | collective-permute-start | bytes 786440 | tf_op jit(solution)/shard_map/ppermute | solution.py:580
  78.5 13.6 %collective-permute-start.11 = (bf16[128,1024]{1,0:T(8,128)(2,1)S(1)}, bf16[128,1024]{1,0:T(8,128)(2,1)S(1)}, u32[]{:S(2)}, u32[]{:S(2)}) collective-permute-start(bf16[128,1024]{1,0:T(8,128)(2,1)S(1)} %bitcast.41), channel_id=1, source_target_pairs={{0,8},{8,0},{16,24},{24,16},{1,9},{9,1},{17,25},{25,17},{2,10},{10... | collective-permute-start | bytes 786440 | tf_op jit(solution)/shard_map/ppermute | solution.py:580
  88.3 13.5 %collective-permute-start.8 = (bf16[512,256]{1,0:T(8,128)(2,1)S(1)}, bf16[512,256]{1,0:T(8,128)(2,1)S(1)}, u32[]{:S(2)}, u32[]{:S(2)}) collective-permute-start(bf16[512,256]{1,0:T(8,128)(2,1)S(1)} %get-tuple-element.79.refs_5_.refs_6_), channel_id=1, source_target_pairs={{0,16},{8,24},{16,0},{24,8},{1,17},{9,25},{17,1},{25,9},{2,18},{10... | collective-permute-start | bytes 786440 | tf_op jit(solution)/shard_map/ppermute | solution.py:580
  127.6 95.7 %reduce-scatter.5.cloned.1.call-start = ((), (), s32[]{:S(2)}) async-start(), calls=%async_computation.7 | async-start | bytes 1392640 | tf_op jit(solution)/shard_map/reduce_scatter | solution.py:760
  128.5 13.8 %collective-permute-start.15 = (bf16[128,1024]{1,0:T(8,128)(2,1)S(1)}, bf16[128,1024]{1,0:T(8,128)(2,1)S(1)}, u32[]{:S(2)}, u32[]{:S(2)}) collective-permute-start(bf16[128,1024]{1,0:T(8,128)(2,1)S(1)} %copy-done.54), channel_id=1, source_target_pairs={{0,16},{8,24},{16,0},{24,8},{1,17},{9,25},{17,1},{25,9},{2,18},{10... | collective-permute-start | bytes 786440 | tf_op jit(solution)/shard_map/ppermute | solution.py:580
  146.1 13.4 %collective-permute-start.17 = (bf16[128,1024]{1,0:T(8,128)(2,1)S(1)}, bf16[128,1024]{1,0:T(8,128)(2,1)S(1)}, u32[]{:S(2)}, u32[]{:S(2)}) collective-permute-start(bf16[128,1024]{1,0:T(8,128)(2,1)S(1)} %get-tuple-element.92.refs_1_), channel_id=1, source_target_pairs={{0,8},{8,0},{16,24},{24,16},{1,9},{9,1},{17,25},{25,17},{2,10},{10... | collective-permute-start | bytes 786440 | tf_op jit(solution)/shard_map/ppermute | solution.py:580
  153.9 12.8 %collective-permute-start.20 = (bf16[128,1024]{1,0:T(8,128)(2,1)S(1)}, bf16[128,1024]{1,0:T(8,128)(2,1)S(1)}, u32[]{:S(2)}, u32[]{:S(2)}) collective-permute-start(bf16[128,1024]{1,0:T(8,128)(2,1)S(1)} %copy-done.49), channel_id=1, source_target_pairs={{0,8},{8,0},{16,24},{24,16},{1,9},{9,1},{17,25},{25,17},{2,10},{10... | collective-permute-start | bytes 786440 | tf_op jit(solution)/shard_map/ppermute | solution.py:580
  198.6 14.4 %collective-permute-start.35 = (bf16[192,1536]{1,0:T(8,128)(2,1)}, bf16[192,1536]{1,0:T(8,128)(2,1)S(1)}, u32[]{:S(2)}, u32[]{:S(2)}) collective-permute-start(bf16[192,1536]{1,0:T(8,128)(2,1)} %bitcast.44), channel_id=1, source_target_pairs={{0,8},{8,0},{16,24},{24,16},{1,9},{9,1},{17,25},{25,17},{2,10},{10... | collective-permute-start | bytes 1769480 | tf_op jit(solution)/shard_map/ppermute | solution.py:580
  202.1 20.2 %collective-permute-start.28 = (bf16[64,1024]{1,0:T(8,128)(2,1)}, bf16[64,1024]{1,0:T(8,128)(2,1)S(1)}, u32[]{:S(2)}, u32[]{:S(2)}) collective-permute-start(bf16[64,1024]{1,0:T(8,128)(2,1)} %get-tuple-element.117), channel_id=1, source_target_pairs={{0,2},{1,3},{2,10},{3,11},{4,18},{5,19},{6,26},{7,27},{8,0},{9,1},... | collective-permute-start | bytes 393224 | tf_op jit(solution)/shard_map/ppermute | solution.py:614
  208.7 27.3 %collective-permute-start.38 = (bf16[96,1536]{1,0:T(8,128)(2,1)S(1)}, bf16[96,1536]{1,0:T(8,128)(2,1)S(1)}, u32[]{:S(2)}, u32[]{:S(2)}) collective-permute-start(bf16[96,1536]{1,0:T(8,128)(2,1)S(1)} %slice.25), channel_id=1, source_target_pairs={{0,8},{8,0},{16,24},{24,16},{1,9},{9,1},{17,25},{25,17},{2,10},{10... | collective-permute-start | bytes 884744 | tf_op jit(solution)/shard_map/ppermute | solution.py:580
  213.0 23.0 %collective-permute-start.37 = (bf16[96,1536]{1,0:T(8,128)(2,1)S(1)}, bf16[96,1536]{1,0:T(8,128)(2,1)S(1)}, u32[]{:S(2)}, u32[]{:S(2)}) collective-permute-start(bf16[96,1536]{1,0:T(8,128)(2,1)S(1)} %slice.24), channel_id=1, source_target_pairs={{0,16},{8,24},{16,0},{24,8},{1,17},{9,25},{17,1},{25,9},{2,18},{10... | collective-permute-start | bytes 884744 | tf_op jit(solution)/shard_map/ppermute | solution.py:580
  217.2 16.3 %collective-permute-start.29 = (bf16[64,1024]{1,0:T(8,128)(2,1)}, bf16[64,1024]{1,0:T(8,128)(2,1)S(1)}, u32[]{:S(2)}, u32[]{:S(2)}) collective-permute-start(bf16[64,1024]{1,0:T(8,128)(2,1)} %get-tuple-element.118), channel_id=1, source_target_pairs={{0,4},{1,5},{2,12},{3,13},{4,20},{5,21},{6,28},{7,29},{8,6},{9,7},... | collective-permute-start | bytes 393224 | tf_op jit(solution)/shard_map/ppermute | solution.py:614
  223.4 17.4 %collective-permute-start.34 = (bf16[136,1024]{1,0:T(8,128)(2,1)}, bf16[136,1024]{1,0:T(8,128)(2,1)S(1)}, u32[]{:S(2)}, u32[]{:S(2)}) collective-permute-start(bf16[136,1024]{1,0:T(8,128)(2,1)} %reduce-scatter.5.cloned.1.call-done.refs_5_.refs_1_.refs_6_), channel_id=1, source_target_pairs={{0,24},{8,16},{16,8},{24,0},{1,25},{9,17},{17,9},{25,1},{2,26},{10... | collective-permute-start | bytes 835592 | tf_op jit(solution)/shard_map/ppermute | solution.py:580
  (82 other events, 685.1 us)
Sparse Core Ops, SparseCore 0:
  11.3 36.5 all-gather.4
  50.1 53.6 all-gather.6
  127.8 55.4 reduce-scatter.2
  186.0 29.3 reduce-scatter.4
